TPU v7x, 32 devices: a whole 2x2x4 slice. The times are simulated.
32 devices in a mesh: fsdp: 4 (over y, x), ctx: 2 (over core), tp: 4 (over z).
Axes of the slice: x: 2, y: 2, z: 4, core: 2. Of those that a mesh axis runs over, the one named last changes fastest.
Arguments:
- tokens: bfloat16 [4, 2048, 1600], P('fsdp', ('ctx', 'tp')), may hold values from -6 to 6
- segments: int32 [4, 2048], P('fsdp'), may hold values from 0 to 7, never falling along the last dimension, each value on 1 to 1536 neighbouring positions
- cotangent: bfloat16 [4, 2048, 1600], P('fsdp', ('ctx', 'tp')), may hold values from -6 to 6
- meta_tokens: bfloat16 [1600, 128], P(('fsdp', 'ctx')), may hold values from -6 to 6
- gain_mix: bfloat16 [1600], P(('fsdp', 'ctx')), may hold values from 0.5 to 1.5
- query_weight: bfloat16 [1600, 1600], P(('fsdp', 'ctx')), may hold values from -0.15625 to 0.15625
- key_value_weight: bfloat16 [1600, 640], P(('fsdp', 'ctx')), may hold values from -0.15625 to 0.15625
- attn_output: bfloat16 [1600, 1600], P(('fsdp', 'ctx')), may hold values from -0.15625 to 0.15625
- gain_attn: bfloat16 [1600], P(('fsdp', 'ctx')), may hold values from 0.5 to 1.5
- mamba_input: bfloat16 [1600, 3, 3200], P(('fsdp', 'ctx'), None, 'tp'), may hold values from -0.15625 to 0.15625
- mamba_select: bfloat16 [1600, 32], P(('fsdp', 'ctx')), may hold values from -0.15625 to 0.15625
- step_bias: float32 [3200], P('tp'), may hold values from -1 to 1
- decay_log: float32 [3200], P('tp'), may hold values from -9.2 to -3
- state_skip: float32 [3200], P('tp'), may hold values from 0.5 to 1.5
- mamba_output: bfloat16 [1600, 3200], P(('fsdp', 'ctx'), 'tp'), may hold values from -0.109375 to 0.109375
- gain_mamba: bfloat16 [1600], P(('fsdp', 'ctx')), may hold values from 0.5 to 1.5
- gain_ffn: bfloat16 [1600], P(('fsdp', 'ctx')), may hold values from 0.5 to 1.5
- ffn_input: bfloat16 [1600, 2, 5504], P(('fsdp', 'ctx')), may hold values from -0.15625 to 0.15625
- ffn_output: bfloat16 [1600, 5504], P(('fsdp', 'ctx')), may hold values from -0.078125 to 0.078125
Outputs:
- layer_out: bfloat16 [4, 2048, 1600], P('fsdp', ('ctx', 'tp'))
- grad_tokens: bfloat16 [4, 2048, 1600], P('fsdp', ('ctx', 'tp'))
- grad_meta: float32 [1600, 128], P(('fsdp', 'ctx'), 'tp')
- grad_gain_mix: float32 [1600], P(('fsdp', 'ctx'))
- grad_query: float32 [1600, 1600], P(('fsdp', 'ctx'), 'tp')
- grad_keyval: float32 [1600, 640], P(('fsdp', 'ctx'), 'tp')
- grad_attn_output: float32 [1600, 1600], P(('fsdp', 'ctx'), 'tp')
- grad_gain_attn: float32 [1600], P(('fsdp', 'ctx'))
- grad_mamba_input: float32 [1600, 3, 3200], P(('fsdp', 'ctx'), None, 'tp')
- grad_mamba_select: float32 [1600, 32], P(('fsdp', 'ctx'), 'tp')
- grad_step_bias: float32 [3200], P('tp')
- grad_decay_log: float32 [3200], P('tp')
- grad_state_skip: float32 [3200], P('tp')
- grad_mamba_output: float32 [1600, 3200], P(('fsdp', 'ctx'), 'tp')
- grad_gain_mamba: float32 [1600], P(('fsdp', 'ctx'))
- grad_gain_ffn: float32 [1600], P(('fsdp', 'ctx'))
- grad_ffn_input: float32 [1600, 2, 5504], P(('fsdp', 'ctx'), None, 'tp')
- grad_ffn_output: float32 [1600, 5504], P(('fsdp', 'ctx'), 'tp')
Inputs may be any that keep to these rules, and one draw needn't show every extreme that they name: `segments`: in every sequence the segment numbers start at 0, never fall, and each document holds at most 1536 tokens.
All inputs are finite; a program needn't handle non-finite values.
Results may differ from a plain program's by a relative error of at most 0.019.
Values may be sent and summed in bfloat16 or wider, within the bound.
A program may use at most 384 MiB of HBM per device.

v0:
```python
import functools

import jax
import jax.numpy as jnp
from jax import lax
from jax.experimental import pallas as pl
from jax.experimental.pallas import tpu as pltpu
from jax.sharding import PartitionSpec as P

HEAD_SIZE = 64
STATE = 16
WIN = 1024
SUB = 4
TILE = 128

bf16 = jnp.bfloat16
f32 = jnp.float32
epsilon = 1e-05
masked_score = -1e30


def mm(a, b):
    return lax.dot_general(a, b, (((1,), (0,)), ((), ())), preferred_element_type=f32)


def mm_nt(a, b):
    return lax.dot_general(a, b, (((1,), (1,)), ((), ())), preferred_element_type=f32)


def iota(shape, dim):
    return lax.broadcasted_iota(jnp.int32, shape, dim)


def split_mm(a, b):
    high = b.astype(bf16)
    return mm(a, high) + mm(a, (b - high.astype(f32)).astype(bf16))


def ones_where(cond):
    return jnp.where(cond, 1.0, 0.0)


def softplus(v):
    return jnp.maximum(v, 0.0) + jnp.log1p(jnp.exp(-jnp.abs(v)))


def logistic(v):
    return 1.0 / (1.0 + jnp.exp(-v))


def group_mask(rows, columns, row_unit, column_unit):
    return iota((rows, columns), 0) // row_unit == iota((rows, columns), 1) // column_unit


def sums_matrix():
    rows = 2 * TILE + TILE // SUB
    row = iota((rows, TILE), 0)
    column = iota((rows, TILE), 1)
    token = row % TILE
    same = token // SUB == column // SUB
    upto = (row < TILE) & same & (column <= token)
    after = (row >= TILE) & (row < 2 * TILE) & same & (column > token)
    whole = (row >= 2 * TILE) & (row - 2 * TILE == column // SUB)
    return ones_where(upto | after | whole).astype(bf16)


def part(mixed, k):
    channels = mixed.shape[1] // 3
    return mixed[:, k * channels : (k + 1) * channels]


def decays(step_raw, bias_ref, rate_ref, alive_last_ref):
    raw = step_raw + bias_ref[...]
    step = softplus(raw)
    log_decay = -step * rate_ref[...]
    sums = split_mm(sums_matrix(), log_decay)
    upto = jnp.exp(sums[:TILE])
    after = sums[TILE : 2 * TILE]
    block = jnp.exp(sums[2 * TILE :]) * alive_last_ref[...]
    return raw, step, log_decay, upto, after, block


def in_blocks(select_t_ref, aux_t_ref):
    width = TILE // SUB * STATE
    tiled = jnp.concatenate([select_t_ref[:STATE, :].astype(f32) * aux_t_ref[1:2, :]] * (TILE // SUB), axis=0)
    return jnp.where(group_mask(width, TILE, STATE, SUB), tiled, 0.0).astype(bf16)


def out_blocks_t(select_t_ref, aux_t_ref):
    width = TILE // SUB * STATE
    tiled = jnp.concatenate([select_t_ref[STATE:, :].astype(f32) * aux_t_ref[0:1, :]] * (TILE // SUB), axis=0)
    return jnp.where(group_mask(width, TILE, STATE, SUB), tiled, 0.0).astype(bf16)


def spread(part, factor):
    width = TILE // SUB * STATE
    places = ones_where(iota((STATE, width), 0) == iota((STATE, width), 1) % STATE).astype(bf16)
    wide = mm(part, places) * factor
    return jnp.where(group_mask(TILE, width, SUB, STATE), wide, 0.0).astype(bf16)


def fold(wide, factor):
    width = TILE // SUB * STATE
    places = ones_where(iota((width, STATE), 0) % STATE == iota((width, STATE), 1)).astype(bf16)
    kept = jnp.where(group_mask(TILE, width, SUB, STATE), wide * factor, 0.0)
    return split_left(kept, places)


def split_left(a, b):
    high = a.astype(bf16)
    return mm(high, b) + mm((a - high.astype(f32)).astype(bf16), b)


def pairs(aux_ref, aux_t_ref, lower):
    row, column = iota((TILE, TILE), 0), iota((TILE, TILE), 1)
    order = column <= row if lower else column >= row
    return (row // SUB == column // SUB) & order & (aux_ref[:, 2:3] == aux_t_ref[2:3, :])


def run_states(state, local_ref, block_ref, keep=None):
    def one(k, state):
        if keep is not None:
            keep[pl.ds(pl.multiple_of(k * STATE, STATE), STATE), :] = state.astype(bf16)
        return block_ref[pl.ds(k, 1), :] * state + local_ref[pl.ds(pl.multiple_of(k * STATE, STATE), STATE), :]

    return lax.fori_loop(0, TILE // SUB, one, state, unroll=8)


def end_state_kernel(mixed, select_t, aux, aux_t, alive_last, bias, rate, end, state, local, block):
    @pl.when(pl.program_id(0) == 0)
    def _():
        state[...] = jnp.zeros_like(state)

    raw, step, log_decay, upto, after, total = decays(part(mixed, 2), bias, rate, alive_last)
    driven = (jnp.exp(after) * step * part(mixed, 0)).astype(bf16)
    local[...] = mm(in_blocks(select_t, aux_t), driven)
    block[...] = total
    state[...] = run_states(state[...], local, block)
    end[...] = state[...]


def forward_kernel(mixed, select, select_t, aux, aux_t, alive_last, bias, rate, skip, start, gated, states, end, state, local, block):
    @pl.when(pl.program_id(0) == 0)
    def _():
        state[...] = start[...]

    raw, step, log_decay, upto, after, total = decays(part(mixed, 2), bias, rate, alive_last)
    x = part(mixed, 0)
    driven = (jnp.exp(after) * step * x).astype(bf16)
    local[...] = mm(in_blocks(select_t, aux_t), driven)
    block[...] = total
    state[...] = run_states(state[...], local, block, states)
    end[...] = state[...]
    out_part = select[:, STATE:]
    cross = jnp.where(pairs(aux, aux_t, True), mm(out_part, select_t[:STATE, :]), 0.0).astype(bf16)
    y = upto * mm(spread(out_part, aux[:, 0:1]), states[...]) + jnp.exp(-after) * mm(cross, driven) + skip[...] * x
    gates = part(mixed, 1)
    gated[...] = (y * gates * logistic(gates)).astype(bf16)


def back_run(carry, local_ref, block_ref, keep, states=None, bound=None):
    count = TILE // SUB

    def one(i, carry):
        k = count - 1 - i
        rows = pl.ds(pl.multiple_of(k * STATE, STATE), STATE)
        if keep is not None:
            keep[rows, :] = carry[0].astype(bf16)
            bound[pl.ds(k, 1), :] = carry[1]
        new = block_ref[pl.ds(k, 1), :] * carry[0] + local_ref[rows, :]
        if keep is None:
            return (new, carry[1])
        return (new, jnp.sum(new * states[rows, :].astype(f32), axis=0, keepdims=True))

    return lax.fori_loop(0, count, one, carry, unroll=8)


def end_adjoint_kernel(gated_grad, mixed, select_t, aux, aux_t, alive_last, bias, rate, end, state, local, block):
    @pl.when(pl.program_id(0) == 0)
    def _():
        state[...] = jnp.zeros_like(state)

    raw, step, log_decay, upto, after, total = decays(part(mixed, 2), bias, rate, alive_last)
    gates = part(mixed, 1)
    dy = gated_grad[...] * gates * logistic(gates)
    local[...] = mm(out_blocks_t(select_t, aux_t), (upto * dy).astype(bf16))
    block[...] = total
    state[...] = back_run((state[...], jnp.zeros((1, state.shape[1]), f32)), local, block, None)[0]
    end[...] = state[...]


def backward_kernel(gated_grad, mixed, select, select_t, states, aux, aux_t, alive_last, bias, rate, skip, start, final,
                    mix_grad, select_grad, sums, state, local, block, adjoint, bound, edge):
    @pl.when(pl.program_id(0) == 0)
    def _():
        state[...] = start[...]
        edge[...] = jnp.sum(start[...] * final[...], axis=0, keepdims=True)
        sums[...] = jnp.zeros_like(sums)

    raw, step, log_decay, upto, after, total = decays(part(mixed, 2), bias, rate, alive_last)
    channels = state.shape[1]
    x = part(mixed, 0)
    decay_after = jnp.exp(after)
    grow = jnp.exp(-after)
    driven = (decay_after * step * x).astype(bf16)
    in_part, out_part = select[:, :STATE], select[:, STATE:]
    in_part_t, out_part_t = select_t[:STATE, :], select_t[STATE:, :]
    lower, upper = pairs(aux, aux_t, True), pairs(aux, aux_t, False)
    cross = jnp.where(lower, mm(out_part, in_part_t), 0.0).astype(bf16)
    cross_t = jnp.where(upper, mm(in_part, out_part_t), 0.0).astype(bf16)
    y = upto * mm(spread(out_part, aux[:, 0:1]), states[...]) + grow * mm(cross, driven)
    gates = part(mixed, 1)
    sigma = logistic(gates)
    grad = gated_grad[...]
    dy = grad * gates * sigma
    mix_grad[:, channels : 2 * channels] = (grad * (y + skip[...] * x) * (sigma * (1.0 + gates * (1.0 - sigma)))).astype(bf16)
    dy_low = (upto * dy).astype(bf16)
    dy_grown = (grow * dy).astype(bf16)
    local[...] = mm(out_blocks_t(select_t, aux_t), dy_low)
    block[...] = total
    new_state, new_edge = back_run((state[...], edge[...]), local, block, adjoint, states, bound)
    state[...] = new_state
    edge[...] = new_edge
    du = decay_after * (mm(spread(in_part, aux[:, 1:2]), adjoint[...]) + mm(cross_t, dy_grown))
    out_grad = fold(mm_nt(dy_low, states[...]), aux[:, 0:1])
    in_grad = fold(mm_nt(driven, adjoint[...]), aux[:, 1:2])
    cross_grad = jnp.where(lower, mm_nt(dy_grown, driven), 0.0)
    cross_grad_t = jnp.where(upper, mm_nt(driven, dy_grown), 0.0)
    out_grad = out_grad + split_left(cross_grad, in_part)
    in_grad = in_grad + split_left(cross_grad_t, out_part)
    select_grad[...] = jnp.concatenate([in_grad, out_grad], axis=1)
    flow = dy * y - step * x * du
    places = ones_where(group_mask(TILE, TILE // SUB, SUB, 1)) * aux[:, 1:2]
    decay_grad = aux[:, 3:4] * (
        split_mm(ones_where(upper).astype(bf16), flow) + split_mm(places.astype(bf16), bound[...])
    )
    step_grad = (x * du - rate[...] * decay_grad) * logistic(raw)
    mix_grad[:, :channels] = (skip[...] * dy + step * du).astype(bf16)
    mix_grad[:, 2 * channels :] = step_grad.astype(bf16)
    sums[0:1, :] += jnp.sum(step_grad, axis=0, keepdims=True)
    sums[1:2, :] += jnp.sum(decay_grad * log_decay, axis=0, keepdims=True)
    sums[2:3, :] += jnp.sum(dy * x, axis=0, keepdims=True)


def scan_specs(tiles, channels, back):
    at = (lambda i: tiles - 1 - i) if back else (lambda i: i)

    mixed = pl.BlockSpec((TILE, 3 * channels), lambda i: (at(i), 0))
    rows = pl.BlockSpec((TILE, channels), lambda i: (at(i), 0))
    select = pl.BlockSpec((TILE, 2 * STATE), lambda i: (at(i), 0))
    select_t = pl.BlockSpec((2 * STATE, TILE), lambda i: (0, at(i)))
    states = pl.BlockSpec((TILE // SUB * STATE, channels), lambda i: (at(i), 0))
    aux = pl.BlockSpec((TILE, 8), lambda i: (at(i), 0))
    aux_t = pl.BlockSpec((8, TILE), lambda i: (0, at(i)))
    last = pl.BlockSpec((TILE // SUB, 1), lambda i: (at(i), 0))
    row = pl.BlockSpec((1, channels), lambda i: (0, 0))
    state = pl.BlockSpec((STATE, channels), lambda i: (0, 0))
    return mixed, rows, select, select_t, states, aux, aux_t, last, row, state


def scan_scratch(channels):
    return [
        pltpu.VMEM((STATE, channels), f32),
        pltpu.VMEM((TILE // SUB * STATE, channels), f32),
        pltpu.VMEM((TILE // SUB, channels), f32),
    ]


PARAMS = pltpu.CompilerParams(vmem_limit_bytes=48 << 20, dimension_semantics=("arbitrary",))


def scan_aux(segment, before):
    count = segment.shape[0]
    blocks = segment.reshape(count // SUB, SUB)
    ends = jnp.concatenate([before[None], blocks[:-1, -1]])
    alive = (blocks == ends[:, None]).reshape(-1).astype(f32)
    tail = (blocks == blocks[:, -1:]).reshape(-1).astype(f32)
    joined = (segment == jnp.concatenate([before[None], segment[:-1]])).astype(f32)
    zero = jnp.zeros_like(alive)
    aux_t = jnp.stack([alive, tail, segment.astype(f32), joined, zero, zero, zero, zero])
    last = (blocks[:, -1] == ends).astype(f32)[:, None]
    return aux_t.T, aux_t, last


def end_state(mixed, select_t, aux, bias, rate):
    tokens, channels = mixed.shape[0], mixed.shape[1] // 3
    tiles = tokens // TILE
    mixed_s, rows, select_s, select_t_s, states_s, aux_s, aux_t_s, last_s, row, state = scan_specs(tiles, channels, False)
    return pl.pallas_call(
        end_state_kernel, grid=(tiles,),
        in_specs=[mixed_s, select_t_s, aux_s, aux_t_s, last_s, row, row],
        out_specs=state, out_shape=jax.ShapeDtypeStruct((STATE, channels), f32),
        scratch_shapes=scan_scratch(channels), compiler_params=PARAMS,
    )(mixed, select_t, *aux, bias, rate)


def forward_scan(mixed, select, select_t, aux, bias, rate, skip, start):
    tokens, channels = mixed.shape[0], mixed.shape[1] // 3
    tiles = tokens // TILE
    mixed_s, rows, select_s, select_t_s, states_s, aux_s, aux_t_s, last_s, row, state = scan_specs(tiles, channels, False)
    return pl.pallas_call(
        forward_kernel, grid=(tiles,),
        in_specs=[mixed_s, select_s, select_t_s, aux_s, aux_t_s, last_s, row, row, row, state],
        out_specs=[rows, states_s, state],
        out_shape=[jax.ShapeDtypeStruct((tokens, channels), bf16), jax.ShapeDtypeStruct((tokens // SUB * STATE, channels), bf16), jax.ShapeDtypeStruct((STATE, channels), f32)],
        scratch_shapes=scan_scratch(channels), compiler_params=PARAMS,
    )(mixed, select, select_t, *aux, bias, rate, skip, start)


def end_adjoint(gated_grad, mixed, select_t, aux, bias, rate):
    tokens, channels = mixed.shape[0], mixed.shape[1] // 3
    tiles = tokens // TILE
    mixed_s, rows, select_s, select_t_s, states_s, aux_s, aux_t_s, last_s, row, state = scan_specs(tiles, channels, True)
    return pl.pallas_call(
        end_adjoint_kernel, grid=(tiles,),
        in_specs=[rows, mixed_s, select_t_s, aux_s, aux_t_s, last_s, row, row],
        out_specs=state, out_shape=jax.ShapeDtypeStruct((STATE, channels), f32),
        scratch_shapes=scan_scratch(channels), compiler_params=PARAMS,
    )(gated_grad, mixed, select_t, *aux, bias, rate)


def backward_scan(gated_grad, mixed, select, select_t, states, aux, bias, rate, skip, start, final):
    tokens, channels = mixed.shape[0], mixed.shape[1] // 3
    tiles = tokens // TILE
    mixed_s, rows, select_s, select_t_s, states_s, aux_s, aux_t_s, last_s, row, state = scan_specs(tiles, channels, True)
    return pl.pallas_call(
        backward_kernel, grid=(tiles,),
        in_specs=[rows, mixed_s, select_s, select_t_s, states_s, aux_s, aux_t_s, last_s, row, row, row, state, state],
        out_specs=[mixed_s, select_s, pl.BlockSpec((8, channels), lambda i: (0, 0))],
        out_shape=[jax.ShapeDtypeStruct((tokens, 3 * channels), bf16), jax.ShapeDtypeStruct((tokens, 2 * STATE), f32), jax.ShapeDtypeStruct((8, channels), f32)],
        scratch_shapes=scan_scratch(channels) + [
            pltpu.VMEM((TILE // SUB * STATE, channels), bf16),
            pltpu.VMEM((TILE // SUB, channels), f32),
            pltpu.VMEM((1, channels), f32),
        ],
        compiler_params=PARAMS,
    )(gated_grad, mixed, select, select_t, states, *aux, bias, rate, skip, start, final)


PARAMS_A = pltpu.CompilerParams(vmem_limit_bytes=56 << 20, dimension_semantics=("arbitrary",))


def attend_kernel(group, query_t, key_t, value_t, bias, out_t, log_total):
    keys = key_t[...].T
    values_t = value_t[...]
    for g in range(group):
        at = slice(g * HEAD_SIZE, (g + 1) * HEAD_SIZE)
        scores = mm(keys, query_t[at, :] * 0.125) + bias[...]
        top = jnp.max(scores, axis=0, keepdims=True)
        probs = jnp.exp(scores - top)
        total = jnp.sum(probs, axis=0, keepdims=True)
        out_t[at, :] = (mm(values_t, probs.astype(bf16)) / total).astype(bf16)
        log_total[g : g + 1, :] = top + jnp.log(total)


def attend_back_kernel(group, query_t, key_t, value_t, bias, out_t, log_total, grad_t, query_grad_t, key_grad_t, value_grad_t):
    keys_t = key_t[...]
    keys = keys_t.T
    values = value_t[...].T
    key_sum = jnp.zeros(key_grad_t.shape, f32)
    value_sum = jnp.zeros(value_grad_t.shape, f32)
    for g in range(group):
        at = slice(g * HEAD_SIZE, (g + 1) * HEAD_SIZE)
        query = query_t[at, :] * 0.125
        grad = grad_t[at, :]
        probs = jnp.exp(mm(keys, query) + bias[...] - log_total[g : g + 1, :])
        centre = jnp.sum(grad.astype(f32) * out_t[at, :].astype(f32), axis=0, keepdims=True)
        score_grad = (probs * (mm(values, grad) - centre)).astype(bf16)
        query_grad_t[at, :] = (mm(keys_t, score_grad) * 0.125).astype(bf16)
        key_sum = key_sum + mm_nt(query, score_grad)
        value_sum = value_sum + mm_nt(grad, probs.astype(bf16))
    key_grad_t[...] = key_sum
    value_grad_t[...] = value_sum


def attend(query_t, keyval_t, bias, key_value_heads):
    width, rows = query_t.shape
    keys = keyval_t.shape[1]
    group = width // HEAD_SIZE // key_value_heads
    kv = key_value_heads
    return pl.pallas_call(
        functools.partial(attend_kernel, group), grid=(kv,),
        in_specs=[
            pl.BlockSpec((group * HEAD_SIZE, rows), lambda h: (h, 0)),
            pl.BlockSpec((HEAD_SIZE, keys), lambda h: (h, 0)),
            pl.BlockSpec((HEAD_SIZE, keys), lambda h: (h + kv, 0)),
            pl.BlockSpec((keys, rows), lambda h: (0, 0)),
        ],
        out_specs=[
            pl.BlockSpec((group * HEAD_SIZE, rows), lambda h: (h, 0)),
            pl.BlockSpec((None, 8, rows), lambda h: (h, 0, 0)),
        ],
        out_shape=[jax.ShapeDtypeStruct((width, rows), bf16), jax.ShapeDtypeStruct((kv, 8, rows), f32)],
        compiler_params=PARAMS_A,
    )(query_t, keyval_t, keyval_t, bias)


def attend_back(query_t, keyval_t, bias, out_t, log_total, grad_t, key_value_heads):
    width, rows = query_t.shape
    keys = keyval_t.shape[1]
    group = width // HEAD_SIZE // key_value_heads
    kv = key_value_heads
    wide = pl.BlockSpec((group * HEAD_SIZE, rows), lambda h: (h, 0))
    head = pl.BlockSpec((HEAD_SIZE, keys), lambda h: (h, 0))
    return pl.pallas_call(
        functools.partial(attend_back_kernel, group), grid=(kv,),
        in_specs=[
            wide, head,
            pl.BlockSpec((HEAD_SIZE, keys), lambda h: (h + kv, 0)),
            pl.BlockSpec((keys, rows), lambda h: (0, 0)),
            wide,
            pl.BlockSpec((None, 8, rows), lambda h: (h, 0, 0)),
            wide,
        ],
        out_specs=[wide, head, head],
        out_shape=[jax.ShapeDtypeStruct((width, rows), bf16), jax.ShapeDtypeStruct((kv * HEAD_SIZE, keys), f32), jax.ShapeDtypeStruct((kv * HEAD_SIZE, keys), f32)],
        compiler_params=PARAMS_A,
    )(query_t, keyval_t, keyval_t, bias, out_t, log_total, grad_t)


def rms_norm(values, gain):
    return values * lax.rsqrt(jnp.mean(values * values, axis=-1, keepdims=True) + epsilon) * gain


def rms_back(values, gain, grad):
    scale = lax.rsqrt(jnp.mean(values * values, axis=-1, keepdims=True) + epsilon)
    normal = values * scale
    weighted = grad * gain
    back = scale * (weighted - normal * jnp.mean(weighted * normal, axis=-1, keepdims=True))
    return back, grad * normal


def dot(left, right, left_dim, right_dim):
    return lax.dot_general(
        left, right, (((left_dim,), (right_dim,)), ((), ())), preferred_element_type=f32
    )


def gather_rows(pieces):
    return lax.all_gather(jnp.concatenate(pieces, axis=1), ("fsdp", "ctx"), axis=0, tiled=True)


def scatter_rows(pieces):
    whole = jnp.concatenate([piece.astype(bf16) for piece in pieces], axis=1)
    return lax.psum_scatter(whole, ("fsdp", "ctx"), scatter_dimension=0, tiled=True)


def cut(values, widths):
    pieces = []
    offset = 0
    for count in widths:
        pieces.append(values[:, offset : offset + count])
        offset = offset + count
    return pieces


def per_device(
    tokens,
    segments,
    cotangent,
    meta_tokens,
    gain_mix,
    query_weight,
    key_value_weight,
    attn_output,
    gain_attn,
    mamba_input,
    mamba_select,
    step_bias,
    decay_log,
    state_skip,
    mamba_output,
    gain_mamba,
    gain_ffn,
    ffn_input,
    ffn_output,
):
    tokens, segments, cotangent = tokens[0], segments[0], cotangent[0]
    rows, width = tokens.shape
    shard = meta_tokens.shape[0]
    tp = lax.axis_size("tp")
    tp_index = lax.axis_index("tp")
    ctx_index = lax.axis_index("ctx")
    span = rows * tp
    query_width = query_weight.shape[1]
    keyval_width = key_value_weight.shape[1]
    heads = keyval_width // (2 * HEAD_SIZE)
    channels = mamba_input.shape[2]
    ff = ffn_input.shape[2] // tp
    meta_count = meta_tokens.shape[1]
    window = WIN + rows

    gains = jnp.stack([gain_mix, gain_attn, gain_mamba, gain_ffn], axis=1)
    flat_input = mamba_input.reshape(shard, 3 * channels)
    first = gather_rows([key_value_weight, meta_tokens, query_weight, flat_input, mamba_select, gains])
    second = gather_rows([mamba_output, attn_output])
    ffn_up_shard = lax.dynamic_slice_in_dim(ffn_input, tp_index * ff, ff, 2).reshape(shard, 2 * ff)
    ffn_down_shard = lax.dynamic_slice_in_dim(ffn_output, tp_index * ff, ff, 1)
    third = gather_rows([ffn_up_shard, ffn_down_shard])
    tokens_group = lax.all_gather(tokens, "tp", axis=0, tiled=True)
    cotangent_group = lax.all_gather(cotangent, "tp", axis=0, tiled=True)

    keyval_map, meta_full, query_map, state_map, select_map, gain_columns = cut(
        first, [keyval_width, meta_count, query_width, 3 * channels, 2 * STATE, 4]
    )
    state_out_map, attn_map = cut(second, [channels, query_width])
    up_map, down_map = cut(third, [2 * ff, ff])
    gain_rows = gain_columns.astype(f32).T
    mix_gain, attn_gain, mamba_gain, ffn_gain = [gain_rows[k : k + 1] for k in range(4)]

    residual = tokens.astype(f32)
    residual_group = tokens_group.astype(f32)
    normed = rms_norm(residual, mix_gain).astype(bf16)
    normed_group = rms_norm(residual_group, mix_gain).astype(bf16)
    meta_rows = meta_full.astype(f32).T
    meta_normed = rms_norm(meta_rows, mix_gain).astype(bf16)

    query_t = dot(query_map, normed, 0, 1).astype(bf16)
    keyval_group_t = dot(keyval_map, normed_group, 0, 1).astype(bf16)
    meta_keyval_t = dot(keyval_map, meta_normed, 0, 1).astype(bf16)
    selects = dot(normed_group, select_map, 1, 0).astype(bf16)
    selects_t = selects.T
    earlier_t = lax.ppermute(keyval_group_t, "ctx", [(0, 1)])
    mixed = dot(normed_group, state_map, 1, 0)

    key_start = span + tp_index * rows - WIN
    keyval_t = jnp.concatenate(
        [
            meta_keyval_t,
            lax.dynamic_slice_in_dim(
                jnp.concatenate([earlier_t, keyval_group_t], axis=1), key_start, window, 1
            ),
        ],
        axis=1,
    )
    query_pos = ctx_index * span + tp_index * rows + jnp.arange(rows, dtype=jnp.int32)
    key_pos = (ctx_index - 1) * span + key_start + jnp.arange(window, dtype=jnp.int32)
    seg_current = lax.dynamic_slice_in_dim(segments, ctx_index * span, span, 0)
    seg_earlier = lax.dynamic_slice_in_dim(segments, jnp.maximum(ctx_index - 1, 0) * span, span, 0)
    seg_query = lax.dynamic_slice_in_dim(seg_current, tp_index * rows, rows, 0)
    seg_keys = lax.dynamic_slice_in_dim(
        jnp.concatenate([seg_earlier, seg_current]), key_start, window, 0
    )
    keep = (
        (key_pos[:, None] <= query_pos[None, :])
        & (query_pos[None, :] - key_pos[:, None] < WIN)
        & (key_pos[:, None] >= 0)
        & (seg_keys[:, None] == seg_query[None, :])
    )
    bias = jnp.concatenate(
        [jnp.zeros((meta_count, rows), f32), jnp.where(keep, 0.0, masked_score)], axis=0
    )
    attended_t, log_total = attend(query_t, keyval_t, bias, heads)
    attended_columns = lax.all_to_all(
        attended_t.reshape(tp, query_width // tp, rows), "tp", 0, 0
    )

    seg_before = jnp.where(
        ctx_index > 0,
        lax.dynamic_index_in_dim(segments, jnp.maximum(ctx_index * span - 1, 0), 0, False),
        -1,
    )
    aux = scan_aux(seg_current, seg_before)
    bias_row = step_bias[None]
    rate_row = jnp.exp(decay_log)[None]
    skip_row = state_skip[None]
    state_end = end_state(mixed, selects_t, aux, bias_row, rate_row)
    state_start = lax.ppermute(state_end, "ctx", [(0, 1)])
    gated, states, state_final = forward_scan(
        mixed, selects, selects_t, aux, bias_row, rate_row, skip_row, state_start
    )
    mamba_part = dot(gated, state_out_map, 1, 1).astype(bf16)
    mamba_out = lax.psum_scatter(mamba_part, "tp", scatter_dimension=0, tiled=True).astype(f32)
    attn_out = dot(attended_t, attn_map, 0, 1)
    mid = residual + 0.5 * (rms_norm(attn_out, attn_gain) + rms_norm(mamba_out, mamba_gain))
    ffn_normed = rms_norm(mid, ffn_gain).astype(bf16)
    ffn_normed_group = lax.all_gather(ffn_normed, "tp", axis=0, tiled=True)

    gate_up = dot(ffn_normed_group, up_map, 1, 0)
    gate, up = gate_up[:, :ff], gate_up[:, ff:]
    sigma = jax.nn.sigmoid(gate)
    hidden = (gate * sigma * up).astype(bf16)
    hidden_grad = dot(cotangent_group, down_map, 1, 0)
    gate_up_grad = jnp.concatenate(
        [
            (hidden_grad * up * (sigma * (1.0 + gate * (1.0 - sigma)))).astype(bf16),
            (hidden_grad * gate * sigma).astype(bf16),
        ],
        axis=1,
    )
    ffn_grad_part = dot(gate_up_grad, up_map, 1, 1).astype(bf16)
    ffn_normed_grad = lax.psum_scatter(
        ffn_grad_part, "tp", scatter_dimension=0, tiled=True
    ).astype(f32)
    out_part = dot(hidden, down_map, 1, 1).astype(bf16)
    layer_out = (
        mid + lax.psum_scatter(out_part, "tp", scatter_dimension=0, tiled=True).astype(f32)
    ).astype(bf16)

    mid_extra, ffn_gain_terms = rms_back(mid, ffn_gain, ffn_normed_grad)
    mid_grad = cotangent.astype(f32) + mid_extra
    attn_grad, attn_gain_terms = rms_back(attn_out, attn_gain, 0.5 * mid_grad)
    mamba_grad, mamba_gain_terms = rms_back(mamba_out, mamba_gain, 0.5 * mid_grad)
    attn_grad = attn_grad.astype(bf16)
    mamba_grad = mamba_grad.astype(bf16)
    mamba_grad_group = lax.all_gather(mamba_grad, "tp", axis=0, tiled=True)
    attn_grad_group = lax.all_gather(attn_grad, "tp", axis=0, tiled=True)

    attended_grad_t = dot(attn_map, attn_grad, 0, 1).astype(bf16)
    query_grad_t, key_grad_t, value_grad_t = attend_back(
        query_t, keyval_t, bias, attended_t, log_total, attended_grad_t, heads
    )
    gated_grad = dot(mamba_grad_group, state_out_map, 1, 0)
    adjoint_end = end_adjoint(gated_grad, mixed, selects_t, aux, bias_row, rate_row)
    adjoint_start = lax.ppermute(adjoint_end, "ctx", [(1, 0)])
    mix_grad, select_grad, scan_sums = backward_scan(
        gated_grad,
        mixed,
        selects,
        selects_t,
        states,
        aux,
        bias_row,
        rate_row,
        skip_row,
        adjoint_start,
        state_final,
    )

    keyval_grad_t = jnp.concatenate([key_grad_t, value_grad_t], axis=0).astype(bf16)
    placed = lax.dynamic_update_slice_in_dim(
        jnp.zeros((keyval_width, 2 * span), bf16), keyval_grad_t[:, meta_count:], key_start, 1
    )
    earlier_back = lax.ppermute(placed[:, :span], "ctx", [(1, 0)])
    current = placed[:, span:].astype(f32) + earlier_back.astype(f32)
    with_meta = jnp.concatenate([keyval_grad_t[:, :meta_count], current.astype(bf16)], axis=1)
    select_rows = jnp.concatenate(
        [jnp.zeros((2 * STATE, meta_count), bf16), select_grad.T.astype(bf16)], axis=1
    )
    columns = jnp.concatenate(
        [
            with_meta.reshape(tp, keyval_width // tp, meta_count + span),
            select_rows.reshape(tp, 2 * STATE // tp, meta_count + span),
        ],
        axis=1,
    )
    columns = lax.psum_scatter(columns, "tp", scatter_dimension=0, tiled=True)[0]
    keyval_columns_t = columns[: keyval_width // tp]
    select_columns_t = columns[keyval_width // tp :, meta_count:]
    query_columns = lax.all_to_all(
        query_grad_t.reshape(tp, query_width // tp, rows), "tp", 0, 0
    )

    keyval_part = lax.dynamic_slice_in_dim(
        keyval_map, tp_index * (keyval_width // tp), keyval_width // tp, 1
    )
    query_term = dot(query_grad_t, query_map, 0, 1)
    normed_grad_part = (
        dot(mix_grad, state_map, 1, 1)
        + dot(select_grad.astype(bf16), select_map, 1, 1)
        + dot(keyval_columns_t[:, meta_count:], keyval_part, 0, 1)
    )
    meta_grad_part = dot(keyval_columns_t[:, :meta_count], keyval_part, 0, 1)
    _, group_terms = rms_back(residual_group, mix_gain, normed_grad_part)
    _, meta_terms = rms_back(meta_rows, mix_gain, meta_grad_part)
    _, query_terms = rms_back(residual, mix_gain, query_term)
    mix_gain_sum = jnp.sum(group_terms, 0) + jnp.sum(meta_terms, 0) + jnp.sum(query_terms, 0)
    gain_sums = jnp.stack(
        [
            mix_gain_sum,
            jnp.sum(attn_gain_terms, 0),
            jnp.sum(mamba_gain_terms, 0),
            jnp.sum(ffn_gain_terms, 0),
        ]
    ).astype(bf16)
    gain_block = jnp.concatenate([gain_sums, jnp.zeros((4, width), bf16)])
    extended = jnp.concatenate(
        [
            normed_grad_part.astype(bf16).reshape(tp, rows, width),
            meta_grad_part.astype(bf16).reshape(tp, meta_count // tp, width),
            jnp.broadcast_to(gain_block[None], (tp, 8, width)),
        ],
        axis=1,
    )
    extended = lax.psum_scatter(extended, "tp", scatter_dimension=0, tiled=True)[0].astype(f32)
    normed_grad = extended[:rows] + query_term
    residual_extra, _ = rms_back(residual, mix_gain, normed_grad)
    grad_tokens = (mid_grad + residual_extra).astype(bf16)
    own_meta_rows = lax.dynamic_slice_in_dim(
        meta_rows, tp_index * (meta_count // tp), meta_count // tp, 0
    )
    own_meta_grad, _ = rms_back(own_meta_rows, mix_gain, extended[rows : rows + meta_count // tp])
    gain_totals = extended[rows + meta_count // tp :][:4]

    ffn_columns = scatter_rows(
        [dot(ffn_normed_group, gate_up_grad, 0, 0), dot(cotangent_group, hidden, 0, 0)]
    ).astype(f32)
    attended_wide = jnp.swapaxes(attended_columns, 1, 2).reshape(span, query_width // tp)
    query_wide = jnp.swapaxes(query_columns, 1, 2).reshape(span, query_width // tp)
    out_columns = scatter_rows(
        [dot(mamba_grad_group, gated, 0, 0), dot(attn_grad_group, attended_wide, 0, 0)]
    ).astype(f32)
    vector_columns = -(-3 * channels // shard)
    vectors = jnp.pad(scan_sums[:3].reshape(-1), (0, vector_columns * shard - 3 * channels))
    vectors = jnp.tile(vectors.reshape(shard, vector_columns), (width // shard, 1))
    last_columns = scatter_rows(
        [
            dot(normed_group, mix_grad, 0, 0),
            dot(normed_group, query_wide, 0, 0),
            dot(normed_group, keyval_columns_t[:, meta_count:], 0, 1)
            + dot(meta_normed, keyval_columns_t[:, :meta_count], 0, 1),
            dot(normed_group, select_columns_t, 0, 1),
            own_meta_grad.T,
            gain_totals.T,
            vectors,
        ]
    ).astype(f32)
    grad_ffn_input, grad_ffn_output = cut(ffn_columns, [2 * ff, ff])
    grad_mamba_output, grad_attn_output = cut(out_columns, [channels, query_width // tp])
    grad_mamba_input, grad_query, grad_keyval, grad_select, grad_meta, grad_gains, grad_vectors = cut(
        last_columns,
        [
            3 * channels,
            query_width // tp,
            keyval_width // tp,
            2 * STATE // tp,
            meta_count // tp,
            4,
            vector_columns,
        ],
    )
    grad_vectors = grad_vectors.reshape(-1)[: 3 * channels].reshape(3, channels)
    return (
        layer_out[None],
        grad_tokens[None],
        grad_meta,
        grad_gains[:, 0],
        grad_query,
        grad_keyval,
        grad_attn_output,
        grad_gains[:, 1],
        grad_mamba_input.reshape(shard, 3, channels),
        grad_select,
        grad_vectors[0],
        grad_vectors[1],
        grad_vectors[2],
        grad_mamba_output,
        grad_gains[:, 2],
        grad_gains[:, 3],
        grad_ffn_input.reshape(shard, 2, ff),
        grad_ffn_output,
    )


def solution(mesh):
    rows = ("fsdp", "ctx")
    in_specs = (
        P("fsdp", ("ctx", "tp"), None),
        P("fsdp", None),
        P("fsdp", ("ctx", "tp"), None),
        P(rows, None),
        P(rows),
        P(rows, None),
        P(rows, None),
        P(rows, None),
        P(rows),
        P(rows, None, "tp"),
        P(rows, None),
        P("tp"),
        P("tp"),
        P("tp"),
        P(rows, "tp"),
        P(rows),
        P(rows),
        P(rows, None, None),
        P(rows, None),
    )
    out_specs = (
        P("fsdp", ("ctx", "tp"), None),
        P("fsdp", ("ctx", "tp"), None),
        P(rows, "tp"),
        P(rows),
        P(rows, "tp"),
        P(rows, "tp"),
        P(rows, "tp"),
        P(rows),
        P(rows, None, "tp"),
        P(rows, "tp"),
        P("tp"),
        P("tp"),
        P("tp"),
        P(rows, "tp"),
        P(rows),
        P(rows),
        P(rows, None, "tp"),
        P(rows, "tp"),
    )
    return jax.shard_map(
        per_device, mesh=mesh, in_specs=in_specs, out_specs=out_specs, check_vma=False
    )
```

profile of v0, /device:TPU:0, one launch (start us, length us, event | category | flops | bytes accessed | tf_op | source)
XLA Modules:
  0.0 1312.0 jit_solution(12646680298905054213)
XLA Ops:
  22.6 55.4 %all-gather.23.cloned.1.call-done = bf16[1,1024,1600]{1,2,0:T(8,128)(2,1)} async-done(((bf16[1,256,1600]{1,2,0:T(8,128)(2,1)}), bf16[1,1024,1600]{1,2,0:T(8,128)(2,1)}) %all-gather.23.cloned.1.call-update) | async-done | bytes 3276816 | tf_op jit(solution)/shard_map/all_gather | solution.py:500
  80.7 82.7 %all-gather.11.cloned.1.call-done = bf16[1600,4804]{1,0:T(8,128)(2,1)} async-done(((bf16[200,4804]{1,0:T(8,128)(2,1)}), bf16[1600,4804]{1,0:T(8,128)(2,1)}) %all-gather.11.cloned.1.call-update) | async-done | bytes 15372816 | tf_op jit(solution)/shard_map/all_gather | solution.py:440
  169.4 15.3 %fusion.8.mixed = f32[1024,2400]{1,0:T(8,128)} fusion(bf16[1024,1600]{0,1:T(8,128)(2,1)S(1)} %fusion.10, bf16[1600,4804]{1,0:T(8,128)(2,1)} %all-gather.11.cloned.1.call-done), kind=kOutput, calls=%fused_computation.14 | convolution fusion | flops 7864320000 | bytes 20889600 | tf_op jit(solution)/shard_map/dot_general | solution.py:434
  184.6 12.5 shard_map.323
  200.2 18.9 %shard_map.324 = (bf16[1024,800]{1,0:T(8,128)(2,1)S(1)}, bf16[4096,800]{1,0:T(8,128)(2,1)}, f32[16,800]{1,0:T(8,128)S(1)}) custom-call(f32[1024,2400]{1,0:T(8,128)} %fusion.8.mixed, bf16[1024,32]{1,0:T(8,128)(2,1)S(1)} %copy.194.select, bf16[32,1024]{1,0:T(8,128)(2,1)S(1)} %bitcast.152, f32[1024,8]{1,0:T(8,128)S(1)} %copy.195.aux, ...), custom_call_target="tpu_custom_call" | custom-call | tf_op jit(solution)/shard_map/pallas_call | solution.py:301
  220.3 7.7 convolution_convert_fusion.3
  260.9 24.9 %shard_map.322 = (bf16[1600,256]{1,0:T(8,128)(2,1)}, f32[5,8,256]{2,1,0:T(8,128)}) custom-call(bf16[1600,256]{1,0:T(8,128)(2,1)} %fusion.45.query_t, bf16[640,1408]{1,0:T(8,128)(2,1)} %pad_maximum_fusion.6.key_t.value_t, bf16[640,1408]{1,0:T(8,128)(2,1)} %pad_maximum_fusion.6.key_t.value_t, f32[1408,256]{1,0:T(8,128)} %concatenate.68.bias), custom_call_target="tpu_custom_call" | custom-call | tf_op jit(solution)/shard_map/pallas_call | solution.py:381
  298.0 70.4 %all-gather.17.cloned.1.call-done = bf16[1600,4128]{1,0:T(8,128)(2,1)} async-done(((bf16[200,4128]{1,0:T(8,128)(2,1)}), bf16[1600,4128]{1,0:T(8,128)(2,1)}) %all-gather.17.cloned.1.call-update) | async-done | bytes 13209616 | tf_op jit(solution)/shard_map/all_gather | solution.py:440
  368.4 67.6 %all-gather.15.cloned.1.call-done = bf16[1024,1600]{0,1:T(8,128)(2,1)} async-done(((bf16[256,1600]{0,1:T(8,128)(2,1)}), bf16[1024,1600]{0,1:T(8,128)(2,1)}) %all-gather.15.cloned.1.call-update) | async-done | bytes 3276816 | tf_op jit(solution)/shard_map/all_gather | solution.py:577
  436.0 16.6 %fusion.2 = f32[1024,2752]{0,1:T(8,128)} fusion(bf16[1024,1600]{0,1:T(8,128)(2,1)} %all-gather.15.cloned.1.call-done, bf16[1600,4128]{1,0:T(8,128)(2,1)} %all-gather.17.cloned.1.call-done), kind=kOutput, calls=%fused_computation.7 | convolution fusion | flops 9017753600 | bytes 23560192 | tf_op jit(solution)/shard_map/dot_general | solution.py:434
  452.6 48.8 %all-gather.25.cloned.1.call-done = bf16[1,1024,1600]{1,2,0:T(8,128)(2,1)} async-done(((bf16[1,256,1600]{1,2,0:T(8,128)(2,1)}), bf16[1,1024,1600]{1,2,0:T(8,128)(2,1)}) %all-gather.25.cloned.1.call-update) | async-done | bytes 3276816 | tf_op jit(solution)/shard_map/all_gather | solution.py:501
  501.3 17.6 %fusion.15 = (bf16[1024,1376]{0,1:T(8,128)(2,1)S(1)}, bf16[1024,1376]{0,1:T(8,128)(2,1)}, bf16[1024,1376]{0,1:T(8,128)(2,1)}) fusion(f32[1024,2752]{0,1:T(8,128)} %fusion.2, bf16[1,1024,1600]{1,2,0:T(8,128)(2,1)} %all-gather.25.cloned.1.call-done, bf16[1600,4128]{1,0:T(8,128)(2,1)} %all-gather.17.cloned.1.call-done), kind=kOutput, calls=%fused_computation.25 | convolution fusion | flops 4531421184 | bytes 27508736 | tf_op jit(solution)/shard_map/dot_general | solution.py:434
  520.5 12.7 fusion.35
  533.3 9.3 fusion.32
  542.6 51.3 %reduce-scatter.16.cloned.1.call-done = bf16[256,1600]{0,1:T(8,128)(2,1)} async-done(((bf16[1024,1600]{0,1:T(8,128)(2,1)}), bf16[256,1600]{0,1:T(8,128)(2,1)}) %reduce-scatter.16.cloned.1.call-update) | async-done | bytes 819216 | tf_op jit(solution)/shard_map/reduce_scatter | solution.py:592
  595.8 62.8 %reduce-scatter.14.cloned.1.call-done = bf16[256,1600]{0,1:T(8,128)(2,1)} async-done(((bf16[1024,1600]{0,1:T(8,128)(2,1)}), bf16[256,1600]{0,1:T(8,128)(2,1)}) %reduce-scatter.14.cloned.1.call-update) | async-done | bytes 819216 | tf_op jit(solution)/shard_map/reduce_scatter | solution.py:597
  672.5 27.7 %shard_map.327 = (bf16[1600,256]{1,0:T(8,128)(2,1)}, f32[320,1408]{1,0:T(8,128)}, f32[320,1408]{1,0:T(8,128)}) custom-call(bf16[1600,256]{1,0:T(8,128)(2,1)} %fusion.45.query_t, bf16[640,1408]{1,0:T(8,128)(2,1)} %pad_maximum_fusion.6.key_t.value_t, bf16[640,1408]{1,0:T(8,128)(2,1)} %pad_maximum_fusion.6.key_t.value_t, f32[1408,256]{1,0:T(8,128)} %concatenate.68.bias, ...), custom_call_target="tpu_custom_call" | custom-call | tf_op jit(solution)/shard_map/pallas_call | solution.py:405
  709.8 21.3 %all-gather.19.cloned.1.call-done = bf16[1024,1600]{0,1:T(8,128)(2,1)} async-done(((bf16[256,1600]{0,1:T(8,128)(2,1)}), bf16[1024,1600]{0,1:T(8,128)(2,1)}) %all-gather.19.cloned.1.call-update) | async-done | bytes 3276816 | tf_op jit(solution)/shard_map/all_gather | solution.py:606
  738.0 12.3 shard_map.325
  753.5 40.5 %shard_map.326 = (bf16[1024,2400]{1,0:T(8,128)(2,1)}, f32[1024,32]{1,0:T(8,128)S(1)}, f32[8,800]{1,0:T(8,128)S(1)}) custom-call(f32[1024,800]{1,0:T(8,128)S(1)} %fusion.48.gated_grad, f32[1024,2400]{1,0:T(8,128)} %fusion.8.mixed, bf16[1024,32]{1,0:T(8,128)(2,1)S(1)} %copy.194.select, bf16[32,1024]{1,0:T(8,128)(2,1)S(1)} %bitcast.154, ...), custom_call_target="tpu_custom_call" | custom-call | tf_op jit(solution)/shard_map/pallas_call | solution.py:326
  810.7 52.2 %all-reduce.7.cloned.1.call-done = bf16[4,168,1152]{2,1,0:T(8,128)(2,1)} async-done(((bf16[4,168,1152]{2,1,0:T(8,128)(2,1)}), bf16[4,168,1152]{2,1,0:T(8,128)(2,1)}) %all-reduce.7.cloned.1.call-update) | async-done | bytes 1548304
  871.7 18.6 %fusion.130 = (bf16[1024,1600]{0,1:T(8,128)(2,1)}, f32[1600]{0:T(1024)S(1)}) fusion(f32[1024]{0:T(1024)S(1)} %copy-done.34, bf16[1,1024,1600]{1,2,0:T(8,128)(2,1)} %all-gather.23.cloned.1.call-done, f32[1024,1600]{0,1:T(8,128)} %fusion.105, f32[1024,1600]{0,1:T(8,128)} %fusion.110, bf16[1024,2400]{1,0:T(8,128)(2,1)} %get-tuple-element.33, ...), kind=kOutput, calls=%fused_computation.224 | convolution fusion | flops 7875787264 | bytes 32434432 | tf_op jit(solution)/shard_map/dot_general | solution.py:434
  910.3 36.0 %all_to_all.10 = bf16[4,400,256]{2,1,0:T(8,128)(2,1)S(1)} all-to-all(bf16[4,400,256]{2,1,0:T(8,128)(2,1)S(1)} %bitcast.162), channel_id=1, replica_groups=mesh['fsdp'=4,'ctx'=2,'tp'=4] {'tp'}, dimensions={0} | all-to-all | bytes 1638400 | tf_op jit(solution)/shard_map/all_to_all | solution.py:554
  963.7 9.2 fusion.13
  972.8 12.9 convolution_convert_fusion
  985.7 10.4 pad_maximum_fusion
  1001.1 45.0 %all-to-all-done = bf16[4,400,256]{2,1,0:T(8,128)(2,1)S(1)} async-done(((bf16[4,400,256]{2,1,0:T(8,128)(2,1)}), bf16[4,400,256]{2,1,0:T(8,128)(2,1)S(1)}, u32[]{:S(2)}, u32[]{:S(2)}) %all-to-all-start) | async-done | bytes 819232 | tf_op jit(solution)/shard_map/all_to_all | solution.py:650
  1052.5 13.7 %convolution_convert_fusion.1 = bf16[1600,2400]{1,0:T(8,128)(2,1)} fusion(bf16[1024,1600]{0,1:T(8,128)(2,1)} %copy-done.4, bf16[1024,2400]{1,0:T(8,128)(2,1)} %get-tuple-element.33), kind=kOutput, calls=%fused_computation.2 | convolution fusion | flops 7868160000 | bytes 15872000 | tf_op jit(solution)/shard_map/dot_general | solution.py:434
  1080.9 16.5 %concatenate.82 = bf16[1600,3016]{1,0:T(8,128)(2,1)} concatenate(bf16[1600,2400]{1,0:T(8,128)(2,1)} %convolution_convert_fusion.1, bf16[1600,400]{1,0:T(8,128)(2,1)} %copy.210, bf16[1600,160]{1,0:T(8,128)(2,1)S(1)} %copy.211, bf16[1600,8]{1,0:T(8,128)(2,1)S(1)} %copy.212, bf16[1600,32]{1,0:T(8,128)(2,1)} %fusion.109, bf16[1600,4]{1,0:T(8,128)(2,1)S(1)} %slice_bitcast_fusion.2, ...), dimensions={1} | concatenate | bytes 19302400 | tf_op jit(solution)/shard_map/concatenate | solution.py:444
  1097.5 10.9 reduce-scatter.22.cloned.1.call-done
  1112.1 98.3 %reduce-scatter.24.cloned.1.call-done = bf16[200,4128]{1,0:T(8,128)(2,1)} async-done(((bf16[1600,4128]{1,0:T(8,128)(2,1)}), bf16[200,4128]{1,0:T(8,128)(2,1)}) %reduce-scatter.24.cloned.1.call-update) | async-done | bytes 1651216
  1223.9 68.2 %reduce-scatter.20.cloned.1.call-done = bf16[200,3016]{1,0:T(8,128)(2,1)} async-done(((bf16[1600,3016]{1,0:T(8,128)(2,1)}), bf16[200,3016]{1,0:T(8,128)(2,1)}) %reduce-scatter.20.cloned.1.call-update) | async-done | bytes 1206416 | tf_op jit(solution)/shard_map/reduce_scatter | solution.py:445
  (295 shorter events, 227.9 us)
Async XLA Ops:
  7.2 229.0 %copy-start = (bf16[200,5504]{1,0:T(8,128)(2,1)S(1)}, bf16[200,5504]{1,0:T(8,128)(2,1)}, u32[]{:S(2)}) copy-start(bf16[200,5504]{1,0:T(8,128)(2,1)} %param.37) | copy-start | bytes 6604804
  7.3 70.7 %all-gather.23.cloned.1.call-start = ((), (), s32[]{:S(2)}) async-start(), calls=%async_computation.20 | async-start | bytes 4096000 | tf_op jit(solution)/shard_map/all_gather | solution.py:500
  8.0 155.4 %all-gather.11.cloned.1.call-start = ((), (), s32[]{:S(2)}) async-start(), calls=%async_computation.9 | async-start | bytes 17510400 | tf_op jit(solution)/shard_map/all_gather | solution.py:440
  17.1 203.1 %all-gather.13.cloned.1.call-start = ((), (), s32[]{:S(2)}) async-start(), calls=%async_computation.10 | async-start | bytes 8755200 | tf_op jit(solution)/shard_map/all_gather | solution.py:440
  18.5 273.6 %reduce-scatter.12.cloned.1.call-start = ((), (), s32[]{:S(2)}) async-start(), calls=%async_computation.11 | async-start | bytes 4096000 | tf_op jit(solution)/shard_map/reduce_scatter | solution.py:573
  80.6 85.7 %copy-start.33 = (f32[1024]{0:T(1024)}, f32[1024]{0:T(1024)S(1)}, u32[]{:S(2)}) copy-start(f32[1024]{0:T(1024)S(1)} %add_rsqrt_fusion) | copy-start | bytes 12292
  166.3 87.0 %copy-start.27 = (f32[1600]{0:T(1024)}, f32[1600]{0:T(1024)S(1)}, u32[]{:S(2)}) copy-start(f32[1600]{0:T(1024)S(1)} %get-tuple-element.145) | copy-start | bytes 19204
  167.1 17.5 %copy-start.4 = (bf16[1024,1600]{0,1:T(8,128)(2,1)}, bf16[1024,1600]{0,1:T(8,128)(2,1)S(1)}, u32[]{:S(2)}) copy-start(bf16[1024,1600]{0,1:T(8,128)(2,1)S(1)} %fusion.10) | copy-start | bytes 9830404
  184.6 15.0 %copy-start.37 = (f32[800]{0:T(1024)S(1)}, f32[800]{0:T(1024)}, u32[]{:S(2)}) copy-start(f32[800]{0:T(1024)} %param.32) | copy-start | bytes 9604
  197.1 3.0 collective-permute-start.1
  228.0 140.4 %all-gather.17.cloned.1.call-start = ((), (), s32[]{:S(2)}) async-start(), calls=%async_computation.13 | async-start | bytes 15206400 | tf_op jit(solution)/shard_map/all_gather | solution.py:440
  239.3 196.7 %all-gather.15.cloned.1.call-start = ((), (), s32[]{:S(2)}) async-start(), calls=%async_computation.12 | async-start | bytes 4096000 | tf_op jit(solution)/shard_map/all_gather | solution.py:577
  245.6 13.2 %collective-permute-start = (bf16[640,1024]{1,0:T(8,128)(2,1)S(1)}, bf16[640,1024]{1,0:T(8,128)(2,1)S(1)}, u32[]{:S(2)}, u32[]{:S(2)}) collective-permute-start(bf16[640,1024]{1,0:T(8,128)(2,1)S(1)} %convolution_convert_fusion.8), channel_id=1, source_target_pairs={{0,4},{1,5},{2,6},{3,7},{8,12},{9,13},{10,14},{11,15},{16,20},{17,... | collective-permute-start | bytes 3932168 | tf_op jit(solution)/shard_map/ppermute | solution.py:523
  297.0 204.3 %all-gather.25.cloned.1.call-start = ((), (), s32[]{:S(2)}) async-start(), calls=%async_computation.21 | async-start | bytes 4096000 | tf_op jit(solution)/shard_map/all_gather | solution.py:501
  297.7 296.2 %reduce-scatter.16.cloned.1.call-start = ((), (), s32[]{:S(2)}) async-start(), calls=%async_computation.15 | async-start | bytes 4096000 | tf_op jit(solution)/shard_map/reduce_scatter | solution.py:592
  501.3 19.2 %copy-start.42 = (bf16[1600,4128]{1,0:T(8,128)(2,1)S(1)}, bf16[1600,4128]{1,0:T(8,128)(2,1)}, u32[]{:S(2)}) copy-start(bf16[1600,4128]{1,0:T(8,128)(2,1)} %all-gather.17.cloned.1.call-done) | copy-start | bytes 39628804
  533.3 125.4 %reduce-scatter.14.cloned.1.call-start = ((), (), s32[]{:S(2)}) async-start(), calls=%async_computation.14 | async-start | bytes 4096000 | tf_op jit(solution)/shard_map/reduce_scatter | solution.py:597
  542.6 188.5 %all-gather.19.cloned.1.call-start = ((), (), s32[]{:S(2)}) async-start(), calls=%async_computation.16 | async-start | bytes 4096000 | tf_op jit(solution)/shard_map/all_gather | solution.py:606
  665.2 7.2 copy-start.21
  665.3 197.6 %all-reduce.7.cloned.1.call-start = ((), (), s32[]{:S(2)}) async-start(), calls=%async_computation.23 | async-start | bytes 3096576
  703.3 4.9 collective-permute-start.3
  738.0 13.6 %copy-start.17 = (bf16[320,1408]{1,0:T(8,128)(2,1)S(1)}, bf16[320,1408]{1,0:T(8,128)(2,1)}, u32[]{:S(2)}) copy-start(bf16[320,1408]{1,0:T(8,128)(2,1)} %copy-done.16) | copy-start | bytes 2703364
  738.0 13.6 %copy-start.20 = (bf16[640,1024]{1,0:T(8,128)(2,1)S(1)}, bf16[640,1024]{1,0:T(8,128)(2,1)}, u32[]{:S(2)}) copy-start(bf16[640,1024]{1,0:T(8,128)(2,1)} %add_convert_fusion) | copy-start | bytes 3932164
  750.4 3.1 collective-permute-start.2
  753.5 40.7 %copy-start.19 = (bf16[640,1152]{1,0:T(8,128)(2,1)S(1)}, bf16[640,1152]{1,0:T(8,128)(2,1)}, u32[]{:S(2)}) copy-start(bf16[640,1152]{1,0:T(8,128)(2,1)} %fusion.87) | copy-start | bytes 4423684
  795.5 151.8 %all-gather.21.cloned.1.call-start = ((), (), s32[]{:S(2)}) async-start(), calls=%async_computation.19 | async-start | bytes 4096000 | tf_op jit(solution)/shard_map/all_gather | solution.py:607
  796.1 280.0 %reduce-scatter.18.cloned.1.call-start = ((), (), s32[]{:S(2)}) async-start(), calls=%async_computation.17 | async-start | bytes 6144000 | tf_op jit(solution)/shard_map/reduce_scatter | solution.py:685
  909.1 199.2 %reduce-scatter.22.cloned.1.call-start = ((), (), s32[]{:S(2)}) async-start(), calls=%async_computation.22 | async-start | bytes 4608000
  963.6 246.8 %reduce-scatter.24.cloned.1.call-start = ((), (), s32[]{:S(2)}) async-start(), calls=%async_computation.24 | async-start | bytes 15206400
  996.2 50.0 %all-to-all-start = ((bf16[4,400,256]{2,1,0:T(8,128)(2,1)}), bf16[4,400,256]{2,1,0:T(8,128)(2,1)S(1)}, u32[]{:S(2)}, u32[]{:S(2)}) async-start(bf16[4,400,256]{2,1,0:T(8,128)(2,1)} %bitcast.27), calls=%async_computation.4 | async-start | bytes 1638400 | tf_op jit(solution)/shard_map/all_to_all | solution.py:650
  999.7 292.5 %reduce-scatter.20.cloned.1.call-start = ((), (), s32[]{:S(2)}) async-start(), calls=%async_computation.18 | async-start | bytes 11059200 | tf_op jit(solution)/shard_map/reduce_scatter | solution.py:445
  1052.5 13.7 %copy-start.5 = (bf16[1024,1600]{0,1:T(8,128)(2,1)S(1)}, bf16[1024,1600]{0,1:T(8,128)(2,1)}, u32[]{:S(2)}) copy-start(bf16[1024,1600]{0,1:T(8,128)(2,1)} %copy-done.4) | copy-start | bytes 9830404
  (35 other events, 131.7 us)
Sparse Core Ops, SparseCore 0:
  9.7 68.2 all-gather.22
  80.4 82.9 all-gather.10
  165.8 51.8 all-gather.12
  228.1 62.3 reduce-scatter.11
  292.2 76.1 all-gather.16
  370.4 65.5 all-gather.14
  437.6 63.7 all-gather.24
  533.4 60.4 reduce-scatter.15
  596.2 62.3 reduce-scatter.13
  665.4 65.6 all-gather.18
  795.6 67.2 all-reduce.6
  864.3 82.1 all-gather.20
  948.8 99.7 reduce-scatter.17
  1052.4 55.8 reduce-scatter.21
  1112.2 98.1 reduce-scatter.23
  1213.8 78.3 reduce-scatter.19
where the time goes:
time: 1320 us; the launch traced here: 1310 us
  waiting for transfers between devices  741 us (56%)
  matrix products  204 us (15%)
  Pallas kernels  137 us (10%)
  local copies, waits for them, and re-layouts  103 us (8%)
  other arithmetic  62 us (5%)
  blocking collectives  36 us (3%)
  between operations  16.1 us (1%)
    dot_general x27, matrix products, dot(): lax.dot_general(left, right, (((left_dim,), (right_dim,)), ((), ())), pre...  204 us
    unnamed x19, waiting for transfers between devices  164 us
    all_gather x3, waiting for transfers between devices, gather_rows(): lax.all_gather(jnp.concatenate(pieces, axis=1), ('fsdp', 'ctx'), axis=0,...  153 us
    reduce_scatter x1, waiting for transfers between devices, scatter_rows(): lax.psum_scatter(whole, ('fsdp', 'ctx'), scatter_dimension=0, tiled=True)  68.2 us
    all_gather x1, waiting for transfers between devices, per_device(): ffn_normed_group = lax.all_gather(ffn_normed, 'tp', axis=0, tiled=True)  67.6 us
    reduce_scatter x1, waiting for transfers between devices, per_device(): lax.psum_scatter(out_part, 'tp', scatter_dimension=0, tiled=True)  62.8 us
    all_gather x1, waiting for transfers between devices, per_device(): tokens_group = lax.all_gather(tokens, 'tp', axis=0, tiled=True)  55.4 us
    reduce_scatter x1, waiting for transfers between devices, per_device(): lax.psum_scatter(ffn_grad_part, 'tp', scatter_dimension=0, tiled=True)  51.3 us
  transfers between devices with their start and end apart: 21, of which 16 were waited for; matrix products, arithmetic and copies ran while one was open for 23% of the time, Pallas kernels for 6%

commit v1 on v0

--- a/solution.py
+++ b/solution.py
@@ -242,8 +242,11 @@
     sums[2:3, :] += jnp.sum(dy * x, axis=0, keepdims=True)
 
 
-def scan_specs(tiles, channels, back):
-    at = (lambda i: tiles - 1 - i) if back else (lambda i: i)
+def scan_specs(tokens, channels, back):
+    tiles = tokens // TILE
+
+    def at(i):
+        return tiles - 1 - i if back else i
 
     mixed = pl.BlockSpec((TILE, 3 * channels), lambda i: (at(i), 0))
     rows = pl.BlockSpec((TILE, channels), lambda i: (at(i), 0))
@@ -255,7 +258,21 @@
     last = pl.BlockSpec((TILE // SUB, 1), lambda i: (at(i), 0))
     row = pl.BlockSpec((1, channels), lambda i: (0, 0))
     state = pl.BlockSpec((STATE, channels), lambda i: (0, 0))
-    return mixed, rows, select, select_t, states, aux, aux_t, last, row, state
+    return tiles, mixed, rows, select, select_t, states, aux, aux_t, last, row, state
+
+
+def scan_call(kernel, name, tiles, in_specs, out_specs, out_shape, scratch, flops):
+    return pl.pallas_call(
+        kernel,
+        name=name,
+        grid=(tiles,),
+        in_specs=in_specs,
+        out_specs=out_specs,
+        scratch_shapes=scratch,
+        out_shape=out_shape,
+        compiler_params=PARAMS,
+        cost_estimate=pl.CostEstimate(flops=flops, bytes_accessed=1 << 24, transcendentals=0),
+    )
 
 
 def scan_scratch(channels):
@@ -284,63 +301,358 @@
 
 def end_state(mixed, select_t, aux, bias, rate):
     tokens, channels = mixed.shape[0], mixed.shape[1] // 3
-    tiles = tokens // TILE
-    mixed_s, rows, select_s, select_t_s, states_s, aux_s, aux_t_s, last_s, row, state = scan_specs(tiles, channels, False)
-    return pl.pallas_call(
-        end_state_kernel, grid=(tiles,),
-        in_specs=[mixed_s, select_t_s, aux_s, aux_t_s, last_s, row, row],
-        out_specs=state, out_shape=jax.ShapeDtypeStruct((STATE, channels), f32),
-        scratch_shapes=scan_scratch(channels), compiler_params=PARAMS,
+    tiles, mixed_s, rows, select_s, select_t_s, states_s, aux_s, aux_t_s, last_s, row, state = scan_specs(
+        tokens, channels, False
+    )
+    return scan_call(
+        end_state_kernel,
+        "end_state",
+        tiles,
+        [mixed_s, select_t_s, aux_s, aux_t_s, last_s, row, row],
+        state,
+        jax.ShapeDtypeStruct((STATE, channels), f32),
+        scan_scratch(channels),
+        10**10,
     )(mixed, select_t, *aux, bias, rate)
 
 
 def forward_scan(mixed, select, select_t, aux, bias, rate, skip, start):
     tokens, channels = mixed.shape[0], mixed.shape[1] // 3
-    tiles = tokens // TILE
-    mixed_s, rows, select_s, select_t_s, states_s, aux_s, aux_t_s, last_s, row, state = scan_specs(tiles, channels, False)
-    return pl.pallas_call(
-        forward_kernel, grid=(tiles,),
-        in_specs=[mixed_s, select_s, select_t_s, aux_s, aux_t_s, last_s, row, row, row, state],
-        out_specs=[rows, states_s, state],
-        out_shape=[jax.ShapeDtypeStruct((tokens, channels), bf16), jax.ShapeDtypeStruct((tokens // SUB * STATE, channels), bf16), jax.ShapeDtypeStruct((STATE, channels), f32)],
-        scratch_shapes=scan_scratch(channels), compiler_params=PARAMS,
+    tiles, mixed_s, rows, select_s, select_t_s, states_s, aux_s, aux_t_s, last_s, row, state = scan_specs(
+        tokens, channels, False
+    )
+    return scan_call(
+        forward_kernel,
+        "forward_scan",
+        tiles,
+        [mixed_s, select_s, select_t_s, aux_s, aux_t_s, last_s, row, row, row, state],
+        [rows, states_s, state],
+        [
+            jax.ShapeDtypeStruct((tokens, channels), bf16),
+            jax.ShapeDtypeStruct((tokens // SUB * STATE, channels), bf16),
+            jax.ShapeDtypeStruct((STATE, channels), f32),
+        ],
+        scan_scratch(channels),
+        16 * 10**9,
     )(mixed, select, select_t, *aux, bias, rate, skip, start)
 
 
 def end_adjoint(gated_grad, mixed, select_t, aux, bias, rate):
     tokens, channels = mixed.shape[0], mixed.shape[1] // 3
-    tiles = tokens // TILE
-    mixed_s, rows, select_s, select_t_s, states_s, aux_s, aux_t_s, last_s, row, state = scan_specs(tiles, channels, True)
-    return pl.pallas_call(
-        end_adjoint_kernel, grid=(tiles,),
-        in_specs=[rows, mixed_s, select_t_s, aux_s, aux_t_s, last_s, row, row],
-        out_specs=state, out_shape=jax.ShapeDtypeStruct((STATE, channels), f32),
-        scratch_shapes=scan_scratch(channels), compiler_params=PARAMS,
+    tiles, mixed_s, rows, select_s, select_t_s, states_s, aux_s, aux_t_s, last_s, row, state = scan_specs(
+        tokens, channels, True
+    )
+    return scan_call(
+        end_adjoint_kernel,
+        "end_adjoint",
+        tiles,
+        [rows, mixed_s, select_t_s, aux_s, aux_t_s, last_s, row, row],
+        state,
+        jax.ShapeDtypeStruct((STATE, channels), f32),
+        scan_scratch(channels),
+        10**10,
     )(gated_grad, mixed, select_t, *aux, bias, rate)
 
 
 def backward_scan(gated_grad, mixed, select, select_t, states, aux, bias, rate, skip, start, final):
     tokens, channels = mixed.shape[0], mixed.shape[1] // 3
-    tiles = tokens // TILE
-    mixed_s, rows, select_s, select_t_s, states_s, aux_s, aux_t_s, last_s, row, state = scan_specs(tiles, channels, True)
-    return pl.pallas_call(
-        backward_kernel, grid=(tiles,),
-        in_specs=[rows, mixed_s, select_s, select_t_s, states_s, aux_s, aux_t_s, last_s, row, row, row, state, state],
-        out_specs=[mixed_s, select_s, pl.BlockSpec((8, channels), lambda i: (0, 0))],
-        out_shape=[jax.ShapeDtypeStruct((tokens, 3 * channels), bf16), jax.ShapeDtypeStruct((tokens, 2 * STATE), f32), jax.ShapeDtypeStruct((8, channels), f32)],
-        scratch_shapes=scan_scratch(channels) + [
+    tiles, mixed_s, rows, select_s, select_t_s, states_s, aux_s, aux_t_s, last_s, row, state = scan_specs(
+        tokens, channels, True
+    )
+    return scan_call(
+        backward_kernel,
+        "backward_scan",
+        tiles,
+        [rows, mixed_s, select_s, select_t_s, states_s, aux_s, aux_t_s, last_s, row, row, row, state, state],
+        [mixed_s, select_s, pl.BlockSpec((8, channels), lambda i: (0, 0))],
+        [
+            jax.ShapeDtypeStruct((tokens, 3 * channels), bf16),
+            jax.ShapeDtypeStruct((tokens, 2 * STATE), f32),
+            jax.ShapeDtypeStruct((8, channels), f32),
+        ],
+        scan_scratch(channels)
+        + [
             pltpu.VMEM((TILE // SUB * STATE, channels), bf16),
             pltpu.VMEM((TILE // SUB, channels), f32),
             pltpu.VMEM((1, channels), f32),
         ],
-        compiler_params=PARAMS,
+        36 * 10**9,
     )(gated_grad, mixed, select, select_t, states, *aux, bias, rate, skip, start, final)
 
 
-PARAMS_A = pltpu.CompilerParams(vmem_limit_bytes=56 << 20, dimension_semantics=("arbitrary",))
-
-
-def attend_kernel(group, query_t, key_t, value_t, bias, out_t, log_total):
+MESH = pl.DeviceIdType.MESH
+COMM = {"has_side_effects": True}
+
+
+def neighbour_barrier(count):
+    place = lax.axis_index("tp")
+    ready = pltpu.get_barrier_semaphore()
+    sides = ((place < count - 1, place + 1), (place > 0, place - 1))
+    for there, other in sides:
+
+        @pl.when(there)
+        def _():
+            pl.semaphore_signal(ready, inc=1, device_id={"tp": other}, device_id_type=MESH)
+
+    peers = jnp.where(place < count - 1, 1, 0) + jnp.where(place > 0, 1, 0)
+    pl.semaphore_wait(ready, peers)
+
+
+def line_steps(count, source, target, copies, send_sems, recv_sems):
+    place = lax.axis_index("tp")
+    width = source.shape[1]
+
+    def at(owner):
+        return target.at[:, pl.ds(pl.multiple_of(owner * width, width), width)]
+
+    def local():
+        return pltpu.make_async_copy(source, at(place), copies)
+
+    def remote(side, step):
+        owner = place - step if side == 0 else place + step
+        return pltpu.make_async_remote_copy(
+            src_ref=source if step == 0 else at(owner),
+            dst_ref=at(owner),
+            send_sem=send_sems.at[side, step],
+            recv_sem=recv_sems.at[side, step],
+            device_id={"tp": place + 1 if side == 0 else place - 1},
+            device_id_type=MESH,
+        )
+
+    def has(side, step):
+        return place - step >= 0 if side == 0 else place + step < count
+
+    def neighbour(side):
+        return place < count - 1 if side == 0 else place > 0
+
+    def send(step):
+        for side in (0, 1):
+
+            @pl.when(neighbour(side) & has(side, step))
+            def _():
+                remote(side, step).start()
+
+    def receive(step):
+        for side in (0, 1):
+
+            @pl.when(has(side, step + 1))
+            def _():
+                remote(side, step).wait_recv()
+
+    def start():
+        neighbour_barrier(count)
+        local().start()
+        send(0)
+
+    def step(k):
+        receive(k - 1)
+        if k < count - 1:
+            send(k)
+
+    def finish():
+        for k in range(count - 1):
+            for side in (0, 1):
+
+                @pl.when(neighbour(side) & has(side, k))
+                def _():
+                    remote(side, k).wait_send()
+
+        local().wait()
+
+    return start, step, finish
+
+
+def line_scratch(count):
+    return [
+        pltpu.SemaphoreType.DMA,
+        pltpu.SemaphoreType.DMA((2, count - 1)),
+        pltpu.SemaphoreType.DMA((2, count - 1)),
+    ]
+
+
+def line_gather_kernel(count, source, target, copies, send_sems, recv_sems):
+    start, step, finish = line_steps(count, source, target, copies, send_sems, recv_sems)
+    start()
+    for k in range(1, count):
+        step(k)
+    finish()
+
+
+def line_gather(source, count, collective):
+    return pl.pallas_call(
+        functools.partial(line_gather_kernel, count),
+        name="line_gather",
+        in_specs=[pl.BlockSpec(memory_space=pl.ANY)],
+        out_specs=pl.BlockSpec(memory_space=pl.ANY),
+        out_shape=jax.ShapeDtypeStruct((source.shape[0], source.shape[1] * count), source.dtype),
+        scratch_shapes=line_scratch(count),
+        compiler_params=pltpu.CompilerParams(collective_id=collective, has_side_effects=True),
+    )(source)
+
+
+def line_sum_steps(count, source, own, sent, got, total, loads, send_sems, recv_sems):
+    place = lax.axis_index("tp")
+    width = total.shape[1]
+
+    def whose(side, step):
+        return place + (count - step) if side == 0 else place - (count - step)
+
+    def sends(side, step):
+        owner = whose(side, step)
+        return owner < count if side == 0 else owner >= 0
+
+    def receives(side, step):
+        return (place >= 1) & (place <= step) if side == 0 else (place <= count - 2) & (place >= count - 1 - step)
+
+    def load(side, step):
+        owner = whose(side, step)
+        return pltpu.make_async_copy(
+            source.at[:, pl.ds(pl.multiple_of(owner * width, width), width)],
+            sent.at[side, step - 1],
+            loads.at[side, step - 1],
+        )
+
+    def mine():
+        return pltpu.make_async_copy(
+            source.at[:, pl.ds(pl.multiple_of(place * width, width), width)], own, loads.at[2, 0]
+        )
+
+    def remote(side, step):
+        return pltpu.make_async_remote_copy(
+            src_ref=sent.at[side, step - 1],
+            dst_ref=got.at[side, step - 1],
+            send_sem=send_sems.at[side, step - 1],
+            recv_sem=recv_sems.at[side, step - 1],
+            device_id={"tp": place + 1 if side == 0 else place - 1},
+            device_id_type=MESH,
+        )
+
+    def start():
+        neighbour_barrier(count)
+        mine().start()
+        for step in range(1, count):
+            for side in (0, 1):
+
+                @pl.when(sends(side, step))
+                def _():
+                    load(side, step).start()
+
+        step_out(1)
+
+    def step_out(step):
+        for side in (0, 1):
+
+            @pl.when(sends(side, step))
+            def _():
+                load(side, step).wait()
+
+            if step > 1:
+
+                @pl.when(sends(side, step) & receives(side, step - 1))
+                def _():
+                    sent[side, step - 1] = (
+                        sent[side, step - 1].astype(f32) + got[side, step - 2].astype(f32)
+                    ).astype(bf16)
+
+            @pl.when(sends(side, step))
+            def _():
+                remote(side, step).start()
+
+    def step(k):
+        for side in (0, 1):
+
+            @pl.when(receives(side, k))
+            def _():
+                remote(side, k).wait_recv()
+
+        if k < count - 1:
+            step_out(k + 1)
+
+    def finish():
+        mine().wait()
+        total[...] = own[...].astype(f32)
+        for side in (0, 1):
+
+            @pl.when(receives(side, count - 1))
+            def _():
+                total[...] = total[...] + got[side, count - 2].astype(f32)
+
+            for k in range(1, count):
+
+                @pl.when(sends(side, k))
+                def _():
+                    remote(side, k).wait_send()
+
+    return start, step, finish
+
+
+def line_sum_scratch(count, height, width):
+    return [
+        pltpu.VMEM((height, width), bf16),
+        pltpu.VMEM((2, count - 1, height, width), bf16),
+        pltpu.VMEM((2, count - 1, height, width), bf16),
+        pltpu.SemaphoreType.DMA((3, count - 1)),
+        pltpu.SemaphoreType.DMA((2, count - 1)),
+        pltpu.SemaphoreType.DMA((2, count - 1)),
+    ]
+
+
+def line_sum_kernel(count, source, total, own, sent, got, loads, send_sems, recv_sems):
+    start, step, finish = line_sum_steps(
+        count, source, own, sent, got, total, loads, send_sems, recv_sems
+    )
+    start()
+    for k in range(1, count):
+        step(k)
+    finish()
+
+
+def line_sum(source, count, collective):
+    height, width = source.shape[0], source.shape[1] // count
+    return pl.pallas_call(
+        functools.partial(line_sum_kernel, count),
+        name="line_sum",
+        in_specs=[pl.BlockSpec(memory_space=pl.ANY)],
+        out_specs=pl.BlockSpec(memory_space=pltpu.VMEM),
+        out_shape=jax.ShapeDtypeStruct((height, width), f32),
+        scratch_shapes=line_sum_scratch(count, height, width),
+        compiler_params=pltpu.CompilerParams(
+            vmem_limit_bytes=24 << 20, collective_id=collective, has_side_effects=True
+        ),
+    )(source)
+
+
+def attend_kernel(
+    group,
+    count,
+    query_t,
+    key_t,
+    value_t,
+    bias,
+    source,
+    out_t,
+    log_total,
+    total_out,
+    own,
+    sent,
+    got,
+    loads,
+    send_sems,
+    recv_sems,
+):
+    head, heads = pl.program_id(0), pl.num_programs(0)
+    start, step, finish = line_sum_steps(
+        count, source, own, sent, got, total_out, loads, send_sems, recv_sems
+    )
+
+    @pl.when(head == 0)
+    def _():
+        start()
+
+    @pl.when(head == heads - 2)
+    def _():
+        step(1)
+
     keys = key_t[...].T
     values_t = value_t[...]
     for g in range(group):
@@ -352,8 +664,43 @@
         out_t[at, :] = (mm(values_t, probs.astype(bf16)) / total).astype(bf16)
         log_total[g : g + 1, :] = top + jnp.log(total)
 
-
-def attend_back_kernel(group, query_t, key_t, value_t, bias, out_t, log_total, grad_t, query_grad_t, key_grad_t, value_grad_t):
+    @pl.when(head == heads - 1)
+    def _():
+        for k in range(2, count):
+            step(k)
+        finish()
+
+
+def attend_back_kernel(
+    group,
+    count,
+    query_t,
+    key_t,
+    value_t,
+    bias,
+    out_t,
+    log_total,
+    grad_t,
+    source,
+    query_grad_t,
+    key_grad_t,
+    value_grad_t,
+    target,
+    copies,
+    send_sems,
+    recv_sems,
+):
+    head, heads = pl.program_id(0), pl.num_programs(0)
+    start, step, finish = line_steps(count, source, target, copies, send_sems, recv_sems)
+
+    @pl.when(head == 0)
+    def _():
+        start()
+
+    @pl.when(head == heads - 2)
+    def _():
+        step(1)
+
     keys_t = key_t[...]
     keys = keys_t.T
     values = value_t[...].T
@@ -372,61 +719,98 @@
     key_grad_t[...] = key_sum
     value_grad_t[...] = value_sum
 
-
-def attend(query_t, keyval_t, bias, key_value_heads):
+    @pl.when(head == heads - 1)
+    def _():
+        for k in range(2, count):
+            step(k)
+        finish()
+
+
+def attend(query_t, keyval_t, bias, source, key_value_heads, count, collective):
     width, rows = query_t.shape
     keys = keyval_t.shape[1]
     group = width // HEAD_SIZE // key_value_heads
     kv = key_value_heads
+    height, each = source.shape[0], source.shape[1] // count
     return pl.pallas_call(
-        functools.partial(attend_kernel, group), grid=(kv,),
+        functools.partial(attend_kernel, group, count),
+        name="attend",
+        grid=(kv,),
         in_specs=[
             pl.BlockSpec((group * HEAD_SIZE, rows), lambda h: (h, 0)),
             pl.BlockSpec((HEAD_SIZE, keys), lambda h: (h, 0)),
             pl.BlockSpec((HEAD_SIZE, keys), lambda h: (h + kv, 0)),
             pl.BlockSpec((keys, rows), lambda h: (0, 0)),
+            pl.BlockSpec(memory_space=pl.ANY),
         ],
         out_specs=[
             pl.BlockSpec((group * HEAD_SIZE, rows), lambda h: (h, 0)),
             pl.BlockSpec((None, 8, rows), lambda h: (h, 0, 0)),
-        ],
-        out_shape=[jax.ShapeDtypeStruct((width, rows), bf16), jax.ShapeDtypeStruct((kv, 8, rows), f32)],
-        compiler_params=PARAMS_A,
-    )(query_t, keyval_t, keyval_t, bias)
-
-
-def attend_back(query_t, keyval_t, bias, out_t, log_total, grad_t, key_value_heads):
+            pl.BlockSpec((height, each), lambda h: (0, 0)),
+        ],
+        out_shape=[
+            jax.ShapeDtypeStruct((width, rows), bf16),
+            jax.ShapeDtypeStruct((kv, 8, rows), f32),
+            jax.ShapeDtypeStruct((height, each), f32),
+        ],
+        scratch_shapes=line_sum_scratch(count, height, each),
+        compiler_params=pltpu.CompilerParams(
+            vmem_limit_bytes=56 << 20,
+            dimension_semantics=("arbitrary",),
+            collective_id=collective,
+            has_side_effects=True,
+        ),
+    )(query_t, keyval_t, keyval_t, bias, source)
+
+
+def attend_back(query_t, keyval_t, bias, out_t, log_total, grad_t, source, key_value_heads, count, collective):
     width, rows = query_t.shape
     keys = keyval_t.shape[1]
     group = width // HEAD_SIZE // key_value_heads
     kv = key_value_heads
     wide = pl.BlockSpec((group * HEAD_SIZE, rows), lambda h: (h, 0))
     head = pl.BlockSpec((HEAD_SIZE, keys), lambda h: (h, 0))
+    anywhere = pl.BlockSpec(memory_space=pl.ANY)
     return pl.pallas_call(
-        functools.partial(attend_back_kernel, group), grid=(kv,),
+        functools.partial(attend_back_kernel, group, count),
+        name="attend_back",
+        grid=(kv,),
         in_specs=[
-            wide, head,
+            wide,
+            head,
             pl.BlockSpec((HEAD_SIZE, keys), lambda h: (h + kv, 0)),
             pl.BlockSpec((keys, rows), lambda h: (0, 0)),
             wide,
             pl.BlockSpec((None, 8, rows), lambda h: (h, 0, 0)),
             wide,
-        ],
-        out_specs=[wide, head, head],
-        out_shape=[jax.ShapeDtypeStruct((width, rows), bf16), jax.ShapeDtypeStruct((kv * HEAD_SIZE, keys), f32), jax.ShapeDtypeStruct((kv * HEAD_SIZE, keys), f32)],
-        compiler_params=PARAMS_A,
-    )(query_t, keyval_t, keyval_t, bias, out_t, log_total, grad_t)
+            anywhere,
+        ],
+        out_specs=[wide, head, head, anywhere],
+        out_shape=[
+            jax.ShapeDtypeStruct((width, rows), bf16),
+            jax.ShapeDtypeStruct((kv * HEAD_SIZE, keys), f32),
+            jax.ShapeDtypeStruct((kv * HEAD_SIZE, keys), f32),
+            jax.ShapeDtypeStruct((source.shape[0], source.shape[1] * count), source.dtype),
+        ],
+        scratch_shapes=line_scratch(count),
+        compiler_params=pltpu.CompilerParams(
+            vmem_limit_bytes=56 << 20,
+            dimension_semantics=("arbitrary",),
+            collective_id=collective,
+            has_side_effects=True,
+        ),
+    )(query_t, keyval_t, keyval_t, bias, out_t, log_total, grad_t, source)
 
 
 def rms_norm(values, gain):
-    return values * lax.rsqrt(jnp.mean(values * values, axis=-1, keepdims=True) + epsilon) * gain
+    return values * lax.rsqrt(jnp.mean(values * values, axis=0, keepdims=True) + epsilon) * gain
 
 
 def rms_back(values, gain, grad):
-    scale = lax.rsqrt(jnp.mean(values * values, axis=-1, keepdims=True) + epsilon)
+    scale = lax.rsqrt(jnp.mean(values * values, axis=0, keepdims=True) + epsilon)
     normal = values * scale
     weighted = grad * gain
-    back = scale * (weighted - normal * jnp.mean(weighted * normal, axis=-1, keepdims=True))
+    back = scale * (weighted - normal * jnp.mean(weighted * normal, axis=0, keepdims=True))
     return back, grad * normal
 
 
@@ -436,13 +820,51 @@
     )
 
 
-def gather_rows(pieces):
-    return lax.all_gather(jnp.concatenate(pieces, axis=1), ("fsdp", "ctx"), axis=0, tiled=True)
-
-
-def scatter_rows(pieces):
-    whole = jnp.concatenate([piece.astype(bf16) for piece in pieces], axis=1)
+def gather_rows(whole):
+    return lax.all_gather(whole, ("fsdp", "ctx"), axis=0, tiled=True)
+
+
+def scatter_rows(whole):
     return lax.psum_scatter(whole, ("fsdp", "ctx"), scatter_dimension=0, tiled=True)
+
+
+def send(values, by):
+    count = lax.axis_size("tp")
+    return lax.ppermute(values, "tp", [(i, (i + by) % count) for i in range(count)])
+
+
+def permute_gather(own):
+    count = lax.axis_size("tp")
+    return [own] + [send(own, k) for k in range(1, count)]
+
+
+def in_order(pieces):
+    count, place = lax.axis_size("tp"), lax.axis_index("tp")
+    return jnp.concatenate(
+        [lax.select_n(lax.rem(place - p + count, count), *pieces) for p in range(count)], axis=1
+    )
+
+
+def permute_sums(values, axis):
+    count, place = lax.axis_size("tp"), lax.axis_index("tp")
+    each = values.shape[axis] // count
+    shares = [
+        lax.dynamic_slice_in_dim(values, lax.rem(place + k, count) * each, each, axis)
+        for k in range(count)
+    ]
+    total = shares[0].astype(f32)
+    for k in (2, 1, 3):
+        total = total + send(shares[k], k).astype(f32)
+    return total
+
+
+def permute_exchange(values):
+    count, place = lax.axis_size("tp"), lax.axis_index("tp")
+    shares = values.reshape(count, values.shape[0] // count, values.shape[1])
+    pieces = [
+        lax.dynamic_index_in_dim(shares, lax.rem(place + k, count), 0, False) for k in range(count)
+    ]
+    return [pieces[0]] + [send(pieces[k], k) for k in range(1, count)]
 
 
 def cut(values, widths):
@@ -475,8 +897,8 @@
     ffn_input,
     ffn_output,
 ):
-    tokens, segments, cotangent = tokens[0], segments[0], cotangent[0]
-    rows, width = tokens.shape
+    tokens_t, segments, cotangent_t = tokens[0].T, segments[0], cotangent[0].T
+    width, rows = tokens_t.shape
     shard = meta_tokens.shape[0]
     tp = lax.axis_size("tp")
     tp_index = lax.axis_index("tp")
@@ -487,41 +909,82 @@
     heads = keyval_width // (2 * HEAD_SIZE)
     channels = mamba_input.shape[2]
     ff = ffn_input.shape[2] // tp
+    ff_wide = -(-ff // 128) * 128
     meta_count = meta_tokens.shape[1]
     window = WIN + rows
 
     gains = jnp.stack([gain_mix, gain_attn, gain_mamba, gain_ffn], axis=1)
     flat_input = mamba_input.reshape(shard, 3 * channels)
-    first = gather_rows([key_value_weight, meta_tokens, query_weight, flat_input, mamba_select, gains])
-    second = gather_rows([mamba_output, attn_output])
-    ffn_up_shard = lax.dynamic_slice_in_dim(ffn_input, tp_index * ff, ff, 2).reshape(shard, 2 * ff)
-    ffn_down_shard = lax.dynamic_slice_in_dim(ffn_output, tp_index * ff, ff, 1)
-    third = gather_rows([ffn_up_shard, ffn_down_shard])
-    tokens_group = lax.all_gather(tokens, "tp", axis=0, tiled=True)
-    cotangent_group = lax.all_gather(cotangent, "tp", axis=0, tiled=True)
-
-    keyval_map, meta_full, query_map, state_map, select_map, gain_columns = cut(
-        first, [keyval_width, meta_count, query_width, 3 * channels, 2 * STATE, 4]
-    )
-    state_out_map, attn_map = cut(second, [channels, query_width])
-    up_map, down_map = cut(third, [2 * ff, ff])
-    gain_rows = gain_columns.astype(f32).T
-    mix_gain, attn_gain, mamba_gain, ffn_gain = [gain_rows[k : k + 1] for k in range(4)]
-
-    residual = tokens.astype(f32)
-    residual_group = tokens_group.astype(f32)
-    normed = rms_norm(residual, mix_gain).astype(bf16)
-    normed_group = rms_norm(residual_group, mix_gain).astype(bf16)
-    meta_rows = meta_full.astype(f32).T
-    meta_normed = rms_norm(meta_rows, mix_gain).astype(bf16)
-
-    query_t = dot(query_map, normed, 0, 1).astype(bf16)
-    keyval_group_t = dot(keyval_map, normed_group, 0, 1).astype(bf16)
-    meta_keyval_t = dot(keyval_map, meta_normed, 0, 1).astype(bf16)
-    selects = dot(normed_group, select_map, 1, 0).astype(bf16)
-    selects_t = selects.T
+    small = jnp.concatenate(
+        [mamba_select, gains, jnp.zeros((shard, 128 - 2 * STATE - 4), bf16)], axis=1
+    )
+    first = jnp.concatenate([small, flat_input], axis=1)
+    first, second_parts = lax.optimization_barrier(
+        (first, (key_value_weight, meta_tokens, query_weight))
+    )
+    second = jnp.concatenate(second_parts, axis=1)
+    first, second, tokens_t = lax.optimization_barrier((first, second, tokens_t))
+    first = gather_rows(first)
+    second = gather_rows(second)
+    tokens_group_t = line_gather(tokens_t, tp, 0)
+    late_cotangent_t, tokens_group_t = lax.optimization_barrier((cotangent_t, tokens_group_t))
+    cotangent_pieces = permute_gather(late_cotangent_t)
+
+    select_map, gain_columns, _, state_map = cut(
+        first, [2 * STATE, 4, 128 - 2 * STATE - 4, 3 * channels]
+    )
+    keyval_map, meta_full, query_map = cut(second, [keyval_width, meta_count, query_width])
+    state_out_map = gather_rows(mamba_output)
+    attn_map = gather_rows(attn_output)
+    gain_columns = gain_columns.astype(f32)
+    mix_gain, attn_gain, mamba_gain, ffn_gain = [gain_columns[:, k : k + 1] for k in range(4)]
+
+    residual = tokens_t.astype(f32)
+    residual_group = tokens_group_t.astype(f32)
+    normed_t = rms_norm(residual, mix_gain).astype(bf16)
+    normed_group_t = rms_norm(residual_group, mix_gain).astype(bf16)
+    meta_rows = meta_full.astype(f32)
+    meta_normed_t = rms_norm(meta_rows, mix_gain).astype(bf16)
+
+    mixed = dot(normed_group_t, state_map, 0, 0)
+    selects_t = dot(select_map, normed_group_t, 0, 0).astype(bf16)
+    selects = selects_t.T
+    seg_current = lax.dynamic_slice_in_dim(segments, ctx_index * span, span, 0)
+    seg_earlier = lax.dynamic_slice_in_dim(segments, jnp.maximum(ctx_index - 1, 0) * span, span, 0)
+    seg_before = jnp.where(
+        ctx_index > 0,
+        lax.dynamic_index_in_dim(segments, jnp.maximum(ctx_index * span - 1, 0), 0, False),
+        -1,
+    )
+    aux = scan_aux(seg_current, seg_before)
+    bias_row = step_bias[None]
+    rate_row = jnp.exp(decay_log)[None]
+    skip_row = state_skip[None]
+    selects_t, late_up, late_down = lax.optimization_barrier((selects_t, ffn_input, ffn_output))
+    ffn_shards = [
+        lax.dynamic_slice_in_dim(whole, tp_index * ff, ff, 1)
+        for whole in (late_up[:, 0], late_up[:, 1], late_down)
+    ]
+    state_end = end_state(mixed, selects_t, aux, bias_row, rate_row)
+    state_start = lax.ppermute(state_end, "ctx", [(0, 1)])
+
+    query_t = dot(query_map, normed_t, 0, 0).astype(bf16)
+    keyval_group_t = dot(keyval_map, normed_group_t, 0, 0).astype(bf16)
+    meta_keyval_t = dot(keyval_map, meta_normed_t, 0, 0).astype(bf16)
     earlier_t = lax.ppermute(keyval_group_t, "ctx", [(0, 1)])
-    mixed = dot(normed_group, state_map, 1, 0)
+
+    gated, states, state_final = forward_scan(
+        mixed, selects, selects_t, aux, bias_row, rate_row, skip_row, state_start
+    )
+    mamba_part_t = dot(state_out_map, gated, 1, 1).astype(bf16)
+    third = jnp.concatenate(
+        [jnp.pad(piece, ((0, 0), (0, ff_wide - ff))) for piece in ffn_shards], axis=1
+    )
+    mamba_part_t, third, *cotangent_pieces = lax.optimization_barrier(
+        (mamba_part_t, third, *cotangent_pieces)
+    )
+    third = gather_rows(third)
+    up_map, down_map = cut(third, [2 * ff_wide, ff_wide])
 
     key_start = span + tp_index * rows - WIN
     keyval_t = jnp.concatenate(
@@ -535,8 +998,6 @@
     )
     query_pos = ctx_index * span + tp_index * rows + jnp.arange(rows, dtype=jnp.int32)
     key_pos = (ctx_index - 1) * span + key_start + jnp.arange(window, dtype=jnp.int32)
-    seg_current = lax.dynamic_slice_in_dim(segments, ctx_index * span, span, 0)
-    seg_earlier = lax.dynamic_slice_in_dim(segments, jnp.maximum(ctx_index - 1, 0) * span, span, 0)
     seg_query = lax.dynamic_slice_in_dim(seg_current, tp_index * rows, rows, 0)
     seg_keys = lax.dynamic_slice_in_dim(
         jnp.concatenate([seg_earlier, seg_current]), key_start, window, 0
@@ -550,69 +1011,82 @@
     bias = jnp.concatenate(
         [jnp.zeros((meta_count, rows), f32), jnp.where(keep, 0.0, masked_score)], axis=0
     )
-    attended_t, log_total = attend(query_t, keyval_t, bias, heads)
-    attended_columns = lax.all_to_all(
-        attended_t.reshape(tp, query_width // tp, rows), "tp", 0, 0
-    )
-
-    seg_before = jnp.where(
-        ctx_index > 0,
-        lax.dynamic_index_in_dim(segments, jnp.maximum(ctx_index * span - 1, 0), 0, False),
-        -1,
-    )
-    aux = scan_aux(seg_current, seg_before)
-    bias_row = step_bias[None]
-    rate_row = jnp.exp(decay_log)[None]
-    skip_row = state_skip[None]
-    state_end = end_state(mixed, selects_t, aux, bias_row, rate_row)
-    state_start = lax.ppermute(state_end, "ctx", [(0, 1)])
-    gated, states, state_final = forward_scan(
-        mixed, selects, selects_t, aux, bias_row, rate_row, skip_row, state_start
-    )
-    mamba_part = dot(gated, state_out_map, 1, 1).astype(bf16)
-    mamba_out = lax.psum_scatter(mamba_part, "tp", scatter_dimension=0, tiled=True).astype(f32)
-    attn_out = dot(attended_t, attn_map, 0, 1)
+    cotangent_group_t = in_order(cotangent_pieces)
+    attended_t, log_total, mamba_out = attend(
+        query_t, keyval_t, bias, mamba_part_t, heads, tp, 3
+    )
+    attn_out = dot(attn_map, attended_t, 1, 0)
+
     mid = residual + 0.5 * (rms_norm(attn_out, attn_gain) + rms_norm(mamba_out, mamba_gain))
-    ffn_normed = rms_norm(mid, ffn_gain).astype(bf16)
-    ffn_normed_group = lax.all_gather(ffn_normed, "tp", axis=0, tiled=True)
-
-    gate_up = dot(ffn_normed_group, up_map, 1, 0)
-    gate, up = gate_up[:, :ff], gate_up[:, ff:]
+    ffn_normed_t = rms_norm(mid, ffn_gain).astype(bf16)
+    ffn_normed_group_t = line_gather(ffn_normed_t, tp, 1)
+
+    gate_up = dot(up_map, ffn_normed_group_t, 0, 0)
+    gate, up = gate_up[:ff_wide], gate_up[ff_wide:]
     sigma = jax.nn.sigmoid(gate)
-    hidden = (gate * sigma * up).astype(bf16)
-    hidden_grad = dot(cotangent_group, down_map, 1, 0)
-    gate_up_grad = jnp.concatenate(
+    hidden_t = (gate * sigma * up).astype(bf16)
+    hidden_grad = dot(down_map, cotangent_group_t, 0, 0)
+    gate_up_grad_t = jnp.concatenate(
         [
             (hidden_grad * up * (sigma * (1.0 + gate * (1.0 - sigma)))).astype(bf16),
             (hidden_grad * gate * sigma).astype(bf16),
         ],
-        axis=1,
-    )
-    ffn_grad_part = dot(gate_up_grad, up_map, 1, 1).astype(bf16)
-    ffn_normed_grad = lax.psum_scatter(
-        ffn_grad_part, "tp", scatter_dimension=0, tiled=True
-    ).astype(f32)
-    out_part = dot(hidden, down_map, 1, 1).astype(bf16)
-    layer_out = (
-        mid + lax.psum_scatter(out_part, "tp", scatter_dimension=0, tiled=True).astype(f32)
-    ).astype(bf16)
-
+        axis=0,
+    )
+    late_attended_t, gate_up_grad_t = lax.optimization_barrier((attended_t, gate_up_grad_t))
+    attended_columns_t = jnp.concatenate(permute_exchange(late_attended_t), axis=1)
+    ffn_grad_part_t = dot(up_map, gate_up_grad_t, 1, 0).astype(bf16)
+    ffn_grad_part_t, attended_columns_t = lax.optimization_barrier(
+        (ffn_grad_part_t, attended_columns_t)
+    )
+    ffn_normed_grad_t = lax.psum_scatter(ffn_grad_part_t, "tp", scatter_dimension=1, tiled=True)
+    up_wide = dot(ffn_normed_group_t, gate_up_grad_t, 1, 1).astype(bf16)
+    down_wide = dot(cotangent_group_t, hidden_t, 1, 1).astype(bf16)
+    ffn_wide = jnp.concatenate([up_wide, down_wide], axis=1)
+    out_part_t = dot(down_map, hidden_t, 1, 0).astype(bf16)
+    ffn_normed_grad_t, ffn_wide, out_part_t = lax.optimization_barrier(
+        (ffn_normed_grad_t, ffn_wide, out_part_t)
+    )
+    ffn_columns = scatter_rows(ffn_wide)
+
+    ffn_normed_grad = ffn_normed_grad_t.astype(f32)
     mid_extra, ffn_gain_terms = rms_back(mid, ffn_gain, ffn_normed_grad)
-    mid_grad = cotangent.astype(f32) + mid_extra
+    mid_grad = cotangent_t.astype(f32) + mid_extra
     attn_grad, attn_gain_terms = rms_back(attn_out, attn_gain, 0.5 * mid_grad)
     mamba_grad, mamba_gain_terms = rms_back(mamba_out, mamba_gain, 0.5 * mid_grad)
-    attn_grad = attn_grad.astype(bf16)
-    mamba_grad = mamba_grad.astype(bf16)
-    mamba_grad_group = lax.all_gather(mamba_grad, "tp", axis=0, tiled=True)
-    attn_grad_group = lax.all_gather(attn_grad, "tp", axis=0, tiled=True)
-
-    attended_grad_t = dot(attn_map, attn_grad, 0, 1).astype(bf16)
-    query_grad_t, key_grad_t, value_grad_t = attend_back(
-        query_t, keyval_t, bias, attended_t, log_total, attended_grad_t, heads
-    )
-    gated_grad = dot(mamba_grad_group, state_out_map, 1, 0)
+    attn_grad_t = attn_grad.astype(bf16)
+    mamba_grad_t = mamba_grad.astype(bf16)
+    attended_grad_t = dot(attn_map, attn_grad_t, 0, 0).astype(bf16)
+    query_grad_t, key_grad_t, value_grad_t, mamba_grad_group_t = attend_back(
+        query_t,
+        keyval_t,
+        bias,
+        attended_t,
+        log_total,
+        attended_grad_t,
+        mamba_grad_t,
+        heads,
+        tp,
+        2,
+    )
+    keyval_grad_t = jnp.concatenate([key_grad_t, value_grad_t], axis=0).astype(bf16)
+    placed = lax.dynamic_update_slice_in_dim(
+        jnp.zeros((keyval_width, 2 * span), bf16), keyval_grad_t[:, meta_count:], key_start, 1
+    )
+    earlier_back = lax.ppermute(placed[:, :span], "ctx", [(1, 0)])
+    current = placed[:, span:].astype(f32) + earlier_back.astype(f32)
+    with_meta = jnp.concatenate([keyval_grad_t[:, :meta_count], current.astype(bf16)], axis=1)
+    keyval_columns_t = permute_sums(with_meta, 0).astype(bf16)
+    out_wide = dot(mamba_grad_group_t, gated, 1, 0).astype(bf16)
+    out_columns = scatter_rows(out_wide)
+    query_pieces = permute_exchange(query_grad_t)
+    late_attn_grad_t, query_grad_t = lax.optimization_barrier((attn_grad_t, query_grad_t))
+    attn_grad_pieces = permute_gather(late_attn_grad_t)
+
+    gated_grad = dot(mamba_grad_group_t, state_out_map, 0, 0)
     adjoint_end = end_adjoint(gated_grad, mixed, selects_t, aux, bias_row, rate_row)
     adjoint_start = lax.ppermute(adjoint_end, "ctx", [(1, 0)])
+    adjoint_start, ffn_columns = lax.optimization_barrier((adjoint_start, ffn_columns))
     mix_grad, select_grad, scan_sums = backward_scan(
         gated_grad,
         mixed,
@@ -626,113 +1100,129 @@
         adjoint_start,
         state_final,
     )
-
-    keyval_grad_t = jnp.concatenate([key_grad_t, value_grad_t], axis=0).astype(bf16)
-    placed = lax.dynamic_update_slice_in_dim(
-        jnp.zeros((keyval_width, 2 * span), bf16), keyval_grad_t[:, meta_count:], key_start, 1
-    )
-    earlier_back = lax.ppermute(placed[:, :span], "ctx", [(1, 0)])
-    current = placed[:, span:].astype(f32) + earlier_back.astype(f32)
-    with_meta = jnp.concatenate([keyval_grad_t[:, :meta_count], current.astype(bf16)], axis=1)
-    select_rows = jnp.concatenate(
-        [jnp.zeros((2 * STATE, meta_count), bf16), select_grad.T.astype(bf16)], axis=1
-    )
-    columns = jnp.concatenate(
-        [
-            with_meta.reshape(tp, keyval_width // tp, meta_count + span),
-            select_rows.reshape(tp, 2 * STATE // tp, meta_count + span),
-        ],
-        axis=1,
-    )
-    columns = lax.psum_scatter(columns, "tp", scatter_dimension=0, tiled=True)[0]
-    keyval_columns_t = columns[: keyval_width // tp]
-    select_columns_t = columns[keyval_width // tp :, meta_count:]
-    query_columns = lax.all_to_all(
-        query_grad_t.reshape(tp, query_width // tp, rows), "tp", 0, 0
-    )
-
+    state_wide = dot(normed_group_t, mix_grad, 1, 0).astype(bf16)
+    state_wide, out_columns = lax.optimization_barrier((state_wide, out_columns))
+    state_columns = scatter_rows(state_wide)
+    (
+        state_wide,
+        mix_grad,
+        keyval_columns_t,
+        out_part_t,
+        query_pieces,
+        attn_grad_pieces,
+    ) = lax.optimization_barrier(
+        (state_wide, mix_grad, keyval_columns_t, out_part_t, query_pieces, attn_grad_pieces)
+    )
+    query_columns_t = in_order(query_pieces)
+    attn_grad_group_t = jnp.concatenate(attn_grad_pieces, axis=1)
+    select_grad_t = select_grad.T.astype(bf16)
     keyval_part = lax.dynamic_slice_in_dim(
         keyval_map, tp_index * (keyval_width // tp), keyval_width // tp, 1
     )
-    query_term = dot(query_grad_t, query_map, 0, 1)
+    query_term = dot(query_map, query_grad_t, 1, 0)
     normed_grad_part = (
-        dot(mix_grad, state_map, 1, 1)
-        + dot(select_grad.astype(bf16), select_map, 1, 1)
-        + dot(keyval_columns_t[:, meta_count:], keyval_part, 0, 1)
-    )
-    meta_grad_part = dot(keyval_columns_t[:, :meta_count], keyval_part, 0, 1)
+        dot(state_map, mix_grad, 1, 1)
+        + dot(select_map, select_grad_t, 1, 0)
+        + dot(keyval_part, keyval_columns_t[:, meta_count:], 1, 0)
+    )
+    meta_grad_part = dot(keyval_part, keyval_columns_t[:, :meta_count], 1, 0)
     _, group_terms = rms_back(residual_group, mix_gain, normed_grad_part)
-    _, meta_terms = rms_back(meta_rows, mix_gain, meta_grad_part)
+    meta_back, meta_terms = rms_back(meta_rows, mix_gain, meta_grad_part)
     _, query_terms = rms_back(residual, mix_gain, query_term)
-    mix_gain_sum = jnp.sum(group_terms, 0) + jnp.sum(meta_terms, 0) + jnp.sum(query_terms, 0)
     gain_sums = jnp.stack(
         [
-            mix_gain_sum,
-            jnp.sum(attn_gain_terms, 0),
-            jnp.sum(mamba_gain_terms, 0),
-            jnp.sum(ffn_gain_terms, 0),
-        ]
-    ).astype(bf16)
-    gain_block = jnp.concatenate([gain_sums, jnp.zeros((4, width), bf16)])
-    extended = jnp.concatenate(
-        [
-            normed_grad_part.astype(bf16).reshape(tp, rows, width),
-            meta_grad_part.astype(bf16).reshape(tp, meta_count // tp, width),
-            jnp.broadcast_to(gain_block[None], (tp, 8, width)),
+            jnp.sum(group_terms, 1) + jnp.sum(meta_terms, 1) + jnp.sum(query_terms, 1),
+            jnp.sum(attn_gain_terms, 1),
+            jnp.sum(mamba_gain_terms, 1),
+            jnp.sum(ffn_gain_terms, 1),
         ],
         axis=1,
     )
-    extended = lax.psum_scatter(extended, "tp", scatter_dimension=0, tiled=True)[0].astype(f32)
-    normed_grad = extended[:rows] + query_term
-    residual_extra, _ = rms_back(residual, mix_gain, normed_grad)
-    grad_tokens = (mid_grad + residual_extra).astype(bf16)
-    own_meta_rows = lax.dynamic_slice_in_dim(
-        meta_rows, tp_index * (meta_count // tp), meta_count // tp, 0
-    )
-    own_meta_grad, _ = rms_back(own_meta_rows, mix_gain, extended[rows : rows + meta_count // tp])
-    gain_totals = extended[rows + meta_count // tp :][:4]
-
-    ffn_columns = scatter_rows(
-        [dot(ffn_normed_group, gate_up_grad, 0, 0), dot(cotangent_group, hidden, 0, 0)]
-    ).astype(f32)
-    attended_wide = jnp.swapaxes(attended_columns, 1, 2).reshape(span, query_width // tp)
-    query_wide = jnp.swapaxes(query_columns, 1, 2).reshape(span, query_width // tp)
-    out_columns = scatter_rows(
-        [dot(mamba_grad_group, gated, 0, 0), dot(attn_grad_group, attended_wide, 0, 0)]
-    ).astype(f32)
     vector_columns = -(-3 * channels // shard)
     vectors = jnp.pad(scan_sums[:3].reshape(-1), (0, vector_columns * shard - 3 * channels))
     vectors = jnp.tile(vectors.reshape(shard, vector_columns), (width // shard, 1))
-    last_columns = scatter_rows(
+    each = query_width // tp
+    each_wide = -(-each // 128) * 128
+    room = ((0, each_wide - each), (0, 0))
+    small = [
+        meta_back,
+        dot(normed_group_t, keyval_columns_t[:, meta_count:], 1, 1)
+        + dot(meta_normed_t, keyval_columns_t[:, :meta_count], 1, 1),
+        dot(normed_group_t, select_grad_t, 1, 1),
+        gain_sums,
+        vectors,
+    ]
+    last_wide = jnp.concatenate(
         [
-            dot(normed_group, mix_grad, 0, 0),
-            dot(normed_group, query_wide, 0, 0),
-            dot(normed_group, keyval_columns_t[:, meta_count:], 0, 1)
-            + dot(meta_normed, keyval_columns_t[:, :meta_count], 0, 1),
-            dot(normed_group, select_columns_t, 0, 1),
-            own_meta_grad.T,
-            gain_totals.T,
-            vectors,
-        ]
-    ).astype(f32)
-    grad_ffn_input, grad_ffn_output = cut(ffn_columns, [2 * ff, ff])
-    grad_mamba_output, grad_attn_output = cut(out_columns, [channels, query_width // tp])
-    grad_mamba_input, grad_query, grad_keyval, grad_select, grad_meta, grad_gains, grad_vectors = cut(
+            dot(attn_grad_group_t, jnp.pad(attended_columns_t, room), 1, 1).astype(bf16),
+            dot(normed_group_t, jnp.pad(query_columns_t, room), 1, 1).astype(bf16),
+            jnp.concatenate([piece.astype(bf16) for piece in small], axis=1),
+        ],
+        axis=1,
+    )
+    last_wide, normed_grad_low = lax.optimization_barrier(
+        (last_wide, normed_grad_part.astype(bf16))
+    )
+    last_wide, state_columns = lax.optimization_barrier((last_wide, state_columns))
+    last_columns = scatter_rows(last_wide)
+    normed_grad = line_sum(normed_grad_low, tp, 4) + query_term
+    late_out_part_t, normed_grad = lax.optimization_barrier((out_part_t, normed_grad))
+    layer_out_t = (mid + line_sum(late_out_part_t, tp, 5)).astype(bf16)
+    residual_extra, _ = rms_back(residual, mix_gain, normed_grad)
+    grad_tokens_t = (mid_grad + residual_extra).astype(bf16)
+    grad_gate, grad_up, grad_ffn_output = [
+        piece[:, :ff].astype(f32) for piece in cut(ffn_columns, [ff_wide] * 3)
+    ]
+    grad_ffn_input = jnp.stack([grad_gate, grad_up], axis=1)
+    grad_mamba_input = state_columns.astype(f32)
+    grad_mamba_output = out_columns.astype(f32)
+    (
+        grad_attn_output,
+        _,
+        grad_query,
+        _,
+        meta_shares,
+        grad_keyval,
+        select_shares,
+        gain_shares,
+        grad_vectors,
+    ) = cut(
         last_columns,
         [
-            3 * channels,
-            query_width // tp,
+            each,
+            each_wide - each,
+            each,
+            each_wide - each,
+            meta_count,
             keyval_width // tp,
-            2 * STATE // tp,
-            meta_count // tp,
+            2 * STATE,
             4,
             vector_columns,
         ],
     )
+    grad_attn_output, grad_query, grad_keyval, grad_vectors = [
+        v.astype(f32) for v in (grad_attn_output, grad_query, grad_keyval, grad_vectors)
+    ]
+    meta_each, select_each = meta_count // tp, 2 * STATE // tp
+
+    def to_device(values):
+        return jnp.swapaxes(values.reshape(shard, tp, values.shape[1] // tp), 0, 1)
+
+    shares = jnp.concatenate(
+        [
+            to_device(meta_shares),
+            to_device(select_shares),
+            jnp.broadcast_to(gain_shares[None], (tp, shard, 4)),
+        ],
+        axis=2,
+    )
+    grad_meta, grad_select, grad_gains = cut(
+        permute_sums(shares, 0)[0], [meta_each, select_each, 4]
+    )
     grad_vectors = grad_vectors.reshape(-1)[: 3 * channels].reshape(3, channels)
     return (
-        layer_out[None],
-        grad_tokens[None],
+        layer_out_t.T[None],
+        grad_tokens_t.T[None],
         grad_meta,
         grad_gains[:, 0],
         grad_query,
@@ -747,7 +1237,7 @@
         grad_mamba_output,
         grad_gains[:, 2],
         grad_gains[:, 3],
-        grad_ffn_input.reshape(shard, 2, ff),
+        grad_ffn_input,
         grad_ffn_output,
     )
 

time: 1320 us -> 930 us (0.70)
  waiting for transfers between devices: 741 us -> 99.1 us
  Pallas kernels: 137 us -> 431 us
  starting transfers between devices: 12.8 us -> 63 us
  local copies, waits for them, and re-layouts: 103 us -> 65.2 us
  blocking collectives: 36 us -> 0 us
  matrix products: 204 us -> 187 us
    all_gather x8 -> x5, waiting for transfers between devices: 346 us -> 6.12 us  [gather_rows(): return lax.all_gather(whole, ('fsdp', 'ctx'), axis=0, tiled=True)]
    pallas_call x6 -> x10, Pallas kernels: 137 us -> 431 us  [the longest x2 114 us: line_gather(): pl.pallas_call(functools.partial(line_gather_kernel, count), name='line_g...]
    unnamed x19 -> x11, waiting for transfers between devices: 164 us -> 1.51 us
    reduce_scatter x5 -> x1, waiting for transfers between devices: 182 us -> 24.8 us  [per_device(): lax.psum_scatter(ffn_grad_part_t, 'tp', scatter_dimension=1, tiled=True)]
    ppermute x0 -> x18, waiting for transfers between devices: none -> 66.7 us  [send(): lax.ppermute(values, 'tp', [(i, (i + by) % count) for i in range(count)])]
    ppermute x0 -> x18, starting transfers between devices: none -> 56 us  [send(): lax.ppermute(values, 'tp', [(i, (i + by) % count) for i in range(count)])]
    all_to_all x1 -> x0, waiting for transfers between devices: 45 us -> none  [per_device(): lax.all_to_all(query_grad_t.reshape(tp, query_width // tp, rows), 'tp', 0...]
    all_to_all x1 -> x0, blocking collectives: 36 us -> none  [per_device(): lax.all_to_all(attended_t.reshape(tp, query_width // tp, rows), 'tp', 0, 0)]
  transfers between devices with their start and end apart: 21 -> 32, of which waited for: 16 -> 7; matrix products, arithmetic and copies ran while one was open for 23% -> 27% of each run, Pallas kernels for 6% -> 47%
where the time goes in v1:
time: 930 us; the launch traced here: 919 us
  Pallas kernels  431 us (46%)
  matrix products  187 us (20%)
  waiting for transfers between devices  99.1 us (11%)
  local copies, waits for them, and re-layouts  65.2 us (7%)
  starting transfers between devices  63 us (7%)
  other arithmetic  55.7 us (6%)
  between operations  17.5 us (2%)
    dot_general x27, matrix products, dot(): lax.dot_general(left, right, (((left_dim,), (right_dim,)), ((), ())), pre...  187 us
    pallas_call x2, Pallas kernels, line_gather(): pl.pallas_call(functools.partial(line_gather_kernel, count), name='line_g...  114 us
    pallas_call x2, Pallas kernels, line_sum(): pl.pallas_call(functools.partial(line_sum_kernel, count), name='line_sum'...  110 us
    ppermute x18, waiting for transfers between devices, send(): lax.ppermute(values, 'tp', [(i, (i + by) % count) for i in range(count)])  66.7 us
    pallas_call x1, Pallas kernels, attend_back(): pl.pallas_call(functools.partial(attend_back_kernel, group, count), name=...  61.6 us
    pallas_call x1, Pallas kernels, attend(): pl.pallas_call(functools.partial(attend_kernel, group, count), name='atte...  61.1 us
    ppermute x18, starting transfers between devices, send(): lax.ppermute(values, 'tp', [(i, (i + by) % count) for i in range(count)])  56 us
    pallas_call x1, Pallas kernels, backward_scan(): scan_call(backward_kernel, 'backward_scan', tiles, [rows, mixed_s, select...  40.4 us
  transfers between devices with their start and end apart: 32, of which 7 were waited for; matrix products, arithmetic and copies ran while one was open for 27% of the time, Pallas kernels for 47%

profile of v1, /device:TPU:0, one launch (start us, length us, event | category | flops | bytes accessed | tf_op | source)
XLA Modules:
  0.0 919.1 jit_solution(3112158666884624776)
XLA Ops:
  13.6 6.3 concatenate.65
  25.3 59.9 %line_gather.2 = bf16[1600,1024]{1,0:T(8,128)(2,1)} custom-call(bf16[1600,256]{1,0:T(8,128)(2,1)} %bitcast.120), custom_call_target="tpu_custom_call" | custom-call | tf_op jit(solution)/shard_map/line_gather/pallas_call | solution.py:482
  103.4 12.6 %fusion.8.mixed = f32[1024,2400]{1,0:T(8,128)} fusion(bf16[1600,1024]{1,0:T(8,128)(2,1)S(1)} %fusion.10, bf16[1600,2528]{1,0:T(8,128)(2,1)S(1)} %bitcast.135), kind=kOutput, calls=%fused_computation.14 | convolution fusion | flops 7864320000 | bytes 20889600 | tf_op jit(solution)/shard_map/dot_general | solution.py:818
  116.1 12.4 %end_state.1 = f32[16,800]{1,0:T(8,128)S(1)} custom-call(f32[1024,2400]{1,0:T(8,128)} %fusion.8.mixed, bf16[32,1024]{1,0:T(8,128)(2,1)S(1)} %convolution_convert_fusion.10.select_t, f32[1024,8]{1,0:T(8,128)S(1)} %copy.162.aux, f32[8,1024]{1,0:T(8,128)S(1)} %stack.56.aux_t, f32[256,1]{1,0:T(8,128)S(1)} %fusion.132.alive_last, ...), custom_call_target="tpu_custom_call" | custom-call | flops 10000000000 | bytes 16777216 | tf_op jit(solution)/shard_map/end_state/pallas_call | solution.py:307
  132.6 18.9 %forward_scan.1 = (bf16[1024,800]{1,0:T(8,128)(2,1)S(1)}, bf16[4096,800]{1,0:T(8,128)(2,1)}, f32[16,800]{1,0:T(8,128)S(1)}) custom-call(f32[1024,2400]{1,0:T(8,128)} %fusion.8.mixed, bf16[1024,32]{1,0:T(8,128)(2,1)S(1)} %copy.161.select, bf16[32,1024]{1,0:T(8,128)(2,1)S(1)} %convolution_convert_fusion.10.select_t, f32[1024,8]{1,0:T(8,128)S(1)} %copy.162.aux, ...), custom_call_target="tpu_custom_call" | custom-call | flops 16000000000 | bytes 16777216 | tf_op jit(solution)/shard_map/forward_scan/pallas_call | solution.py:324
  151.4 7.6 fusion.39.source
  161.5 6.1 all-gather.6.cloned.1.call-done
  168.8 5.3 convolution_convert_fusion.8
  186.4 61.1 %attend.1 = (bf16[1600,256]{1,0:T(8,128)(2,1)}, f32[5,8,256]{2,1,0:T(8,128)}, f32[1600,256]{1,0:T(8,128)}) custom-call(bf16[1600,256]{1,0:T(8,128)(2,1)} %fusion.45.query_t, bf16[640,1408]{1,0:T(8,128)(2,1)} %pad_maximum_fusion.3.key_t.value_t, bf16[640,1408]{1,0:T(8,128)(2,1)} %pad_maximum_fusion.3.key_t.value_t, f32[1408,256]{1,0:T(8,128)} %concatenate.70.bias, ...), custom_call_target="tpu_custom_call" | custom-call | tf_op jit(solution)/shard_map/attend/pallas_call | solution.py:735
  257.1 54.0 %line_gather.3 = bf16[1600,1024]{1,0:T(8,128)(2,1)} custom-call(bf16[1600,256]{1,0:T(8,128)(2,1)} %multiply_convert_fusion.4.source), custom_call_target="tpu_custom_call" | custom-call | tf_op jit(solution)/shard_map/line_gather/pallas_call | solution.py:482
  311.2 17.0 %fusion.2 = f32[2816,1024]{1,0:T(8,128)} fusion(bf16[1600,1024]{1,0:T(8,128)(2,1)} %line_gather.3, bf16[1600,4224]{1,0:T(8,128)(2,1)} %all-gather.14.cloned.1.call-done), kind=kOutput, calls=%fused_computation.7 | convolution fusion | flops 9227468800 | bytes 23822336 | tf_op jit(solution)/shard_map/dot_general | solution.py:818
  328.2 13.5 %multiply_convert_fusion.2 = (bf16[1408,1024]{1,0:T(8,128)(2,1)S(1)}, bf16[1408,1024]{1,0:T(8,128)(2,1)S(1)}, bf16[1408,1024]{1,0:T(8,128)(2,1)}) fusion(f32[2816,1024]{1,0:T(8,128)} %fusion.2, bf16[1600,256]{1,0:T(8,128)(2,1)S(1)} %copy-done.42, bf16[1600,256]{1,0:T(8,128)(2,1)S(1)} %copy-done.43, bf16[1600,256]{1,0:T(8,128)(2,1)S(1)} %copy-done.44, ...), kind=kOutput, calls=%fused_computation.23 | convolution fusion | flops 4649910272 | bytes 27967488 | tf_op jit(solution)/shard_map/dot_general | solution.py:818
  346.2 13.3 %fusion.24 = bf16[1600,1024]{1,0:T(8,128)(2,1)} fusion(bf16[2816,1024]{1,0:T(8,128)(2,1)S(1)} %pad_maximum_fusion.1, bf16[1600,4224]{1,0:T(8,128)(2,1)} %all-gather.14.cloned.1.call-done), kind=kOutput, calls=%fused_computation.36 | convolution fusion | flops 9229107200 | bytes 18055168 | tf_op jit(solution)/shard_map/dot_general | solution.py:818
  363.0 8.0 convolution_convert_fusion.2
  371.0 9.0 fusion.21.source
  380.0 12.9 %convolution_convert_fusion.1 = bf16[1600,2816]{1,0:T(8,128)(2,1)S(1)} fusion(bf16[1600,1024]{1,0:T(8,128)(2,1)} %line_gather.3, bf16[2816,1024]{1,0:T(8,128)(2,1)} %copy-done.30), kind=kOutput, calls=%fused_computation.2 | convolution fusion | flops 9231974400 | bytes 18055168 | tf_op jit(solution)/shard_map/dot_general | solution.py:818
  392.9 6.4 pad_maximum_fusion
  399.3 24.8 %reduce-scatter.11.cloned.1.call-done = bf16[1600,256]{1,0:T(8,128)(2,1)} async-done(((bf16[1600,1024]{1,0:T(8,128)(2,1)}), bf16[1600,256]{1,0:T(8,128)(2,1)}) %reduce-scatter.11.cloned.1.call-update) | async-done | bytes 819216 | tf_op jit(solution)/shard_map/reduce_scatter | solution.py:1042
  432.2 7.0 fusion.48.grad_t
  439.2 61.6 %attend_back.1 = (bf16[1600,256]{1,0:T(8,128)(2,1)}, f32[320,1408]{1,0:T(8,128)}, f32[320,1408]{1,0:T(8,128)}, bf16[1600,1024]{1,0:T(8,128)(2,1)}) custom-call(bf16[1600,256]{1,0:T(8,128)(2,1)} %fusion.45.query_t, bf16[640,1408]{1,0:T(8,128)(2,1)} %pad_maximum_fusion.3.key_t.value_t, bf16[640,1408]{1,0:T(8,128)(2,1)} %pad_maximum_fusion.3.key_t.value_t, ...), custom_call_target="tpu_custom_call" | custom-call | tf_op jit(solution)/shard_map/attend_back/pallas_call | solution.py:774
  500.8 5.9 fusion.155.gated_grad
  506.7 13.2 %end_adjoint.1 = f32[16,800]{1,0:T(8,128)S(1)} custom-call(f32[1024,800]{1,0:T(8,128)S(1)} %fusion.155.gated_grad, f32[1024,2400]{1,0:T(8,128)} %fusion.8.mixed, bf16[32,1024]{1,0:T(8,128)(2,1)S(1)} %convolution_convert_fusion.10.select_t, f32[1024,8]{1,0:T(8,128)S(1)} %copy.162.aux, f32[8,1024]{1,0:T(8,128)S(1)} %stack.56.aux_t, ...), custom_call_target="tpu_custom_call" | custom-call | flops 10000000000 | bytes 16777216 | tf_op jit(solution)/shard_map/end_adjoint/pallas_call | solution.py:345
  528.7 40.4 %backward_scan.1 = (bf16[1024,2400]{1,0:T(8,128)(2,1)}, f32[1024,32]{1,0:T(8,128)S(1)}, f32[8,800]{1,0:T(8,128)S(1)}) custom-call(f32[1024,800]{1,0:T(8,128)S(1)} %copy-done.6, f32[1024,2400]{1,0:T(8,128)} %fusion.8.mixed, bf16[1024,32]{1,0:T(8,128)(2,1)S(1)} %copy-done.4, bf16[32,1024]{1,0:T(8,128)(2,1)S(1)} %convolution_convert_fusion.10.select_t, ...), custom_call_target="tpu_custom_call" | custom-call | flops 35999997952 | bytes 16777216 | tf_op jit(solution)/shard_map/backward_scan/pallas_call | solution.py:362
  569.1 13.3 %convolution_convert_fusion = bf16[1600,2400]{1,0:T(8,128)(2,1)} fusion(bf16[1600,1024]{1,0:T(8,128)(2,1)S(1)} %copy-done.10, bf16[1024,2400]{1,0:T(8,128)(2,1)} %get-tuple-element.129), kind=kOutput, calls=%fused_computation.1 | convolution fusion | flops 7868160000 | bytes 15872000 | tf_op jit(solution)/shard_map/dot_general | solution.py:818
  602.0 5.4 fusion.67
  611.2 60.1 %collective-permute-done.10 = bf16[160,1152]{1,0:T(8,128)(2,1)S(1)} collective-permute-done((bf16[160,1152]{1,0:T(8,128)(2,1)S(1)}, bf16[160,1152]{1,0:T(8,128)(2,1)S(1)}, u32[]{:S(2)}, u32[]{:S(2)}) %collective-permute-start.10) | collective-permute-done | bytes 368672 | tf_op jit(solution)/shard_map/ppermute | solution.py:833
  676.0 22.8 %collective-permute-start.14 = (bf16[400,256]{1,0:T(8,128)(2,1)}, bf16[400,256]{1,0:T(8,128)(2,1)S(1)}, u32[]{:S(2)}, u32[]{:S(2)}) collective-permute-start(bf16[400,256]{1,0:T(8,128)(2,1)} %get-tuple-element.278), channel_id=1, source_target_pairs={{0,2},{1,3},{2,0},{3,1},{4,6},{5,7},{6,4},{7,5},{8,10},{9,11},{10,... | collective-permute-start | bytes 614408 | tf_op jit(solution)/shard_map/ppermute | solution.py:833
  703.0 11.0 %collective-permute-start.13 = (bf16[400,256]{1,0:T(8,128)(2,1)}, bf16[400,256]{1,0:T(8,128)(2,1)S(1)}, u32[]{:S(2)}, u32[]{:S(2)}) collective-permute-start(bf16[400,256]{1,0:T(8,128)(2,1)} %get-tuple-element.279), channel_id=1, source_target_pairs={{0,1},{1,2},{2,3},{3,0},{4,5},{5,6},{6,7},{7,4},{8,9},{9,10},{10,1... | collective-permute-start | bytes 614408 | tf_op jit(solution)/shard_map/ppermute | solution.py:833
  729.2 14.5 %fusion.6 = f32[1600,1024]{1,0:T(8,128)} fusion(bf16[1024,2400]{1,0:T(8,128)(2,1)} %get-tuple-element.129, bf16[1600,2528]{1,0:T(8,128)(2,1)} %all-gather.8.cloned.1.call-done), kind=kOutput, calls=%fused_computation.12 | convolution fusion | flops 7864320000 | bytes 19316736 | tf_op jit(solution)/shard_map/dot_general | solution.py:818
  760.9 9.2 concatenate.84
  776.3 57.4 %line_sum.2 = f32[1600,256]{1,0:T(8,128)S(1)} custom-call(bf16[1600,1024]{1,0:T(8,128)(2,1)S(1)} %get-tuple-element.132.source), custom_call_target="tpu_custom_call" | custom-call | tf_op jit(solution)/shard_map/line_sum/pallas_call | solution.py:612
  836.0 52.6 %line_sum.3 = f32[1600,256]{1,0:T(8,128)S(1)} custom-call(bf16[1600,1024]{1,0:T(8,128)(2,1)S(1)} %copy-done.2), custom_call_target="tpu_custom_call" | custom-call | tf_op jit(solution)/shard_map/line_sum/pallas_call | solution.py:612
  (356 shorter events, 178.3 us)
Async XLA Ops:
  7.2 88.0 %all-gather.8.cloned.1.call-start = ((), (), s32[]{:S(2)}) async-start(), calls=%async_computation.5 | async-start | bytes 9216000 | tf_op jit(solution)/shard_map/all_gather | solution.py:824
  23.8 127.7 %all-gather.10.cloned.1.call-start = ((), (), s32[]{:S(2)}) async-start(), calls=%async_computation.6 | async-start | bytes 3225600 | tf_op jit(solution)/shard_map/all_gather | solution.py:824
  24.5 143.0 %all-gather.6.cloned.1.call-start = ((), (), s32[]{:S(2)}) async-start(), calls=%async_computation.4 | async-start | bytes 8755200 | tf_op jit(solution)/shard_map/all_gather | solution.py:824
  25.3 224.4 %all-gather.12.cloned.1.call-start = ((), (), s32[]{:S(2)}) async-start(), calls=%async_computation.7 | async-start | bytes 5990400 | tf_op jit(solution)/shard_map/all_gather | solution.py:824
  85.2 73.8 %collective-permute-start.4 = (bf16[1600,256]{1,0:T(8,128)(2,1)}, bf16[1600,256]{1,0:T(8,128)(2,1)}, u32[]{:S(2)}, u32[]{:S(2)}) collective-permute-start(bf16[1600,256]{1,0:T(8,128)(2,1)} %bitcast.4), channel_id=1, source_target_pairs={{0,3},{1,0},{2,1},{3,2},{4,7},{5,4},{6,5},{7,6},{8,11},{9,8},{10,9... | collective-permute-start | bytes 2457608 | tf_op jit(solution)/shard_map/ppermute | solution.py:833
  87.7 71.4 %collective-permute-start.3 = (bf16[1600,256]{1,0:T(8,128)(2,1)}, bf16[1600,256]{1,0:T(8,128)(2,1)}, u32[]{:S(2)}, u32[]{:S(2)}) collective-permute-start(bf16[1600,256]{1,0:T(8,128)(2,1)} %bitcast.4), channel_id=1, source_target_pairs={{0,2},{1,3},{2,0},{3,1},{4,6},{5,7},{6,4},{7,5},{8,10},{9,11},{10,... | collective-permute-start | bytes 2457608 | tf_op jit(solution)/shard_map/ppermute | solution.py:833
  87.7 71.4 %collective-permute-start.2 = (bf16[1600,256]{1,0:T(8,128)(2,1)}, bf16[1600,256]{1,0:T(8,128)(2,1)}, u32[]{:S(2)}, u32[]{:S(2)}) collective-permute-start(bf16[1600,256]{1,0:T(8,128)(2,1)} %bitcast.4), channel_id=1, source_target_pairs={{0,1},{1,2},{2,3},{3,0},{4,5},{5,6},{6,7},{7,4},{8,9},{9,10},{10,1... | collective-permute-start | bytes 2457608 | tf_op jit(solution)/shard_map/ppermute | solution.py:833
  88.4 222.8 %all-gather.14.cloned.1.call-start = ((), (), s32[]{:S(2)}) async-start(), calls=%async_computation.8 | async-start | bytes 15206400 | tf_op jit(solution)/shard_map/all_gather | solution.py:824
  128.5 4.1 collective-permute-start.1
  159.1 265.0 %reduce-scatter.11.cloned.1.call-start = ((), (), s32[]{:S(2)}) async-start(), calls=%async_computation.9 | async-start | bytes 4096000 | tf_op jit(solution)/shard_map/reduce_scatter | solution.py:1042
  174.1 10.1 %collective-permute-start = (bf16[640,1024]{1,0:T(8,128)(2,1)S(1)}, bf16[640,1024]{1,0:T(8,128)(2,1)S(1)}, u32[]{:S(2)}, u32[]{:S(2)}) collective-permute-start(bf16[640,1024]{1,0:T(8,128)(2,1)S(1)} %convolution_convert_fusion.8), channel_id=1, source_target_pairs={{0,4},{1,5},{2,6},{3,7},{8,12},{9,13},{10,14},{11,15},{16,20},{17,... | collective-permute-start | bytes 3932168 | tf_op jit(solution)/shard_map/ppermute | solution.py:974
  344.1 15.4 %collective-permute-start.7 = (bf16[400,256]{1,0:T(8,128)(2,1)}, bf16[400,256]{1,0:T(8,128)(2,1)S(1)}, u32[]{:S(2)}, u32[]{:S(2)}) collective-permute-start(bf16[400,256]{1,0:T(8,128)(2,1)} %get-tuple-element.282), channel_id=1, source_target_pairs={{0,3},{1,0},{2,1},{3,2},{4,7},{5,4},{6,5},{7,6},{8,11},{9,8},{10,9... | collective-permute-start | bytes 614408 | tf_op jit(solution)/shard_map/ppermute | solution.py:833
  345.5 15.5 %collective-permute-start.6 = (bf16[400,256]{1,0:T(8,128)(2,1)}, bf16[400,256]{1,0:T(8,128)(2,1)S(1)}, u32[]{:S(2)}, u32[]{:S(2)}) collective-permute-start(bf16[400,256]{1,0:T(8,128)(2,1)} %get-tuple-element.283), channel_id=1, source_target_pairs={{0,2},{1,3},{2,0},{3,1},{4,6},{5,7},{6,4},{7,5},{8,10},{9,11},{10,... | collective-permute-start | bytes 614408 | tf_op jit(solution)/shard_map/ppermute | solution.py:833
  345.5 15.5 %collective-permute-start.5 = (bf16[400,256]{1,0:T(8,128)(2,1)S(1)}, bf16[400,256]{1,0:T(8,128)(2,1)}, u32[]{:S(2)}, u32[]{:S(2)}) collective-permute-start(bf16[400,256]{1,0:T(8,128)(2,1)S(1)} %get-tuple-element.284), channel_id=1, source_target_pairs={{0,1},{1,2},{2,3},{3,0},{4,5},{5,6},{6,7},{7,4},{8,9},{9,10},{10,1... | collective-permute-start | bytes 614408 | tf_op jit(solution)/shard_map/ppermute | solution.py:833
  362.9 163.7 %reduce-scatter.13.cloned.1.call-start = ((), (), s32[]{:S(2)}) async-start(), calls=%async_computation.11 | async-start | bytes 15206400
  424.2 158.2 %reduce-scatter.15.cloned.1.call-start = ((), (), s32[]{:S(2)}) async-start(), calls=%async_computation.12 | async-start | bytes 3225600
  520.0 6.6 collective-permute-start.8
  526.5 243.5 %reduce-scatter.17.cloned.1.call-start = ((), (), s32[]{:S(2)}) async-start(), calls=%async_computation.13 | async-start | bytes 8755200
  582.4 314.0 %all-reduce.12.cloned.1.call-start = ((), (), s32[]{:S(2)}) async-start(), calls=%async_computation.10 | async-start | bytes 9011200
  586.7 8.2 collective-permute-start.9
  592.3 126.6 %collective-permute-start.18 = (bf16[1600,256]{1,0:T(8,128)(2,1)}, bf16[1600,256]{1,0:T(8,128)(2,1)}, u32[]{:S(2)}, u32[]{:S(2)}) collective-permute-start(bf16[1600,256]{1,0:T(8,128)(2,1)} %get-tuple-element.118), channel_id=1, source_target_pairs={{0,3},{1,0},{2,1},{3,2},{4,7},{5,4},{6,5},{7,6},{8,11},{9,8},{10,9... | collective-permute-start | bytes 2457608 | tf_op jit(solution)/shard_map/ppermute | solution.py:833
  594.8 124.1 %collective-permute-start.17 = (bf16[1600,256]{1,0:T(8,128)(2,1)}, bf16[1600,256]{1,0:T(8,128)(2,1)}, u32[]{:S(2)}, u32[]{:S(2)}) collective-permute-start(bf16[1600,256]{1,0:T(8,128)(2,1)} %get-tuple-element.118), channel_id=1, source_target_pairs={{0,2},{1,3},{2,0},{3,1},{4,6},{5,7},{6,4},{7,5},{8,10},{9,11},{10,... | collective-permute-start | bytes 2457608 | tf_op jit(solution)/shard_map/ppermute | solution.py:833
  597.0 74.4 %collective-permute-start.10 = (bf16[160,1152]{1,0:T(8,128)(2,1)S(1)}, bf16[160,1152]{1,0:T(8,128)(2,1)S(1)}, u32[]{:S(2)}, u32[]{:S(2)}) collective-permute-start(bf16[160,1152]{1,0:T(8,128)(2,1)S(1)} %get-tuple-element.270), channel_id=1, source_target_pairs={{0,2},{1,3},{2,0},{3,1},{4,6},{5,7},{6,4},{7,5},{8,10},{9,11},{10,... | collective-permute-start | bytes 1105928 | tf_op jit(solution)/shard_map/ppermute | solution.py:833
  600.0 73.2 %collective-permute-start.12 = (bf16[160,1152]{1,0:T(8,128)(2,1)S(1)}, bf16[160,1152]{1,0:T(8,128)(2,1)S(1)}, u32[]{:S(2)}, u32[]{:S(2)}) collective-permute-start(bf16[160,1152]{1,0:T(8,128)(2,1)S(1)} %get-tuple-element.271), channel_id=1, source_target_pairs={{0,3},{1,0},{2,1},{3,2},{4,7},{5,4},{6,5},{7,6},{8,11},{9,8},{10,9... | collective-permute-start | bytes 1105928 | tf_op jit(solution)/shard_map/ppermute | solution.py:833
  600.5 75.5 %collective-permute-start.11 = (bf16[160,1152]{1,0:T(8,128)(2,1)S(1)}, bf16[160,1152]{1,0:T(8,128)(2,1)S(1)}, u32[]{:S(2)}, u32[]{:S(2)}) collective-permute-start(bf16[160,1152]{1,0:T(8,128)(2,1)S(1)} %get-tuple-element.272), channel_id=1, source_target_pairs={{0,1},{1,2},{2,3},{3,0},{4,5},{5,6},{6,7},{7,4},{8,9},{9,10},{10,1... | collective-permute-start | bytes 1105928 | tf_op jit(solution)/shard_map/ppermute | solution.py:833
  671.3 47.6 %collective-permute-start.16 = (bf16[1600,256]{1,0:T(8,128)(2,1)}, bf16[1600,256]{1,0:T(8,128)(2,1)}, u32[]{:S(2)}, u32[]{:S(2)}) collective-permute-start(bf16[1600,256]{1,0:T(8,128)(2,1)} %get-tuple-element.118), channel_id=1, source_target_pairs={{0,1},{1,2},{2,3},{3,0},{4,5},{5,6},{6,7},{7,4},{8,9},{9,10},{10,1... | collective-permute-start | bytes 2457608 | tf_op jit(solution)/shard_map/ppermute | solution.py:833
  673.2 29.8 %collective-permute-start.15 = (bf16[400,256]{1,0:T(8,128)(2,1)S(1)}, bf16[400,256]{1,0:T(8,128)(2,1)S(1)}, u32[]{:S(2)}, u32[]{:S(2)}) collective-permute-start(bf16[400,256]{1,0:T(8,128)(2,1)S(1)} %get-tuple-element.277), channel_id=1, source_target_pairs={{0,3},{1,0},{2,1},{3,2},{4,7},{5,4},{6,5},{7,6},{8,11},{9,8},{10,9... | collective-permute-start | bytes 614408 | tf_op jit(solution)/shard_map/ppermute | solution.py:833
  676.0 41.9 %collective-permute-start.14 = (bf16[400,256]{1,0:T(8,128)(2,1)}, bf16[400,256]{1,0:T(8,128)(2,1)S(1)}, u32[]{:S(2)}, u32[]{:S(2)}) collective-permute-start(bf16[400,256]{1,0:T(8,128)(2,1)} %get-tuple-element.278), channel_id=1, source_target_pairs={{0,2},{1,3},{2,0},{3,1},{4,6},{5,7},{6,4},{7,5},{8,10},{9,11},{10,... | collective-permute-start | bytes 614408 | tf_op jit(solution)/shard_map/ppermute | solution.py:833
  703.0 15.9 %collective-permute-start.13 = (bf16[400,256]{1,0:T(8,128)(2,1)}, bf16[400,256]{1,0:T(8,128)(2,1)S(1)}, u32[]{:S(2)}, u32[]{:S(2)}) collective-permute-start(bf16[400,256]{1,0:T(8,128)(2,1)} %get-tuple-element.279), channel_id=1, source_target_pairs={{0,1},{1,2},{2,3},{3,0},{4,5},{5,6},{6,7},{7,4},{8,9},{9,10},{10,1... | collective-permute-start | bytes 614408 | tf_op jit(solution)/shard_map/ppermute | solution.py:833
  899.6 10.3 %collective-permute-start.19 = (bf16[1,200,44]{1,2,0:T(8,128)(2,1)S(1)}, bf16[1,200,44]{1,2,0:T(8,128)(2,1)S(1)}, u32[]{:S(2)}, u32[]{:S(2)}) collective-permute-start(bf16[1,200,44]{1,2,0:T(8,128)(2,1)S(1)} %get-tuple-element.287), channel_id=1, source_target_pairs={{0,2},{1,3},{2,0},{3,1},{4,6},{5,7},{6,4},{7,5},{8,10},{9,11},{10,... | collective-permute-start | bytes 52808 | tf_op jit(solution)/shard_map/ppermute | solution.py:833
  902.4 7.6 collective-permute-start.21
  904.4 5.6 collective-permute-start.20
  (73 other events, 1419.6 us)
Sparse Core Ops, SparseCore 0:
  23.9 56.2 all-gather.7
  82.0 31.1 all-gather.9
  115.7 51.8 all-gather.5
  169.3 41.4 all-gather.11
  212.5 76.0 all-gather.13
  363.1 61.0 reduce-scatter.10
  427.7 98.2 reduce-scatter.12
  529.8 48.6 reduce-scatter.14
  582.5 82.2 reduce-scatter.16
  770.2 83.8 all-reduce.11

commit v2 on v1

--- a/solution.py
+++ b/solution.py
@@ -4,6 +4,7 @@
 import jax.numpy as jnp
 from jax import lax
 from jax.experimental import pallas as pl
+from jax.experimental.layout import Layout, with_layout_constraint
 from jax.experimental.pallas import tpu as pltpu
 from jax.sharding import PartitionSpec as P
 
@@ -189,13 +190,54 @@
     end[...] = state[...]
 
 
-def backward_kernel(gated_grad, mixed, select, select_t, states, aux, aux_t, alive_last, bias, rate, skip, start, final,
-                    mix_grad, select_grad, sums, state, local, block, adjoint, bound, edge):
-    @pl.when(pl.program_id(0) == 0)
+def backward_kernel(
+    count,
+    gated_grad,
+    mixed,
+    select,
+    select_t,
+    states,
+    aux,
+    aux_t,
+    alive_last,
+    bias,
+    rate,
+    skip,
+    start,
+    final,
+    source,
+    mix_grad,
+    select_grad,
+    sums,
+    total_out,
+    state,
+    local,
+    block,
+    adjoint,
+    bound,
+    edge,
+    own,
+    sent,
+    got,
+    loads,
+    send_sems,
+    recv_sems,
+):
+    tile, tiles = pl.program_id(0), pl.num_programs(0)
+    begin, step_line, finish = line_sum_steps(
+        count, source, own, sent, got, total_out, loads, send_sems, recv_sems
+    )
+
+    @pl.when(tile == 0)
     def _():
+        begin()
         state[...] = start[...]
         edge[...] = jnp.sum(start[...] * final[...], axis=0, keepdims=True)
         sums[...] = jnp.zeros_like(sums)
+
+    @pl.when(tile == tiles // 2)
+    def _():
+        step_line(1)
 
     raw, step, log_decay, upto, after, total = decays(part(mixed, 2), bias, rate, alive_last)
     channels = state.shape[1]
@@ -241,6 +283,12 @@
     sums[1:2, :] += jnp.sum(decay_grad * log_decay, axis=0, keepdims=True)
     sums[2:3, :] += jnp.sum(dy * x, axis=0, keepdims=True)
 
+    @pl.when(tile == tiles - 1)
+    def _():
+        for k in range(2, count):
+            step_line(k)
+        finish()
+
 
 def scan_specs(tokens, channels, back):
     tiles = tokens // TILE
@@ -261,7 +309,15 @@
     return tiles, mixed, rows, select, select_t, states, aux, aux_t, last, row, state
 
 
-def scan_call(kernel, name, tiles, in_specs, out_specs, out_shape, scratch, flops):
+def scan_scratch(channels):
+    return [
+        pltpu.VMEM((STATE, channels), f32),
+        pltpu.VMEM((TILE // SUB * STATE, channels), f32),
+        pltpu.VMEM((TILE // SUB, channels), f32),
+    ]
+
+
+def scan_call(kernel, name, tiles, in_specs, out_specs, out_shape, scratch, flops, collective=None):
     return pl.pallas_call(
         kernel,
         name=name,
@@ -270,20 +326,14 @@
         out_specs=out_specs,
         scratch_shapes=scratch,
         out_shape=out_shape,
-        compiler_params=PARAMS,
+        compiler_params=pltpu.CompilerParams(
+            vmem_limit_bytes=48 << 20,
+            dimension_semantics=("arbitrary",),
+            collective_id=collective,
+            has_side_effects=collective is not None,
+        ),
         cost_estimate=pl.CostEstimate(flops=flops, bytes_accessed=1 << 24, transcendentals=0),
     )
-
-
-def scan_scratch(channels):
-    return [
-        pltpu.VMEM((STATE, channels), f32),
-        pltpu.VMEM((TILE // SUB * STATE, channels), f32),
-        pltpu.VMEM((TILE // SUB, channels), f32),
-    ]
-
-
-PARAMS = pltpu.CompilerParams(vmem_limit_bytes=48 << 20, dimension_semantics=("arbitrary",))
 
 
 def scan_aux(segment, before):
@@ -354,30 +404,42 @@
     )(gated_grad, mixed, select_t, *aux, bias, rate)
 
 
-def backward_scan(gated_grad, mixed, select, select_t, states, aux, bias, rate, skip, start, final):
+def backward_scan(
+    gated_grad, mixed, select, select_t, states, aux, bias, rate, skip, start, final, source, count, collective
+):
+    height, each = source.shape[0], source.shape[1] // count
     tokens, channels = mixed.shape[0], mixed.shape[1] // 3
     tiles, mixed_s, rows, select_s, select_t_s, states_s, aux_s, aux_t_s, last_s, row, state = scan_specs(
         tokens, channels, True
     )
     return scan_call(
-        backward_kernel,
+        functools.partial(backward_kernel, count),
         "backward_scan",
         tiles,
-        [rows, mixed_s, select_s, select_t_s, states_s, aux_s, aux_t_s, last_s, row, row, row, state, state],
-        [mixed_s, select_s, pl.BlockSpec((8, channels), lambda i: (0, 0))],
+        [rows, mixed_s, select_s, select_t_s, states_s, aux_s, aux_t_s, last_s, row, row, row, state, state]
+        + [pl.BlockSpec(memory_space=pl.ANY)],
+        [
+            mixed_s,
+            select_s,
+            pl.BlockSpec((8, channels), lambda i: (0, 0)),
+            pl.BlockSpec((height, each), lambda i: (0, 0)),
+        ],
         [
             jax.ShapeDtypeStruct((tokens, 3 * channels), bf16),
             jax.ShapeDtypeStruct((tokens, 2 * STATE), f32),
             jax.ShapeDtypeStruct((8, channels), f32),
+            jax.ShapeDtypeStruct((height, each), f32),
         ],
         scan_scratch(channels)
         + [
             pltpu.VMEM((TILE // SUB * STATE, channels), bf16),
             pltpu.VMEM((TILE // SUB, channels), f32),
             pltpu.VMEM((1, channels), f32),
-        ],
+        ]
+        + line_sum_scratch(count, height, each),
         36 * 10**9,
-    )(gated_grad, mixed, select, select_t, states, *aux, bias, rate, skip, start, final)
+        collective,
+    )(gated_grad, mixed, select, select_t, states, *aux, bias, rate, skip, start, final, source)
 
 
 MESH = pl.DeviceIdType.MESH
@@ -683,8 +745,7 @@
     grad_t,
     source,
     query_grad_t,
-    key_grad_t,
-    value_grad_t,
+    keyval_grad_t,
     target,
     copies,
     send_sems,
@@ -704,8 +765,8 @@
     keys_t = key_t[...]
     keys = keys_t.T
     values = value_t[...].T
-    key_sum = jnp.zeros(key_grad_t.shape, f32)
-    value_sum = jnp.zeros(value_grad_t.shape, f32)
+    key_sum = jnp.zeros(keys_t.shape, f32)
+    value_sum = jnp.zeros(keys_t.shape, f32)
     for g in range(group):
         at = slice(g * HEAD_SIZE, (g + 1) * HEAD_SIZE)
         query = query_t[at, :] * 0.125
@@ -716,8 +777,8 @@
         query_grad_t[at, :] = (mm(keys_t, score_grad) * 0.125).astype(bf16)
         key_sum = key_sum + mm_nt(query, score_grad)
         value_sum = value_sum + mm_nt(grad, probs.astype(bf16))
-    key_grad_t[...] = key_sum
-    value_grad_t[...] = value_sum
+    keyval_grad_t[0] = key_sum.astype(bf16)
+    keyval_grad_t[1] = value_sum.astype(bf16)
 
     @pl.when(head == heads - 1)
     def _():
@@ -785,11 +846,10 @@
             wide,
             anywhere,
         ],
-        out_specs=[wide, head, head, anywhere],
+        out_specs=[wide, pl.BlockSpec((2, HEAD_SIZE, keys), lambda h: (0, h, 0)), anywhere],
         out_shape=[
             jax.ShapeDtypeStruct((width, rows), bf16),
-            jax.ShapeDtypeStruct((kv * HEAD_SIZE, keys), f32),
-            jax.ShapeDtypeStruct((kv * HEAD_SIZE, keys), f32),
+            jax.ShapeDtypeStruct((2, kv * HEAD_SIZE, keys), bf16),
             jax.ShapeDtypeStruct((source.shape[0], source.shape[1] * count), source.dtype),
         ],
         scratch_shapes=line_scratch(count),
@@ -824,8 +884,14 @@
     return lax.all_gather(whole, ("fsdp", "ctx"), axis=0, tiled=True)
 
 
+def by_rows(values):
+    return with_layout_constraint(values, Layout((0, 1)))
+
+
 def scatter_rows(whole):
-    return lax.psum_scatter(whole, ("fsdp", "ctx"), scatter_dimension=0, tiled=True)
+    return by_rows(
+        lax.psum_scatter(by_rows(whole), ("fsdp", "ctx"), scatter_dimension=0, tiled=True)
+    )
 
 
 def send(values, by):
@@ -1033,12 +1099,7 @@
         ],
         axis=0,
     )
-    late_attended_t, gate_up_grad_t = lax.optimization_barrier((attended_t, gate_up_grad_t))
-    attended_columns_t = jnp.concatenate(permute_exchange(late_attended_t), axis=1)
     ffn_grad_part_t = dot(up_map, gate_up_grad_t, 1, 0).astype(bf16)
-    ffn_grad_part_t, attended_columns_t = lax.optimization_barrier(
-        (ffn_grad_part_t, attended_columns_t)
-    )
     ffn_normed_grad_t = lax.psum_scatter(ffn_grad_part_t, "tp", scatter_dimension=1, tiled=True)
     up_wide = dot(ffn_normed_group_t, gate_up_grad_t, 1, 1).astype(bf16)
     down_wide = dot(cotangent_group_t, hidden_t, 1, 1).astype(bf16)
@@ -1057,7 +1118,7 @@
     attn_grad_t = attn_grad.astype(bf16)
     mamba_grad_t = mamba_grad.astype(bf16)
     attended_grad_t = dot(attn_map, attn_grad_t, 0, 0).astype(bf16)
-    query_grad_t, key_grad_t, value_grad_t, mamba_grad_group_t = attend_back(
+    query_grad_t, keyval_grad_t, mamba_grad_group_t = attend_back(
         query_t,
         keyval_t,
         bias,
@@ -1069,25 +1130,50 @@
         tp,
         2,
     )
-    keyval_grad_t = jnp.concatenate([key_grad_t, value_grad_t], axis=0).astype(bf16)
+    query_pieces = permute_exchange(query_grad_t)
+    keyval_grad_t = keyval_grad_t.reshape(keyval_width, meta_count + window)
     placed = lax.dynamic_update_slice_in_dim(
         jnp.zeros((keyval_width, 2 * span), bf16), keyval_grad_t[:, meta_count:], key_start, 1
     )
     earlier_back = lax.ppermute(placed[:, :span], "ctx", [(1, 0)])
     current = placed[:, span:].astype(f32) + earlier_back.astype(f32)
-    with_meta = jnp.concatenate([keyval_grad_t[:, :meta_count], current.astype(bf16)], axis=1)
-    keyval_columns_t = permute_sums(with_meta, 0).astype(bf16)
-    out_wide = dot(mamba_grad_group_t, gated, 1, 0).astype(bf16)
-    out_columns = scatter_rows(out_wide)
-    query_pieces = permute_exchange(query_grad_t)
-    late_attn_grad_t, query_grad_t = lax.optimization_barrier((attn_grad_t, query_grad_t))
-    attn_grad_pieces = permute_gather(late_attn_grad_t)
-
+    keyval_part_t = current.astype(bf16)
+    keyval_meta_t = keyval_grad_t[:, :meta_count]
     gated_grad = dot(mamba_grad_group_t, state_out_map, 0, 0)
     adjoint_end = end_adjoint(gated_grad, mixed, selects_t, aux, bias_row, rate_row)
+    adjoint_end, late_attended_t, late_gated = lax.optimization_barrier(
+        (adjoint_end, attended_t, gated)
+    )
     adjoint_start = lax.ppermute(adjoint_end, "ctx", [(1, 0)])
-    adjoint_start, ffn_columns = lax.optimization_barrier((adjoint_start, ffn_columns))
-    mix_grad, select_grad, scan_sums = backward_scan(
+    late_attended_t, late_gated, query_pieces = lax.optimization_barrier(
+        (late_attended_t, late_gated, query_pieces)
+    )
+    meta_back, meta_terms = rms_back(meta_rows, mix_gain, dot(keyval_map, keyval_meta_t, 1, 0))
+    query_columns_t = in_order(query_pieces)
+    each = query_width // tp
+
+    def room(count):
+        return ((0, -count % 128), (0, 0))
+
+    query_wide = dot(normed_group_t, jnp.pad(query_columns_t, room(each)), 1, 1)
+    keyval_wide = dot(normed_group_t, keyval_part_t, 1, 1) + dot(
+        meta_normed_t, keyval_meta_t, 1, 1
+    )
+    early_pieces = [
+        dot(attn_grad_t, jnp.pad(late_attended_t, room(query_width)), 1, 1),
+        query_wide,
+        meta_back,
+        keyval_wide,
+        dot(mamba_grad_group_t, late_gated, 1, 0),
+    ]
+    early_wide = by_rows(
+        jnp.concatenate([by_rows(piece.astype(bf16)) for piece in early_pieces], axis=1)
+    )
+    early_columns = scatter_rows(early_wide)
+    adjoint_start, early_wide, ffn_columns = lax.optimization_barrier(
+        (adjoint_start, early_wide, ffn_columns)
+    )
+    mix_grad, select_grad, scan_sums, out_total = backward_scan(
         gated_grad,
         mixed,
         selects,
@@ -1099,126 +1185,95 @@
         skip_row,
         adjoint_start,
         state_final,
-    )
-    state_wide = dot(normed_group_t, mix_grad, 1, 0).astype(bf16)
-    state_wide, out_columns = lax.optimization_barrier((state_wide, out_columns))
-    state_columns = scatter_rows(state_wide)
-    (
-        state_wide,
-        mix_grad,
-        keyval_columns_t,
         out_part_t,
-        query_pieces,
-        attn_grad_pieces,
-    ) = lax.optimization_barrier(
-        (state_wide, mix_grad, keyval_columns_t, out_part_t, query_pieces, attn_grad_pieces)
-    )
-    query_columns_t = in_order(query_pieces)
-    attn_grad_group_t = jnp.concatenate(attn_grad_pieces, axis=1)
+        tp,
+        5,
+    )
+    layer_out_t = (mid + out_total).astype(bf16)
     select_grad_t = select_grad.T.astype(bf16)
-    keyval_part = lax.dynamic_slice_in_dim(
-        keyval_map, tp_index * (keyval_width // tp), keyval_width // tp, 1
-    )
     query_term = dot(query_map, query_grad_t, 1, 0)
     normed_grad_part = (
         dot(state_map, mix_grad, 1, 1)
         + dot(select_map, select_grad_t, 1, 0)
-        + dot(keyval_part, keyval_columns_t[:, meta_count:], 1, 0)
-    )
-    meta_grad_part = dot(keyval_part, keyval_columns_t[:, :meta_count], 1, 0)
+        + dot(keyval_map, keyval_part_t, 1, 0)
+    )
     _, group_terms = rms_back(residual_group, mix_gain, normed_grad_part)
-    meta_back, meta_terms = rms_back(meta_rows, mix_gain, meta_grad_part)
     _, query_terms = rms_back(residual, mix_gain, query_term)
-    gain_sums = jnp.stack(
-        [
-            jnp.sum(group_terms, 1) + jnp.sum(meta_terms, 1) + jnp.sum(query_terms, 1),
-            jnp.sum(attn_gain_terms, 1),
-            jnp.sum(mamba_gain_terms, 1),
-            jnp.sum(ffn_gain_terms, 1),
-        ],
-        axis=1,
-    )
+    normed_grad_low, mix_grad = lax.optimization_barrier(
+        (normed_grad_part.astype(bf16), mix_grad)
+    )
+    state_wide = dot(normed_group_t, mix_grad, 1, 0)
     vector_columns = -(-3 * channels // shard)
     vectors = jnp.pad(scan_sums[:3].reshape(-1), (0, vector_columns * shard - 3 * channels))
     vectors = jnp.tile(vectors.reshape(shard, vector_columns), (width // shard, 1))
-    each = query_width // tp
-    each_wide = -(-each // 128) * 128
-    room = ((0, each_wide - each), (0, 0))
-    small = [
-        meta_back,
-        dot(normed_group_t, keyval_columns_t[:, meta_count:], 1, 1)
-        + dot(meta_normed_t, keyval_columns_t[:, :meta_count], 1, 1),
+    tail = [
         dot(normed_group_t, select_grad_t, 1, 1),
-        gain_sums,
+        (jnp.sum(group_terms, 1) + jnp.sum(meta_terms, 1) + jnp.sum(query_terms, 1))[:, None],
+        jnp.sum(attn_gain_terms, 1, keepdims=True),
+        jnp.sum(mamba_gain_terms, 1, keepdims=True),
+        jnp.sum(ffn_gain_terms, 1, keepdims=True),
         vectors,
     ]
-    last_wide = jnp.concatenate(
-        [
-            dot(attn_grad_group_t, jnp.pad(attended_columns_t, room), 1, 1).astype(bf16),
-            dot(normed_group_t, jnp.pad(query_columns_t, room), 1, 1).astype(bf16),
-            jnp.concatenate([piece.astype(bf16) for piece in small], axis=1),
-        ],
-        axis=1,
-    )
-    last_wide, normed_grad_low = lax.optimization_barrier(
-        (last_wide, normed_grad_part.astype(bf16))
-    )
-    last_wide, state_columns = lax.optimization_barrier((last_wide, state_columns))
+    tail = jnp.concatenate([piece.astype(bf16) for piece in tail], axis=1)
+    tail = jnp.pad(tail, ((0, 0), (0, -tail.shape[1] % 128)))
+    last_wide = by_rows(
+        jnp.concatenate([by_rows(tail), by_rows(state_wide.astype(bf16))], axis=1)
+    )
+    last_wide, early_columns = lax.optimization_barrier((last_wide, early_columns))
     last_columns = scatter_rows(last_wide)
+    normed_grad_low, last_wide = lax.optimization_barrier((normed_grad_low, last_wide))
     normed_grad = line_sum(normed_grad_low, tp, 4) + query_term
-    late_out_part_t, normed_grad = lax.optimization_barrier((out_part_t, normed_grad))
-    layer_out_t = (mid + line_sum(late_out_part_t, tp, 5)).astype(bf16)
+    early_columns, ffn_columns, normed_grad = lax.optimization_barrier(
+        (early_columns, ffn_columns, normed_grad)
+    )
     residual_extra, _ = rms_back(residual, mix_gain, normed_grad)
     grad_tokens_t = (mid_grad + residual_extra).astype(bf16)
     grad_gate, grad_up, grad_ffn_output = [
         piece[:, :ff].astype(f32) for piece in cut(ffn_columns, [ff_wide] * 3)
     ]
     grad_ffn_input = jnp.stack([grad_gate, grad_up], axis=1)
-    grad_mamba_input = state_columns.astype(f32)
-    grad_mamba_output = out_columns.astype(f32)
-    (
-        grad_attn_output,
-        _,
-        grad_query,
-        _,
-        meta_shares,
-        grad_keyval,
-        select_shares,
-        gain_shares,
-        grad_vectors,
-    ) = cut(
+    attn_shares, _, grad_query, _, meta_shares, keyval_shares, grad_mamba_output = cut(
+        early_columns,
+        [
+            query_width,
+            -query_width % 128,
+            each,
+            -each % 128,
+            meta_count,
+            keyval_width,
+            channels,
+        ],
+    )
+
+    def to_device(values):
+        return jnp.swapaxes(values.reshape(shard, tp, values.shape[1] // tp), 0, 1)
+
+    shares = jnp.concatenate(
+        [to_device(attn_shares), to_device(keyval_shares), to_device(meta_shares)], axis=2
+    )
+    grad_attn_output, grad_keyval, grad_meta = cut(
+        permute_sums(shares, 0)[0], [each, keyval_width // tp, meta_count // tp]
+    )
+    last_columns, grad_attn_output, grad_keyval, grad_meta, grad_tokens_t = lax.optimization_barrier(
+        (last_columns, grad_attn_output, grad_keyval, grad_meta, grad_tokens_t)
+    )
+    select_shares, gain_shares, grad_vectors, _, grad_mamba_input = cut(
         last_columns,
         [
-            each,
-            each_wide - each,
-            each,
-            each_wide - each,
-            meta_count,
-            keyval_width // tp,
             2 * STATE,
             4,
             vector_columns,
+            -(2 * STATE + 4 + vector_columns) % 128,
+            3 * channels,
         ],
     )
-    grad_attn_output, grad_query, grad_keyval, grad_vectors = [
-        v.astype(f32) for v in (grad_attn_output, grad_query, grad_keyval, grad_vectors)
+    grad_mamba_output, grad_mamba_input, grad_query, grad_vectors = [
+        v.astype(f32) for v in (grad_mamba_output, grad_mamba_input, grad_query, grad_vectors)
     ]
-    meta_each, select_each = meta_count // tp, 2 * STATE // tp
-
-    def to_device(values):
-        return jnp.swapaxes(values.reshape(shard, tp, values.shape[1] // tp), 0, 1)
-
     shares = jnp.concatenate(
-        [
-            to_device(meta_shares),
-            to_device(select_shares),
-            jnp.broadcast_to(gain_shares[None], (tp, shard, 4)),
-        ],
-        axis=2,
-    )
-    grad_meta, grad_select, grad_gains = cut(
-        permute_sums(shares, 0)[0], [meta_each, select_each, 4]
-    )
+        [to_device(select_shares), jnp.broadcast_to(gain_shares[None], (tp, shard, 4))], axis=2
+    )
+    grad_select, grad_gains = cut(permute_sums(shares, 0)[0], [2 * STATE // tp, 4])
     grad_vectors = grad_vectors.reshape(-1)[: 3 * channels].reshape(3, channels)
     return (
         layer_out_t.T[None],

time: 930 us -> 794 us (0.85)
  waiting for transfers between devices: 99.1 us -> 41.8 us
  starting transfers between devices: 63 us -> 25.9 us
  Pallas kernels: 431 us -> 406 us
  local copies, waits for them, and re-layouts: 65.2 us -> 50.4 us
    pallas_call x2 -> x1, Pallas kernels: 110 us -> 57.6 us  [line_sum(): pl.pallas_call(functools.partial(line_sum_kernel, count), name='line_sum'...]
    ppermute x18 -> x12, waiting for transfers between devices: 66.7 us -> 15.2 us  [send(): lax.ppermute(values, 'tp', [(i, (i + by) % count) for i in range(count)])]
    ppermute x18 -> x12, starting transfers between devices: 56 us -> 18.5 us  [send(): lax.ppermute(values, 'tp', [(i, (i + by) % count) for i in range(count)])]
    pallas_call x1, Pallas kernels: 40.4 us -> 67.6 us  [backward_scan(): scan_call(functools.partial(backward_kernel, count), 'backward_scan', til...]
  transfers between devices with their start and end apart: 32 -> 25, of which waited for: 7 -> 5; matrix products, arithmetic and copies ran while one was open for 27% -> 28% of each run, Pallas kernels for 47% -> 52%
where the time goes in v2:
time: 794 us; the launch traced here: 784 us
  Pallas kernels  406 us (51%)
  matrix products  189 us (24%)
  other arithmetic  53.9 us (7%)
  local copies, waits for them, and re-layouts  50.4 us (6%)
  waiting for transfers between devices  41.8 us (5%)
  starting transfers between devices  25.9 us (3%)
  between operations  16.2 us (2%)
    dot_general x27, matrix products, dot(): lax.dot_general(left, right, (((left_dim,), (right_dim,)), ((), ())), pre...  189 us
    pallas_call x2, Pallas kernels, line_gather(): pl.pallas_call(functools.partial(line_gather_kernel, count), name='line_g...  114 us
    pallas_call x1, Pallas kernels, backward_scan(): scan_call(functools.partial(backward_kernel, count), 'backward_scan', til...  67.6 us
    pallas_call x1, Pallas kernels, attend_back(): pl.pallas_call(functools.partial(attend_back_kernel, group, count), name=...  61.8 us
    pallas_call x1, Pallas kernels, attend(): pl.pallas_call(functools.partial(attend_kernel, group, count), name='atte...  60.6 us
    pallas_call x1, Pallas kernels, line_sum(): pl.pallas_call(functools.partial(line_sum_kernel, count), name='line_sum'...  57.6 us
    reduce_scatter x1, waiting for transfers between devices, per_device(): lax.psum_scatter(ffn_grad_part_t, 'tp', scatter_dimension=1, tiled=True)  20.3 us
    pallas_call x1, Pallas kernels, forward_scan(): scan_call(forward_kernel, 'forward_scan', tiles, [mixed_s, select_s, sele...  18.9 us
  transfers between devices with their start and end apart: 25, of which 5 were waited for; matrix products, arithmetic and copies ran while one was open for 28% of the time, Pallas kernels for 52%

profile of v2, /device:TPU:0, one launch (start us, length us, event | category | flops | bytes accessed | tf_op | source)
XLA Modules:
  0.0 783.7 jit_solution(13424942150516334260)
XLA Ops:
  13.6 6.3 concatenate.60
  25.3 59.9 %line_gather.2 = bf16[1600,1024]{1,0:T(8,128)(2,1)} custom-call(bf16[1600,256]{1,0:T(8,128)(2,1)} %bitcast.112), custom_call_target="tpu_custom_call" | custom-call | tf_op jit(solution)/shard_map/line_gather/pallas_call | solution.py:544
  104.4 12.9 %fusion.11.mixed = f32[1024,2400]{1,0:T(8,128)} fusion(bf16[1600,2528]{1,0:T(8,128)(2,1)S(1)} %copy-done.46, bf16[1600,1024]{1,0:T(8,128)(2,1)S(1)} %copy-done.13, f32[1600]{0:T(1024)S(1)} %get-tuple-element.219, f32[1024]{0:T(1024)S(1)} %add_rsqrt_fusion), kind=kOutput, calls=%fused_computation.19 | convolution fusion | flops 7870873600 | bytes 20901888 | tf_op jit(solution)/shard_map/dot_general | solution.py:878
  117.3 12.3 %end_state.1 = f32[16,800]{1,0:T(8,128)S(1)} custom-call(f32[1024,2400]{1,0:T(8,128)} %fusion.11.mixed, bf16[32,1024]{1,0:T(8,128)(2,1)S(1)} %convolution_convert_fusion.10.select_t, f32[1024,8]{1,0:T(8,128)S(1)} %copy.135.aux, f32[8,1024]{1,0:T(8,128)S(1)} %stack.41.aux_t, f32[256,1]{1,0:T(8,128)S(1)} %fusion.125.alive_last, ...), custom_call_target="tpu_custom_call" | custom-call | flops 10000000000 | bytes 16777216 | tf_op jit(solution)/shard_map/end_state/pallas_call | solution.py:357
  134.1 18.9 %forward_scan.1 = (bf16[1024,800]{1,0:T(8,128)(2,1)S(1)}, bf16[4096,800]{1,0:T(8,128)(2,1)}, f32[16,800]{1,0:T(8,128)S(1)}) custom-call(f32[1024,2400]{1,0:T(8,128)} %fusion.11.mixed, bf16[1024,32]{1,0:T(8,128)(2,1)S(1)} %copy.134.select, bf16[32,1024]{1,0:T(8,128)(2,1)S(1)} %convolution_convert_fusion.10.select_t, f32[1024,8]{1,0:T(8,128)S(1)} %copy.135.aux, ...), custom_call_target="tpu_custom_call" | custom-call | flops 16000000000 | bytes 16777216 | tf_op jit(solution)/shard_map/forward_scan/pallas_call | solution.py:374
  153.0 7.5 fusion.35.source
  162.9 4.7 all-gather.6.cloned.1.call-done
  168.8 5.5 convolution_convert_fusion.9
  186.8 60.6 %attend.1 = (bf16[1600,256]{1,0:T(8,128)(2,1)}, f32[5,8,256]{2,1,0:T(8,128)}, f32[1600,256]{1,0:T(8,128)}) custom-call(bf16[1600,256]{1,0:T(8,128)(2,1)} %fusion.38.query_t, bf16[640,1408]{1,0:T(8,128)(2,1)} %pad_maximum_fusion.5.key_t.value_t, bf16[640,1408]{1,0:T(8,128)(2,1)} %pad_maximum_fusion.5.key_t.value_t, f32[1408,256]{1,0:T(8,128)} %concatenate.65.bias, ...), custom_call_target="tpu_custom_call" | custom-call | tf_op jit(solution)/shard_map/attend/pallas_call | solution.py:796
  249.6 4.9 multiply_reduce_fusion.4
  257.1 53.8 %line_gather.3 = bf16[1600,1024]{1,0:T(8,128)(2,1)} custom-call(bf16[1600,256]{1,0:T(8,128)(2,1)} %multiply_convert_fusion.4.source), custom_call_target="tpu_custom_call" | custom-call | tf_op jit(solution)/shard_map/line_gather/pallas_call | solution.py:544
  311.0 17.1 %fusion.4 = f32[2816,1024]{1,0:T(8,128)} fusion(bf16[1600,1024]{1,0:T(8,128)(2,1)} %line_gather.3, bf16[1600,4224]{1,0:T(8,128)(2,1)} %all-gather.14.cloned.1.call-done), kind=kOutput, calls=%fused_computation.10 | convolution fusion | flops 9227468800 | bytes 23822336 | tf_op jit(solution)/shard_map/dot_general | solution.py:878
  328.1 13.5 %multiply_convert_fusion.2 = (bf16[1408,1024]{1,0:T(8,128)(2,1)S(1)}, bf16[1408,1024]{1,0:T(8,128)(2,1)S(1)}, bf16[1408,1024]{1,0:T(8,128)(2,1)}) fusion(f32[2816,1024]{1,0:T(8,128)} %fusion.4, bf16[1600,256]{1,0:T(8,128)(2,1)S(1)} %copy-done.41, bf16[1600,256]{1,0:T(8,128)(2,1)S(1)} %copy-done.42, bf16[1600,256]{1,0:T(8,128)(2,1)S(1)} %copy-done.43, ...), kind=kOutput, calls=%fused_computation.28 | convolution fusion | flops 4649910272 | bytes 27967488 | tf_op jit(solution)/shard_map/dot_general | solution.py:878
  344.1 13.1 %fusion.27 = bf16[1600,1024]{1,0:T(8,128)(2,1)} fusion(bf16[1600,4224]{1,0:T(8,128)(2,1)} %all-gather.14.cloned.1.call-done, bf16[1408,1024]{1,0:T(8,128)(2,1)S(1)} %get-tuple-element.229, bf16[1408,1024]{1,0:T(8,128)(2,1)S(1)} %get-tuple-element.228), kind=kOutput, calls=%fused_computation.42 | convolution fusion | flops 9240641536 | bytes 18055168 | tf_op jit(solution)/shard_map/dot_general | solution.py:878
  357.2 9.9 %convolution_convert_fusion.2 = bf16[1600,1408]{1,0:T(8,128)(2,1)} fusion(bf16[1408,1024]{1,0:T(8,128)(2,1)} %get-tuple-element.230, bf16[1600,256]{1,0:T(8,128)(2,1)} %get-tuple-element.236, bf16[1600,256]{1,0:T(8,128)(2,1)} %get-tuple-element.237, bf16[1600,256]{1,0:T(8,128)(2,1)} %get-tuple-element.238, bf16[1600,256]{1,0:T(8,128)(2,1)} %get-tuple-element.235), kind=kOutput, calls=%fused_computation.14 | convolution fusion | flops 4629094400 | bytes 10665984 | tf_op jit(solution)/shard_map/dot_general | solution.py:878
  367.1 9.0 %fusion.24.source = bf16[1600,1024]{1,0:T(8,128)(2,1)} fusion(bf16[1408,1024]{1,0:T(8,128)(2,1)S(1)} %copy-done.59, bf16[1600,4224]{1,0:T(8,128)(2,1)} %all-gather.14.cloned.1.call-done), kind=kOutput, calls=%fused_computation.41 | convolution fusion | flops 4615372800 | bytes 10665984 | tf_op jit(solution)/shard_map/dot_general | solution.py:878
  376.1 13.0 %convolution_convert_fusion.1 = bf16[1600,2816]{1,0:T(8,128)(2,1)S(1)} fusion(bf16[1600,1024]{1,0:T(8,128)(2,1)} %line_gather.3, bf16[1408,1024]{1,0:T(8,128)(2,1)} %copy-done.61, bf16[1408,1024]{1,0:T(8,128)(2,1)} %copy-done.60), kind=kOutput, calls=%fused_computation.4 | convolution fusion | flops 9243508736 | bytes 18055168 | tf_op jit(solution)/shard_map/dot_general | solution.py:878
  389.1 8.2 %pad_maximum_fusion = bf16[1600,4224]{1,0:T(8,128)(2,1)} fusion(bf16[1600,1408]{1,0:T(8,128)(2,1)} %convolution_convert_fusion.2, bf16[1600,2816]{1,0:T(8,128)(2,1)S(1)} %convolution_convert_fusion.1), kind=kLoop, calls=%fused_computation.2 | loop fusion | flops 27033600 | bytes 27033600 | tf_op jit(solution)/shard_map/concatenate | solution.py:1106
  397.3 20.3 %reduce-scatter.7.cloned.1.call-done = bf16[1600,256]{1,0:T(8,128)(2,1)} async-done(((bf16[1600,1024]{1,0:T(8,128)(2,1)}), bf16[1600,256]{1,0:T(8,128)(2,1)}) %reduce-scatter.7.cloned.1.call-update) | async-done | bytes 819216 | tf_op jit(solution)/shard_map/reduce_scatter | solution.py:1103
  425.5 6.8 fusion.41.grad_t
  432.3 61.8 %attend_back.1 = (bf16[1600,256]{1,0:T(8,128)(2,1)}, bf16[2,320,1408]{2,1,0:T(8,128)(2,1)}, bf16[1600,1024]{1,0:T(8,128)(2,1)}) custom-call(bf16[1600,256]{1,0:T(8,128)(2,1)} %fusion.38.query_t, bf16[640,1408]{1,0:T(8,128)(2,1)} %pad_maximum_fusion.5.key_t.value_t, bf16[640,1408]{1,0:T(8,128)(2,1)} %pad_maximum_fusion.5.key_t.value_t, ...), custom_call_target="tpu_custom_call" | custom-call | tf_op jit(solution)/shard_map/attend_back/pallas_call | solution.py:835
  494.1 5.9 fusion.153.gated_grad
  500.1 13.4 %end_adjoint.1 = f32[16,800]{1,0:T(8,128)S(1)} custom-call(f32[1024,800]{1,0:T(8,128)S(1)} %fusion.153.gated_grad, f32[1024,2400]{1,0:T(8,128)} %fusion.11.mixed, bf16[32,1024]{1,0:T(8,128)(2,1)S(1)} %convolution_convert_fusion.10.select_t, f32[1024,8]{1,0:T(8,128)S(1)} %copy.135.aux, f32[8,1024]{1,0:T(8,128)S(1)} %stack.41.aux_t, ...), custom_call_target="tpu_custom_call" | custom-call | flops 10000000000 | bytes 16777216 | tf_op jit(solution)/shard_map/end_adjoint/pallas_call | solution.py:395
  522.7 8.9 %collective-permute-done.7 = bf16[400,256]{1,0:T(8,128)(2,1)S(1)} collective-permute-done((bf16[400,256]{1,0:T(8,128)(2,1)S(1)}, bf16[400,256]{1,0:T(8,128)(2,1)S(1)}, u32[]{:S(2)}, u32[]{:S(2)}) %collective-permute-start.7) | collective-permute-done | bytes 204832 | tf_op jit(solution)/shard_map/ppermute | solution.py:899
  545.7 4.9 fusion.30
  552.2 5.6 fusion.59
  557.8 67.6 %backward_scan.1 = (bf16[1024,2400]{1,0:T(8,128)(2,1)}, f32[1024,32]{1,0:T(8,128)S(1)}, f32[8,800]{1,0:T(8,128)S(1)}, f32[1600,256]{1,0:T(8,128)S(1)}) custom-call(f32[1024,800]{1,0:T(8,128)} %copy-done.8, f32[1024,2400]{1,0:T(8,128)} %fusion.11.mixed, bf16[1024,32]{1,0:T(8,128)(2,1)S(1)} %copy-done.7, ...), custom_call_target="tpu_custom_call" | custom-call | flops 35999997952 | bytes 16777216 | tf_op jit(solution)/shard_map/backward_scan/pallas_call | solution.py:415
  629.0 14.4 %fusion.9 = f32[1600,1024]{1,0:T(8,128)} fusion(bf16[1024,2400]{1,0:T(8,128)(2,1)} %get-tuple-element.120, bf16[1600,2528]{1,0:T(8,128)(2,1)} %all-gather.8.cloned.1.call-done), kind=kOutput, calls=%fused_computation.17 | convolution fusion | flops 7864320000 | bytes 19316736 | tf_op jit(solution)/shard_map/dot_general | solution.py:878
  643.5 7.0 fusion.148
  654.4 12.2 %convolution_convert_fusion = bf16[1600,2400]{1,0:T(8,128)(2,1)S(1)} fusion(bf16[1024,2400]{1,0:T(8,128)(2,1)} %get-tuple-element.120, bf16[1600,1024]{1,0:T(8,128)(2,1)} %line_gather.2, f32[1600]{0:T(1024)S(1)} %copy-done.45, f32[1024]{0:T(1024)S(1)} %copy-done.49), kind=kOutput, calls=%fused_computation.3 | convolution fusion | flops 7874713600 | bytes 15882496 | tf_op jit(solution)/shard_map/dot_general | solution.py:878
  670.3 57.6 %line_sum.1 = f32[1600,256]{1,0:T(8,128)S(1)} custom-call(bf16[1600,1024]{1,0:T(8,128)(2,1)S(1)} %get-tuple-element.125.source), custom_call_target="tpu_custom_call" | custom-call | tf_op jit(solution)/shard_map/line_sum/pallas_call | solution.py:674
  758.0 5.3 collective-permute-start.13
  (322 shorter events, 144.7 us)
Async XLA Ops:
  7.2 124.3 %copy-start = (bf16[200,5504]{1,0:T(8,128)(2,1)S(1)}, bf16[200,5504]{1,0:T(8,128)(2,1)}, u32[]{:S(2)}) copy-start(bf16[200,5504]{1,0:T(8,128)(2,1)} %param.37) | copy-start | bytes 6604804
  7.2 88.0 %all-gather.8.cloned.1.call-start = ((), (), s32[]{:S(2)}) async-start(), calls=%async_computation.5 | async-start | bytes 9216000 | tf_op jit(solution)/shard_map/all_gather | solution.py:884
  23.8 67.8 %copy-start.53 = (f32[800]{0:T(1024)S(1)}, f32[800]{0:T(1024)}, u32[]{:S(2)}) copy-start(f32[800]{0:T(1024)} %param.30) | copy-start | bytes 9604
  23.8 67.8 %copy-start.54 = (f32[800]{0:T(1024)S(1)}, f32[800]{0:T(1024)}, u32[]{:S(2)}) copy-start(f32[800]{0:T(1024)} %param.32) | copy-start | bytes 9604
  23.8 67.8 %copy-start.52 = (f32[800]{0:T(1024)S(1)}, f32[800]{0:T(1024)}, u32[]{:S(2)}) copy-start(f32[800]{0:T(1024)} %param.31) | copy-start | bytes 9604
  23.8 129.2 %all-gather.10.cloned.1.call-start = ((), (), s32[]{:S(2)}) async-start(), calls=%async_computation.6 | async-start | bytes 3225600 | tf_op jit(solution)/shard_map/all_gather | solution.py:884
  24.6 143.0 %all-gather.6.cloned.1.call-start = ((), (), s32[]{:S(2)}) async-start(), calls=%async_computation.4 | async-start | bytes 8755200 | tf_op jit(solution)/shard_map/all_gather | solution.py:884
  25.3 224.3 %all-gather.12.cloned.1.call-start = ((), (), s32[]{:S(2)}) async-start(), calls=%async_computation.7 | async-start | bytes 5990400 | tf_op jit(solution)/shard_map/all_gather | solution.py:884
  85.2 75.3 %collective-permute-start.4 = (bf16[1600,256]{1,0:T(8,128)(2,1)}, bf16[1600,256]{1,0:T(8,128)(2,1)}, u32[]{:S(2)}, u32[]{:S(2)}) collective-permute-start(bf16[1600,256]{1,0:T(8,128)(2,1)} %bitcast.4), channel_id=1, source_target_pairs={{0,3},{1,0},{2,1},{3,2},{4,7},{5,4},{6,5},{7,6},{8,11},{9,8},{10,9... | collective-permute-start | bytes 2457608 | tf_op jit(solution)/shard_map/ppermute | solution.py:899
  87.7 72.8 %collective-permute-start.3 = (bf16[1600,256]{1,0:T(8,128)(2,1)}, bf16[1600,256]{1,0:T(8,128)(2,1)}, u32[]{:S(2)}, u32[]{:S(2)}) collective-permute-start(bf16[1600,256]{1,0:T(8,128)(2,1)} %bitcast.4), channel_id=1, source_target_pairs={{0,2},{1,3},{2,0},{3,1},{4,6},{5,7},{6,4},{7,5},{8,10},{9,11},{10,... | collective-permute-start | bytes 2457608 | tf_op jit(solution)/shard_map/ppermute | solution.py:899
  87.7 72.8 %collective-permute-start.2 = (bf16[1600,256]{1,0:T(8,128)(2,1)}, bf16[1600,256]{1,0:T(8,128)(2,1)}, u32[]{:S(2)}, u32[]{:S(2)}) collective-permute-start(bf16[1600,256]{1,0:T(8,128)(2,1)} %bitcast.4), channel_id=1, source_target_pairs={{0,1},{1,2},{2,3},{3,0},{4,5},{5,6},{6,7},{7,4},{8,9},{9,10},{10,1... | collective-permute-start | bytes 2457608 | tf_op jit(solution)/shard_map/ppermute | solution.py:899
  88.4 222.6 %all-gather.14.cloned.1.call-start = ((), (), s32[]{:S(2)}) async-start(), calls=%async_computation.8 | async-start | bytes 15206400 | tf_op jit(solution)/shard_map/all_gather | solution.py:884
  95.1 73.7 %copy-start.48 = (f32[1024]{0:T(1024)}, f32[1024]{0:T(1024)S(1)}, u32[]{:S(2)}) copy-start(f32[1024]{0:T(1024)S(1)} %add_rsqrt_fusion) | copy-start | bytes 12292
  98.2 79.6 %copy-start.44 = (f32[1600]{0:T(1024)}, f32[1600]{0:T(1024)S(1)}, u32[]{:S(2)}) copy-start(f32[1600]{0:T(1024)S(1)} %get-tuple-element.219) | copy-start | bytes 19204
  129.7 4.5 collective-permute-start.1
  160.5 257.1 %reduce-scatter.7.cloned.1.call-start = ((), (), s32[]{:S(2)}) async-start(), calls=%async_computation.9 | async-start | bytes 4096000 | tf_op jit(solution)/shard_map/reduce_scatter | solution.py:1103
  174.3 10.3 %collective-permute-start = (bf16[640,1024]{1,0:T(8,128)(2,1)S(1)}, bf16[640,1024]{1,0:T(8,128)(2,1)S(1)}, u32[]{:S(2)}, u32[]{:S(2)}) collective-permute-start(bf16[640,1024]{1,0:T(8,128)(2,1)S(1)} %convolution_convert_fusion.9), channel_id=1, source_target_pairs={{0,4},{1,5},{2,6},{3,7},{8,12},{9,13},{10,14},{11,15},{16,20},{17,... | collective-permute-start | bytes 3932168 | tf_op jit(solution)/shard_map/ppermute | solution.py:1040
  255.7 164.2 %copy-start.11 = (f32[1600,256]{1,0:T(8,128)}, f32[1600,256]{1,0:T(8,128)S(1)}, u32[]{:S(2)}) copy-start(f32[1600,256]{1,0:T(8,128)S(1)} %get-tuple-element.225) | copy-start | bytes 4915204
  357.2 200.7 %reduce-scatter.13.cloned.1.call-start = ((), (), s32[]{:S(2)}) async-start(), calls=%async_computation.12 | async-start | bytes 15206400
  417.7 252.6 %reduce-scatter.9.cloned.1.call-start = ((), (), s32[]{:S(2)}) async-start(), calls=%async_computation.10 | async-start | bytes 13824000 | tf_op jit(solution)/shard_map/reduce_scatter | solution.py:893
  513.6 9.1 %collective-permute-start.8 = (bf16[400,256]{1,0:T(8,128)(2,1)S(1)}, bf16[400,256]{1,0:T(8,128)(2,1)S(1)}, u32[]{:S(2)}, u32[]{:S(2)}) collective-permute-start(bf16[400,256]{1,0:T(8,128)(2,1)S(1)} %get-tuple-element.251), channel_id=1, source_target_pairs={{0,3},{1,0},{2,1},{3,2},{4,7},{5,4},{6,5},{7,6},{8,11},{9,8},{10,9... | collective-permute-start | bytes 614408 | tf_op jit(solution)/shard_map/ppermute | solution.py:899
  515.5 16.0 %collective-permute-start.7 = (bf16[400,256]{1,0:T(8,128)(2,1)S(1)}, bf16[400,256]{1,0:T(8,128)(2,1)S(1)}, u32[]{:S(2)}, u32[]{:S(2)}) collective-permute-start(bf16[400,256]{1,0:T(8,128)(2,1)S(1)} %get-tuple-element.252), channel_id=1, source_target_pairs={{0,2},{1,3},{2,0},{3,1},{4,6},{5,7},{6,4},{7,5},{8,10},{9,11},{10,... | collective-permute-start | bytes 614408 | tf_op jit(solution)/shard_map/ppermute | solution.py:899
  515.5 16.0 %collective-permute-start.6 = (bf16[400,256]{1,0:T(8,128)(2,1)S(1)}, bf16[400,256]{1,0:T(8,128)(2,1)S(1)}, u32[]{:S(2)}, u32[]{:S(2)}) collective-permute-start(bf16[400,256]{1,0:T(8,128)(2,1)S(1)} %get-tuple-element.253), channel_id=1, source_target_pairs={{0,1},{1,2},{2,3},{3,0},{4,5},{5,6},{6,7},{7,4},{8,9},{9,10},{10,1... | collective-permute-start | bytes 614408 | tf_op jit(solution)/shard_map/ppermute | solution.py:899
  516.8 24.4 %collective-permute-start.9 = (bf16[640,1024]{1,0:T(8,128)(2,1)S(1)}, bf16[640,1024]{1,0:T(8,128)(2,1)S(1)}, u32[]{:S(2)}, u32[]{:S(2)}) collective-permute-start(bf16[640,1024]{1,0:T(8,128)(2,1)S(1)} %slice.223), channel_id=1, source_target_pairs={{4,0},{5,1},{6,2},{7,3},{12,8},{13,9},{14,10},{15,11},{20,16},{21,... | collective-permute-start | bytes 3932168 | tf_op jit(solution)/shard_map/ppermute | solution.py:1138
  550.7 202.7 %reduce-scatter.11.cloned.1.call-start = ((), (), s32[]{:S(2)}) async-start(), calls=%async_computation.11 | async-start | bytes 9216000 | tf_op jit(solution)/shard_map/reduce_scatter | solution.py:893
  550.7 7.1 collective-permute-start.5
  733.8 15.7 %collective-permute-start.10 = (bf16[1,200,592]{2,1,0:T(8,128)(2,1)S(1)}, bf16[1,200,592]{2,1,0:T(8,128)(2,1)S(1)}, u32[]{:S(2)}, u32[]{:S(2)}) collective-permute-start(bf16[1,200,592]{2,1,0:T(8,128)(2,1)S(1)} %get-tuple-element.244), channel_id=1, source_target_pairs={{0,2},{1,3},{2,0},{3,1},{4,6},{5,7},{6,4},{7,5},{8,10},{9,11},{10,... | collective-permute-start | bytes 710408 | tf_op jit(solution)/shard_map/ppermute | solution.py:899
  735.2 14.2 %collective-permute-start.12 = (bf16[1,200,592]{2,1,0:T(8,128)(2,1)S(1)}, bf16[1,200,592]{2,1,0:T(8,128)(2,1)S(1)}, u32[]{:S(2)}, u32[]{:S(2)}) collective-permute-start(bf16[1,200,592]{2,1,0:T(8,128)(2,1)S(1)} %get-tuple-element.245), channel_id=1, source_target_pairs={{0,3},{1,0},{2,1},{3,2},{4,7},{5,4},{6,5},{7,6},{8,11},{9,8},{10,9... | collective-permute-start | bytes 710408 | tf_op jit(solution)/shard_map/ppermute | solution.py:899
  737.3 14.9 %collective-permute-start.11 = (bf16[1,200,592]{2,1,0:T(8,128)(2,1)S(1)}, bf16[1,200,592]{2,1,0:T(8,128)(2,1)S(1)}, u32[]{:S(2)}, u32[]{:S(2)}) collective-permute-start(bf16[1,200,592]{2,1,0:T(8,128)(2,1)S(1)} %get-tuple-element.246), channel_id=1, source_target_pairs={{0,1},{1,2},{2,3},{3,0},{4,5},{5,6},{6,7},{7,4},{8,9},{9,10},{10,1... | collective-permute-start | bytes 710408 | tf_op jit(solution)/shard_map/ppermute | solution.py:899
  758.0 17.6 %collective-permute-start.13 = (bf16[1,200,12]{1,2,0:T(8,128)(2,1)S(1)}, bf16[1,200,12]{1,2,0:T(8,128)(2,1)S(1)}, u32[]{:S(2)}, u32[]{:S(2)}) collective-permute-start(bf16[1,200,12]{1,2,0:T(8,128)(2,1)S(1)} %get-tuple-element.257), channel_id=1, source_target_pairs={{0,2},{1,3},{2,0},{3,1},{4,6},{5,7},{6,4},{7,5},{8,10},{9,11},{10,... | collective-permute-start | bytes 14408 | tf_op jit(solution)/shard_map/ppermute | solution.py:899
  763.4 12.3 %collective-permute-start.14 = (bf16[1,200,12]{1,2,0:T(8,128)(2,1)S(1)}, bf16[1,200,12]{1,2,0:T(8,128)(2,1)S(1)}, u32[]{:S(2)}, u32[]{:S(2)}) collective-permute-start(bf16[1,200,12]{1,2,0:T(8,128)(2,1)S(1)} %get-tuple-element.258), channel_id=1, source_target_pairs={{0,1},{1,2},{2,3},{3,0},{4,5},{5,6},{6,7},{7,4},{8,9},{9,10},{10,1... | collective-permute-start | bytes 14408 | tf_op jit(solution)/shard_map/ppermute | solution.py:899
  763.7 12.0 %collective-permute-start.15 = (bf16[1,200,12]{1,2,0:T(8,128)(2,1)S(1)}, bf16[1,200,12]{1,2,0:T(8,128)(2,1)S(1)}, u32[]{:S(2)}, u32[]{:S(2)}) collective-permute-start(bf16[1,200,12]{1,2,0:T(8,128)(2,1)S(1)} %get-tuple-element.259), channel_id=1, source_target_pairs={{0,3},{1,0},{2,1},{3,2},{4,7},{5,4},{6,5},{7,6},{8,11},{9,8},{10,9... | collective-permute-start | bytes 14408 | tf_op jit(solution)/shard_map/ppermute | solution.py:899
  (59 other events, 561.4 us)
Sparse Core Ops, SparseCore 0:
  23.9 56.2 all-gather.7
  82.0 31.1 all-gather.9
  115.7 51.8 all-gather.5
  169.3 41.4 all-gather.11
  212.5 76.0 all-gather.13
  357.3 60.3 reduce-scatter.6
  421.2 98.3 reduce-scatter.12
  550.8 91.5 reduce-scatter.8
  670.4 68.8 reduce-scatter.10

commit v3 on v2

--- a/solution.py
+++ b/solution.py
@@ -13,6 +13,7 @@
 WIN = 1024
 SUB = 4
 TILE = 128
+HEAD = 128
 
 bf16 = jnp.bfloat16
 f32 = jnp.float32
@@ -45,16 +46,13 @@
     return jnp.maximum(v, 0.0) + jnp.log1p(jnp.exp(-jnp.abs(v)))
 
 
-def logistic(v):
-    return 1.0 / (1.0 + jnp.exp(-v))
-
-
 def group_mask(rows, columns, row_unit, column_unit):
     return iota((rows, columns), 0) // row_unit == iota((rows, columns), 1) // column_unit
 
 
-def sums_matrix():
+def scan_tables():
     rows = 2 * TILE + TILE // SUB
+    width = TILE // SUB * STATE
     row = iota((rows, TILE), 0)
     column = iota((rows, TILE), 1)
     token = row % TILE
@@ -62,54 +60,44 @@
     upto = (row < TILE) & same & (column <= token)
     after = (row >= TILE) & (row < 2 * TILE) & same & (column > token)
     whole = (row >= 2 * TILE) & (row - 2 * TILE == column // SUB)
-    return ones_where(upto | after | whole).astype(bf16)
+    places = iota((STATE, width), 0) == iota((STATE, width), 1) % STATE
+    tables = (upto | after | whole, group_mask(width, TILE, STATE, SUB), places)
+    sums, mask, places = [ones_where(table).astype(bf16) for table in tables]
+    return sums, mask, mask.T, places, places.T
 
 
 def part(mixed, k):
-    channels = mixed.shape[1] // 3
-    return mixed[:, k * channels : (k + 1) * channels]
-
-
-def decays(step_raw, bias_ref, rate_ref, alive_last_ref):
+    channels = (mixed.shape[1] - HEAD) // 3
+    return mixed[:, HEAD + k * channels : HEAD + (k + 1) * channels]
+
+
+def both_ways(mixed):
+    head = mixed[:, :HEAD]
+    return head.astype(bf16), head.T.astype(bf16)
+
+
+def decays(step_raw, bias_ref, rate_ref, alive_last_ref, sums_ref):
     raw = step_raw + bias_ref[...]
     step = softplus(raw)
     log_decay = -step * rate_ref[...]
-    sums = split_mm(sums_matrix(), log_decay)
+    sums = split_mm(sums_ref[...], log_decay)
     upto = jnp.exp(sums[:TILE])
     after = sums[TILE : 2 * TILE]
     block = jnp.exp(sums[2 * TILE :]) * alive_last_ref[...]
     return raw, step, log_decay, upto, after, block
 
 
-def in_blocks(select_t_ref, aux_t_ref):
-    width = TILE // SUB * STATE
-    tiled = jnp.concatenate([select_t_ref[:STATE, :].astype(f32) * aux_t_ref[1:2, :]] * (TILE // SUB), axis=0)
-    return jnp.where(group_mask(width, TILE, STATE, SUB), tiled, 0.0).astype(bf16)
-
-
-def out_blocks_t(select_t_ref, aux_t_ref):
-    width = TILE // SUB * STATE
-    tiled = jnp.concatenate([select_t_ref[STATE:, :].astype(f32) * aux_t_ref[0:1, :]] * (TILE // SUB), axis=0)
-    return jnp.where(group_mask(width, TILE, STATE, SUB), tiled, 0.0).astype(bf16)
-
-
-def spread(part, factor):
-    width = TILE // SUB * STATE
-    places = ones_where(iota((STATE, width), 0) == iota((STATE, width), 1) % STATE).astype(bf16)
-    wide = mm(part, places) * factor
-    return jnp.where(group_mask(TILE, width, SUB, STATE), wide, 0.0).astype(bf16)
-
-
-def fold(wide, factor):
-    width = TILE // SUB * STATE
-    places = ones_where(iota((width, STATE), 0) % STATE == iota((width, STATE), 1)).astype(bf16)
-    kept = jnp.where(group_mask(TILE, width, SUB, STATE), wide * factor, 0.0)
-    return split_left(kept, places)
-
-
-def split_left(a, b):
-    high = a.astype(bf16)
-    return mm(high, b) + mm((a - high.astype(f32)).astype(bf16), b)
+def in_blocks(values_t, factor_t, mask):
+    kept = values_t * factor_t.astype(bf16)
+    return jnp.concatenate([kept] * (TILE // SUB), axis=0) * mask[...]
+
+
+def spread(values, factor, mask_t, places):
+    return mm(values * factor.astype(bf16), places[...]).astype(bf16) * mask_t[...]
+
+
+def fold(wide, factor, mask_t, places_t):
+    return mm(wide.astype(bf16) * mask_t[...], places_t[...]) * factor
 
 
 def pairs(aux_ref, aux_t_ref, lower):
@@ -127,36 +115,68 @@
     return lax.fori_loop(0, TILE // SUB, one, state, unroll=8)
 
 
-def end_state_kernel(mixed, select_t, aux, aux_t, alive_last, bias, rate, end, state, local, block):
+def end_state_kernel(
+    mixed, aux, aux_t, alive_last, bias, rate, sums_table, mask, mask_t, places, places_t, end, state, local, block
+):
     @pl.when(pl.program_id(0) == 0)
     def _():
         state[...] = jnp.zeros_like(state)
 
-    raw, step, log_decay, upto, after, total = decays(part(mixed, 2), bias, rate, alive_last)
+    _, maps_t = both_ways(mixed)
+    raw, step, log_decay, upto, after, total = decays(
+        part(mixed, 2), bias, rate, alive_last, sums_table
+    )
     driven = (jnp.exp(after) * step * part(mixed, 0)).astype(bf16)
-    local[...] = mm(in_blocks(select_t, aux_t), driven)
+    local[...] = mm(in_blocks(maps_t[:STATE], aux_t[1:2, :], mask), driven)
     block[...] = total
     state[...] = run_states(state[...], local, block)
     end[...] = state[...]
 
 
-def forward_kernel(mixed, select, select_t, aux, aux_t, alive_last, bias, rate, skip, start, gated, states, end, state, local, block):
+def forward_kernel(
+    mixed,
+    aux,
+    aux_t,
+    alive_last,
+    bias,
+    rate,
+    sums_table,
+    mask,
+    mask_t,
+    places,
+    places_t,
+    skip,
+    start,
+    gated,
+    states,
+    end,
+    state,
+    local,
+    block,
+):
     @pl.when(pl.program_id(0) == 0)
     def _():
         state[...] = start[...]
 
-    raw, step, log_decay, upto, after, total = decays(part(mixed, 2), bias, rate, alive_last)
+    maps, maps_t = both_ways(mixed)
+    raw, step, log_decay, upto, after, total = decays(
+        part(mixed, 2), bias, rate, alive_last, sums_table
+    )
     x = part(mixed, 0)
     driven = (jnp.exp(after) * step * x).astype(bf16)
-    local[...] = mm(in_blocks(select_t, aux_t), driven)
+    local[...] = mm(in_blocks(maps_t[:STATE], aux_t[1:2, :], mask), driven)
     block[...] = total
     state[...] = run_states(state[...], local, block, states)
     end[...] = state[...]
-    out_part = select[:, STATE:]
-    cross = jnp.where(pairs(aux, aux_t, True), mm(out_part, select_t[:STATE, :]), 0.0).astype(bf16)
-    y = upto * mm(spread(out_part, aux[:, 0:1]), states[...]) + jnp.exp(-after) * mm(cross, driven) + skip[...] * x
+    out_part = maps[:, STATE : 2 * STATE]
+    cross = jnp.where(pairs(aux, aux_t, True), mm(out_part, maps_t[:STATE]), 0.0).astype(bf16)
+    y = (
+        upto * mm(spread(out_part, aux[:, 0:1], mask_t, places), states[...])
+        + jnp.exp(-after) * mm(cross, driven)
+        + skip[...] * x
+    )
     gates = part(mixed, 1)
-    gated[...] = (y * gates * logistic(gates)).astype(bf16)
+    gated[...] = (y * gates * lax.logistic(gates)).astype(bf16)
 
 
 def back_run(carry, local_ref, block_ref, keep, states=None, bound=None):
@@ -176,38 +196,86 @@
     return lax.fori_loop(0, count, one, carry, unroll=8)
 
 
-def end_adjoint_kernel(gated_grad, mixed, select_t, aux, aux_t, alive_last, bias, rate, end, state, local, block):
-    @pl.when(pl.program_id(0) == 0)
+def end_adjoint_kernel(
+    count,
+    gated_grad,
+    mixed,
+    aux,
+    aux_t,
+    alive_last,
+    bias,
+    rate,
+    sums_table,
+    mask,
+    mask_t,
+    places,
+    places_t,
+    source,
+    end,
+    total_out,
+    state,
+    local,
+    block,
+    own,
+    sent,
+    got,
+    loads,
+    send_sems,
+    recv_sems,
+):
+    tile, tiles = pl.program_id(0), pl.num_programs(0)
+    begin, step_line, finish = line_sum_steps(
+        count, source, own, sent, got, total_out, loads, send_sems, recv_sems
+    )
+
+    @pl.when(tile == 0)
     def _():
+        begin()
         state[...] = jnp.zeros_like(state)
 
-    raw, step, log_decay, upto, after, total = decays(part(mixed, 2), bias, rate, alive_last)
+    for k in range(1, count - 1):
+
+        @pl.when(tile == tiles * k // (count - 1))
+        def _():
+            step_line(k)
+
+    _, maps_t = both_ways(mixed)
+    raw, step, log_decay, upto, after, total = decays(
+        part(mixed, 2), bias, rate, alive_last, sums_table
+    )
     gates = part(mixed, 1)
-    dy = gated_grad[...] * gates * logistic(gates)
-    local[...] = mm(out_blocks_t(select_t, aux_t), (upto * dy).astype(bf16))
+    dy = gated_grad[...] * gates * lax.logistic(gates)
+    local[...] = mm(in_blocks(maps_t[STATE : 2 * STATE], aux_t[0:1, :], mask), (upto * dy).astype(bf16))
     block[...] = total
     state[...] = back_run((state[...], jnp.zeros((1, state.shape[1]), f32)), local, block, None)[0]
     end[...] = state[...]
+
+    @pl.when(tile == tiles - 1)
+    def _():
+        step_line(count - 1)
+        finish()
 
 
 def backward_kernel(
     count,
     gated_grad,
     mixed,
-    select,
-    select_t,
     states,
     aux,
     aux_t,
     alive_last,
     bias,
     rate,
+    sums_table,
+    mask,
+    mask_t,
+    places,
+    places_t,
     skip,
     start,
     final,
     source,
     mix_grad,
-    select_grad,
     sums,
     total_out,
     state,
@@ -235,78 +303,96 @@
         edge[...] = jnp.sum(start[...] * final[...], axis=0, keepdims=True)
         sums[...] = jnp.zeros_like(sums)
 
-    @pl.when(tile == tiles // 2)
-    def _():
-        step_line(1)
-
-    raw, step, log_decay, upto, after, total = decays(part(mixed, 2), bias, rate, alive_last)
+    for k in range(1, count - 1):
+
+        @pl.when(tile == tiles * k // (count - 1))
+        def _():
+            step_line(k)
+
+    maps, maps_t = both_ways(mixed)
+    raw, step, log_decay, upto, after, total = decays(
+        part(mixed, 2), bias, rate, alive_last, sums_table
+    )
     channels = state.shape[1]
     x = part(mixed, 0)
     decay_after = jnp.exp(after)
     grow = jnp.exp(-after)
     driven = (decay_after * step * x).astype(bf16)
-    in_part, out_part = select[:, :STATE], select[:, STATE:]
-    in_part_t, out_part_t = select_t[:STATE, :], select_t[STATE:, :]
+    in_part, out_part = maps[:, :STATE], maps[:, STATE : 2 * STATE]
+    in_part_t, out_part_t = maps_t[:STATE], maps_t[STATE : 2 * STATE]
     lower, upper = pairs(aux, aux_t, True), pairs(aux, aux_t, False)
     cross = jnp.where(lower, mm(out_part, in_part_t), 0.0).astype(bf16)
     cross_t = jnp.where(upper, mm(in_part, out_part_t), 0.0).astype(bf16)
-    y = upto * mm(spread(out_part, aux[:, 0:1]), states[...]) + grow * mm(cross, driven)
+    y = upto * mm(spread(out_part, aux[:, 0:1], mask_t, places), states[...]) + grow * mm(cross, driven)
     gates = part(mixed, 1)
-    sigma = logistic(gates)
+    sigma = lax.logistic(gates)
     grad = gated_grad[...]
     dy = grad * gates * sigma
-    mix_grad[:, channels : 2 * channels] = (grad * (y + skip[...] * x) * (sigma * (1.0 + gates * (1.0 - sigma)))).astype(bf16)
+    mix_grad[:, HEAD + channels : HEAD + 2 * channels] = (
+        grad * (y + skip[...] * x) * (sigma * (1.0 + gates * (1.0 - sigma)))
+    ).astype(bf16)
     dy_low = (upto * dy).astype(bf16)
     dy_grown = (grow * dy).astype(bf16)
-    local[...] = mm(out_blocks_t(select_t, aux_t), dy_low)
+    local[...] = mm(in_blocks(out_part_t, aux_t[0:1, :], mask), dy_low)
     block[...] = total
     new_state, new_edge = back_run((state[...], edge[...]), local, block, adjoint, states, bound)
     state[...] = new_state
     edge[...] = new_edge
-    du = decay_after * (mm(spread(in_part, aux[:, 1:2]), adjoint[...]) + mm(cross_t, dy_grown))
-    out_grad = fold(mm_nt(dy_low, states[...]), aux[:, 0:1])
-    in_grad = fold(mm_nt(driven, adjoint[...]), aux[:, 1:2])
-    cross_grad = jnp.where(lower, mm_nt(dy_grown, driven), 0.0)
-    cross_grad_t = jnp.where(upper, mm_nt(driven, dy_grown), 0.0)
-    out_grad = out_grad + split_left(cross_grad, in_part)
-    in_grad = in_grad + split_left(cross_grad_t, out_part)
-    select_grad[...] = jnp.concatenate([in_grad, out_grad], axis=1)
+    du = decay_after * (
+        mm(spread(in_part, aux[:, 1:2], mask_t, places), adjoint[...]) + mm(cross_t, dy_grown)
+    )
+    out_grad = fold(mm_nt(dy_low, states[...]), aux[:, 0:1], mask_t, places_t)
+    in_grad = fold(mm_nt(driven, adjoint[...]), aux[:, 1:2], mask_t, places_t)
+    cross_grad = jnp.where(lower, mm_nt(dy_grown, driven), 0.0).astype(bf16)
+    cross_grad_t = jnp.where(upper, mm_nt(driven, dy_grown), 0.0).astype(bf16)
+    out_grad = out_grad + mm(cross_grad, in_part)
+    in_grad = in_grad + mm(cross_grad_t, out_part)
+    mix_grad[:, :HEAD] = jnp.concatenate(
+        [in_grad, out_grad, jnp.zeros((TILE, HEAD - 2 * STATE), f32)], axis=1
+    ).astype(bf16)
     flow = dy * y - step * x * du
-    places = ones_where(group_mask(TILE, TILE // SUB, SUB, 1)) * aux[:, 1:2]
+    to_tokens = ones_where(group_mask(TILE, TILE // SUB, SUB, 1)) * aux[:, 1:2]
     decay_grad = aux[:, 3:4] * (
-        split_mm(ones_where(upper).astype(bf16), flow) + split_mm(places.astype(bf16), bound[...])
-    )
-    step_grad = (x * du - rate[...] * decay_grad) * logistic(raw)
-    mix_grad[:, :channels] = (skip[...] * dy + step * du).astype(bf16)
-    mix_grad[:, 2 * channels :] = step_grad.astype(bf16)
+        mm(ones_where(upper).astype(bf16), flow.astype(bf16))
+        + split_mm(to_tokens.astype(bf16), bound[...])
+    )
+    step_grad = (x * du - rate[...] * decay_grad) * lax.logistic(raw)
+    mix_grad[:, HEAD : HEAD + channels] = (skip[...] * dy + step * du).astype(bf16)
+    mix_grad[:, HEAD + 2 * channels :] = step_grad.astype(bf16)
     sums[0:1, :] += jnp.sum(step_grad, axis=0, keepdims=True)
     sums[1:2, :] += jnp.sum(decay_grad * log_decay, axis=0, keepdims=True)
     sums[2:3, :] += jnp.sum(dy * x, axis=0, keepdims=True)
 
     @pl.when(tile == tiles - 1)
     def _():
-        for k in range(2, count):
-            step_line(k)
+        step_line(count - 1)
         finish()
 
 
 def scan_specs(tokens, channels, back):
     tiles = tokens // TILE
-
-    def at(i):
-        return tiles - 1 - i if back else i
-
-    mixed = pl.BlockSpec((TILE, 3 * channels), lambda i: (at(i), 0))
+    at = (lambda i: tiles - 1 - i) if back else (lambda i: i)
+
+    def fixed(*shape):
+        return pl.BlockSpec(shape, lambda i: (0,) * len(shape))
+
+    width = TILE // SUB * STATE
+    mixed = pl.BlockSpec((TILE, HEAD + 3 * channels), lambda i: (at(i), 0))
     rows = pl.BlockSpec((TILE, channels), lambda i: (at(i), 0))
-    select = pl.BlockSpec((TILE, 2 * STATE), lambda i: (at(i), 0))
-    select_t = pl.BlockSpec((2 * STATE, TILE), lambda i: (0, at(i)))
-    states = pl.BlockSpec((TILE // SUB * STATE, channels), lambda i: (at(i), 0))
-    aux = pl.BlockSpec((TILE, 8), lambda i: (at(i), 0))
-    aux_t = pl.BlockSpec((8, TILE), lambda i: (0, at(i)))
-    last = pl.BlockSpec((TILE // SUB, 1), lambda i: (at(i), 0))
-    row = pl.BlockSpec((1, channels), lambda i: (0, 0))
-    state = pl.BlockSpec((STATE, channels), lambda i: (0, 0))
-    return tiles, mixed, rows, select, select_t, states, aux, aux_t, last, row, state
+    states = pl.BlockSpec((width, channels), lambda i: (at(i), 0))
+    side = [
+        pl.BlockSpec((TILE, 8), lambda i: (at(i), 0)),
+        pl.BlockSpec((8, TILE), lambda i: (0, at(i))),
+        pl.BlockSpec((TILE // SUB, 1), lambda i: (at(i), 0)),
+        fixed(1, channels),
+        fixed(1, channels),
+        fixed(2 * TILE + TILE // SUB, TILE),
+        fixed(width, TILE),
+        fixed(TILE, width),
+        fixed(STATE, width),
+        fixed(width, STATE),
+    ]
+    return tiles, mixed, rows, states, side, fixed(1, channels), fixed(STATE, channels)
 
 
 def scan_scratch(channels):
@@ -349,34 +435,30 @@
     return aux_t.T, aux_t, last
 
 
-def end_state(mixed, select_t, aux, bias, rate):
-    tokens, channels = mixed.shape[0], mixed.shape[1] // 3
-    tiles, mixed_s, rows, select_s, select_t_s, states_s, aux_s, aux_t_s, last_s, row, state = scan_specs(
-        tokens, channels, False
-    )
+def end_state(mixed, side):
+    tokens, channels = mixed.shape[0], (mixed.shape[1] - HEAD) // 3
+    tiles, mixed_s, rows, states, side_s, row, state = scan_specs(tokens, channels, False)
     return scan_call(
         end_state_kernel,
         "end_state",
         tiles,
-        [mixed_s, select_t_s, aux_s, aux_t_s, last_s, row, row],
+        [mixed_s, *side_s],
         state,
         jax.ShapeDtypeStruct((STATE, channels), f32),
         scan_scratch(channels),
         10**10,
-    )(mixed, select_t, *aux, bias, rate)
-
-
-def forward_scan(mixed, select, select_t, aux, bias, rate, skip, start):
-    tokens, channels = mixed.shape[0], mixed.shape[1] // 3
-    tiles, mixed_s, rows, select_s, select_t_s, states_s, aux_s, aux_t_s, last_s, row, state = scan_specs(
-        tokens, channels, False
-    )
+    )(mixed, *side)
+
+
+def forward_scan(mixed, side, skip, start):
+    tokens, channels = mixed.shape[0], (mixed.shape[1] - HEAD) // 3
+    tiles, mixed_s, rows, states, side_s, row, state = scan_specs(tokens, channels, False)
     return scan_call(
         forward_kernel,
         "forward_scan",
         tiles,
-        [mixed_s, select_s, select_t_s, aux_s, aux_t_s, last_s, row, row, row, state],
-        [rows, states_s, state],
+        [mixed_s, *side_s, row, state],
+        [rows, states, state],
         [
             jax.ShapeDtypeStruct((tokens, channels), bf16),
             jax.ShapeDtypeStruct((tokens // SUB * STATE, channels), bf16),
@@ -384,49 +466,54 @@
         ],
         scan_scratch(channels),
         16 * 10**9,
-    )(mixed, select, select_t, *aux, bias, rate, skip, start)
-
-
-def end_adjoint(gated_grad, mixed, select_t, aux, bias, rate):
-    tokens, channels = mixed.shape[0], mixed.shape[1] // 3
-    tiles, mixed_s, rows, select_s, select_t_s, states_s, aux_s, aux_t_s, last_s, row, state = scan_specs(
-        tokens, channels, True
-    )
+    )(mixed, *side, skip, start)
+
+
+def end_adjoint(gated_grad, mixed, side, source, count, collective):
+    height, each = source.shape[0], source.shape[1] // count
+    tokens, channels = mixed.shape[0], (mixed.shape[1] - HEAD) // 3
+    tiles, mixed_s, rows, states, side_s, row, state = scan_specs(tokens, channels, True)
     return scan_call(
-        end_adjoint_kernel,
+        functools.partial(end_adjoint_kernel, count),
         "end_adjoint",
         tiles,
-        [rows, mixed_s, select_t_s, aux_s, aux_t_s, last_s, row, row],
-        state,
-        jax.ShapeDtypeStruct((STATE, channels), f32),
-        scan_scratch(channels),
+        [rows, mixed_s, *side_s, pl.BlockSpec(memory_space=pl.ANY)],
+        [state, pl.BlockSpec((height, each), lambda i: (0, 0))],
+        [
+            jax.ShapeDtypeStruct((STATE, channels), f32),
+            jax.ShapeDtypeStruct((height, each), f32),
+        ],
+        scan_scratch(channels) + line_sum_scratch(count, height, each),
         10**10,
-    )(gated_grad, mixed, select_t, *aux, bias, rate)
-
-
-def backward_scan(
-    gated_grad, mixed, select, select_t, states, aux, bias, rate, skip, start, final, source, count, collective
-):
+        collective,
+    )(gated_grad, mixed, *side, source)
+
+
+def backward_scan(gated_grad, mixed, states, side, skip, start, final, source, count, collective):
     height, each = source.shape[0], source.shape[1] // count
-    tokens, channels = mixed.shape[0], mixed.shape[1] // 3
-    tiles, mixed_s, rows, select_s, select_t_s, states_s, aux_s, aux_t_s, last_s, row, state = scan_specs(
-        tokens, channels, True
-    )
+    tokens, channels = mixed.shape[0], (mixed.shape[1] - HEAD) // 3
+    tiles, mixed_s, rows, states_s, side_s, row, state = scan_specs(tokens, channels, True)
     return scan_call(
         functools.partial(backward_kernel, count),
         "backward_scan",
         tiles,
-        [rows, mixed_s, select_s, select_t_s, states_s, aux_s, aux_t_s, last_s, row, row, row, state, state]
-        + [pl.BlockSpec(memory_space=pl.ANY)],
+        [
+            rows,
+            mixed_s,
+            states_s,
+            *side_s,
+            row,
+            state,
+            state,
+            pl.BlockSpec(memory_space=pl.ANY),
+        ],
         [
             mixed_s,
-            select_s,
             pl.BlockSpec((8, channels), lambda i: (0, 0)),
             pl.BlockSpec((height, each), lambda i: (0, 0)),
         ],
         [
-            jax.ShapeDtypeStruct((tokens, 3 * channels), bf16),
-            jax.ShapeDtypeStruct((tokens, 2 * STATE), f32),
+            jax.ShapeDtypeStruct(mixed.shape, bf16),
             jax.ShapeDtypeStruct((8, channels), f32),
             jax.ShapeDtypeStruct((height, each), f32),
         ],
@@ -439,7 +526,7 @@
         + line_sum_scratch(count, height, each),
         36 * 10**9,
         collective,
-    )(gated_grad, mixed, select, select_t, states, *aux, bias, rate, skip, start, final, source)
+    )(gated_grad, mixed, states, *side, skip, start, final, source)
 
 
 MESH = pl.DeviceIdType.MESH
@@ -979,14 +1066,13 @@
     meta_count = meta_tokens.shape[1]
     window = WIN + rows
 
-    gains = jnp.stack([gain_mix, gain_attn, gain_mamba, gain_ffn], axis=1)
-    flat_input = mamba_input.reshape(shard, 3 * channels)
-    small = jnp.concatenate(
-        [mamba_select, gains, jnp.zeros((shard, 128 - 2 * STATE - 4), bf16)], axis=1
-    )
-    first = jnp.concatenate([small, flat_input], axis=1)
+    place_of = jnp.arange(HEAD, dtype=jnp.int32)[None]
+    head = jnp.pad(mamba_select, ((0, 0), (0, HEAD - 2 * STATE)))
+    for k, gain in enumerate((gain_mix, gain_attn, gain_mamba, gain_ffn)):
+        head = jnp.where(place_of == 2 * STATE + k, gain[:, None], head)
+    first = jnp.concatenate([head] + [mamba_input[:, k] for k in range(3)], axis=1)
     first, second_parts = lax.optimization_barrier(
-        (first, (key_value_weight, meta_tokens, query_weight))
+        (first, (key_value_weight, meta_tokens, query_weight, mamba_output))
     )
     second = jnp.concatenate(second_parts, axis=1)
     first, second, tokens_t = lax.optimization_barrier((first, second, tokens_t))
@@ -996,11 +1082,10 @@
     late_cotangent_t, tokens_group_t = lax.optimization_barrier((cotangent_t, tokens_group_t))
     cotangent_pieces = permute_gather(late_cotangent_t)
 
-    select_map, gain_columns, _, state_map = cut(
-        first, [2 * STATE, 4, 128 - 2 * STATE - 4, 3 * channels]
-    )
-    keyval_map, meta_full, query_map = cut(second, [keyval_width, meta_count, query_width])
-    state_out_map = gather_rows(mamba_output)
+    gain_columns = first[:, 2 * STATE : 2 * STATE + 4]
+    keyval_map, meta_full, query_map, state_out_map = cut(
+        second, [keyval_width, meta_count, query_width, channels]
+    )
     attn_map = gather_rows(attn_output)
     gain_columns = gain_columns.astype(f32)
     mix_gain, attn_gain, mamba_gain, ffn_gain = [gain_columns[:, k : k + 1] for k in range(4)]
@@ -1012,9 +1097,7 @@
     meta_rows = meta_full.astype(f32)
     meta_normed_t = rms_norm(meta_rows, mix_gain).astype(bf16)
 
-    mixed = dot(normed_group_t, state_map, 0, 0)
-    selects_t = dot(select_map, normed_group_t, 0, 0).astype(bf16)
-    selects = selects_t.T
+    mixed = dot(normed_group_t, first, 0, 0)
     seg_current = lax.dynamic_slice_in_dim(segments, ctx_index * span, span, 0)
     seg_earlier = lax.dynamic_slice_in_dim(segments, jnp.maximum(ctx_index - 1, 0) * span, span, 0)
     seg_before = jnp.where(
@@ -1022,16 +1105,19 @@
         lax.dynamic_index_in_dim(segments, jnp.maximum(ctx_index * span - 1, 0), 0, False),
         -1,
     )
-    aux = scan_aux(seg_current, seg_before)
-    bias_row = step_bias[None]
-    rate_row = jnp.exp(decay_log)[None]
+    side = (
+        *scan_aux(seg_current, seg_before),
+        step_bias[None],
+        jnp.exp(decay_log)[None],
+        *scan_tables(),
+    )
     skip_row = state_skip[None]
-    selects_t, late_up, late_down = lax.optimization_barrier((selects_t, ffn_input, ffn_output))
+    state_end = end_state(mixed, side)
+    state_end, late_up, late_down = lax.optimization_barrier((state_end, ffn_input, ffn_output))
     ffn_shards = [
         lax.dynamic_slice_in_dim(whole, tp_index * ff, ff, 1)
         for whole in (late_up[:, 0], late_up[:, 1], late_down)
     ]
-    state_end = end_state(mixed, selects_t, aux, bias_row, rate_row)
     state_start = lax.ppermute(state_end, "ctx", [(0, 1)])
 
     query_t = dot(query_map, normed_t, 0, 0).astype(bf16)
@@ -1039,9 +1125,7 @@
     meta_keyval_t = dot(keyval_map, meta_normed_t, 0, 0).astype(bf16)
     earlier_t = lax.ppermute(keyval_group_t, "ctx", [(0, 1)])
 
-    gated, states, state_final = forward_scan(
-        mixed, selects, selects_t, aux, bias_row, rate_row, skip_row, state_start
-    )
+    gated, states, state_final = forward_scan(mixed, side, skip_row, state_start)
     mamba_part_t = dot(state_out_map, gated, 1, 1).astype(bf16)
     third = jnp.concatenate(
         [jnp.pad(piece, ((0, 0), (0, ff_wide - ff))) for piece in ffn_shards], axis=1
@@ -1104,9 +1188,13 @@
     up_wide = dot(ffn_normed_group_t, gate_up_grad_t, 1, 1).astype(bf16)
     down_wide = dot(cotangent_group_t, hidden_t, 1, 1).astype(bf16)
     ffn_wide = jnp.concatenate([up_wide, down_wide], axis=1)
-    out_part_t = dot(down_map, hidden_t, 1, 0).astype(bf16)
-    ffn_normed_grad_t, ffn_wide, out_part_t = lax.optimization_barrier(
-        (ffn_normed_grad_t, ffn_wide, out_part_t)
+    fourth = width // 4 // 16 * 16
+    out_parts = [
+        dot(down_map[:fourth], hidden_t, 1, 0).astype(bf16),
+        dot(down_map[fourth:], hidden_t, 1, 0).astype(bf16),
+    ]
+    ffn_normed_grad_t, ffn_wide, out_parts = lax.optimization_barrier(
+        (ffn_normed_grad_t, ffn_wide, out_parts)
     )
     ffn_columns = scatter_rows(ffn_wide)
 
@@ -1140,14 +1228,11 @@
     keyval_part_t = current.astype(bf16)
     keyval_meta_t = keyval_grad_t[:, :meta_count]
     gated_grad = dot(mamba_grad_group_t, state_out_map, 0, 0)
-    adjoint_end = end_adjoint(gated_grad, mixed, selects_t, aux, bias_row, rate_row)
-    adjoint_end, late_attended_t, late_gated = lax.optimization_barrier(
-        (adjoint_end, attended_t, gated)
+    adjoint_end, out_head = end_adjoint(gated_grad, mixed, side, out_parts[0], tp, 6)
+    adjoint_end, late_attended_t, late_gated, query_pieces = lax.optimization_barrier(
+        (adjoint_end, attended_t, gated, query_pieces)
     )
     adjoint_start = lax.ppermute(adjoint_end, "ctx", [(1, 0)])
-    late_attended_t, late_gated, query_pieces = lax.optimization_barrier(
-        (late_attended_t, late_gated, query_pieces)
-    )
     meta_back, meta_terms = rms_back(meta_rows, mix_gain, dot(keyval_map, keyval_meta_t, 1, 0))
     query_columns_t = in_order(query_pieces)
     each = query_width // tp
@@ -1173,52 +1258,39 @@
     adjoint_start, early_wide, ffn_columns = lax.optimization_barrier(
         (adjoint_start, early_wide, ffn_columns)
     )
-    mix_grad, select_grad, scan_sums, out_total = backward_scan(
+    mix_grad, scan_sums, out_rest = backward_scan(
         gated_grad,
         mixed,
-        selects,
-        selects_t,
         states,
-        aux,
-        bias_row,
-        rate_row,
+        side,
         skip_row,
         adjoint_start,
         state_final,
-        out_part_t,
+        out_parts[1],
         tp,
         5,
     )
-    layer_out_t = (mid + out_total).astype(bf16)
-    select_grad_t = select_grad.T.astype(bf16)
+    layer_out_t = (mid + jnp.concatenate([out_head, out_rest], axis=0)).astype(bf16)
     query_term = dot(query_map, query_grad_t, 1, 0)
-    normed_grad_part = (
-        dot(state_map, mix_grad, 1, 1)
-        + dot(select_map, select_grad_t, 1, 0)
-        + dot(keyval_map, keyval_part_t, 1, 0)
-    )
+    normed_grad_part = dot(first, mix_grad, 1, 1) + dot(keyval_map, keyval_part_t, 1, 0)
     _, group_terms = rms_back(residual_group, mix_gain, normed_grad_part)
     _, query_terms = rms_back(residual, mix_gain, query_term)
     normed_grad_low, mix_grad = lax.optimization_barrier(
         (normed_grad_part.astype(bf16), mix_grad)
     )
-    state_wide = dot(normed_group_t, mix_grad, 1, 0)
     vector_columns = -(-3 * channels // shard)
     vectors = jnp.pad(scan_sums[:3].reshape(-1), (0, vector_columns * shard - 3 * channels))
     vectors = jnp.tile(vectors.reshape(shard, vector_columns), (width // shard, 1))
     tail = [
-        dot(normed_group_t, select_grad_t, 1, 1),
         (jnp.sum(group_terms, 1) + jnp.sum(meta_terms, 1) + jnp.sum(query_terms, 1))[:, None],
         jnp.sum(attn_gain_terms, 1, keepdims=True),
         jnp.sum(mamba_gain_terms, 1, keepdims=True),
         jnp.sum(ffn_gain_terms, 1, keepdims=True),
         vectors,
     ]
-    tail = jnp.concatenate([piece.astype(bf16) for piece in tail], axis=1)
-    tail = jnp.pad(tail, ((0, 0), (0, -tail.shape[1] % 128)))
-    last_wide = by_rows(
-        jnp.concatenate([by_rows(tail), by_rows(state_wide.astype(bf16))], axis=1)
-    )
+    tail = jnp.concatenate(tail, axis=1)
+    tail = jnp.pad(tail, ((0, 0), (2 * STATE, first.shape[1] - 2 * STATE - tail.shape[1])))
+    last_wide = by_rows((dot(normed_group_t, mix_grad, 1, 0) + tail).astype(bf16))
     last_wide, early_columns = lax.optimization_barrier((last_wide, early_columns))
     last_columns = scatter_rows(last_wide)
     normed_grad_low, last_wide = lax.optimization_barrier((normed_grad_low, last_wide))
@@ -1254,26 +1326,21 @@
     grad_attn_output, grad_keyval, grad_meta = cut(
         permute_sums(shares, 0)[0], [each, keyval_width // tp, meta_count // tp]
     )
-    last_columns, grad_attn_output, grad_keyval, grad_meta, grad_tokens_t = lax.optimization_barrier(
-        (last_columns, grad_attn_output, grad_keyval, grad_meta, grad_tokens_t)
-    )
-    select_shares, gain_shares, grad_vectors, _, grad_mamba_input = cut(
-        last_columns,
-        [
-            2 * STATE,
-            4,
-            vector_columns,
-            -(2 * STATE + 4 + vector_columns) % 128,
-            3 * channels,
-        ],
-    )
-    grad_mamba_output, grad_mamba_input, grad_query, grad_vectors = [
-        v.astype(f32) for v in (grad_mamba_output, grad_mamba_input, grad_query, grad_vectors)
-    ]
+    select_shares, gain_shares, grad_vectors = cut(last_columns, [2 * STATE, 4, vector_columns])
     shares = jnp.concatenate(
         [to_device(select_shares), jnp.broadcast_to(gain_shares[None], (tp, shard, 4))], axis=2
     )
     grad_select, grad_gains = cut(permute_sums(shares, 0)[0], [2 * STATE // tp, 4])
+    grad_mamba_input = jnp.stack(
+        [
+            last_columns[:, HEAD + k * channels : HEAD + (k + 1) * channels].astype(f32)
+            for k in range(3)
+        ],
+        axis=1,
+    )
+    grad_mamba_output, grad_query, grad_vectors = [
+        v.astype(f32) for v in (grad_mamba_output, grad_query, grad_vectors)
+    ]
     grad_vectors = grad_vectors.reshape(-1)[: 3 * channels].reshape(3, channels)
     return (
         layer_out_t.T[None],
@@ -1284,7 +1351,7 @@
         grad_keyval,
         grad_attn_output,
         grad_gains[:, 1],
-        grad_mamba_input.reshape(shard, 3, channels),
+        grad_mamba_input,
         grad_select,
         grad_vectors[0],
         grad_vectors[1],

time: 794 us -> 763 us (0.961)
  waiting for transfers between devices: 41.8 us -> 27.8 us
  local copies, waits for them, and re-layouts: 50.4 us -> 41.9 us
  Pallas kernels: 406 us -> 398 us
    pallas_call x1, Pallas kernels: 67.6 us -> 51.4 us  [backward_scan(): scan_call(functools.partial(backward_kernel, count), 'backward_scan', til...]
    ppermute x12, waiting for transfers between devices: 15.2 us -> 5.38 us  [send(): lax.ppermute(values, 'tp', [(i, (i + by) % count) for i in range(count)])]
    pallas_call x3, Pallas kernels: 44.6 us -> 53.2 us  [the longest x1 22.2 us: end_adjoint(): scan_call(functools.partial(end_adjoint_kernel, count), 'end_adjoint', ti...]
    unnamed x129 -> x127, local copies, waits for them, and re-layouts: 17.1 us -> 13.1 us
    dot_general x27 -> x25, matrix products: 189 us -> 193 us  [dot(): lax.dot_general(left, right, (((left_dim,), (right_dim,)), ((), ())), pre...]
  transfers between devices with their start and end apart: 25 -> 24, of which waited for: 5 -> 3; matrix products, arithmetic and copies ran while one was open for 28% -> 29% of each run, Pallas kernels for 52% -> 53%
where the time goes in v3:
time: 763 us; the launch traced here: 754 us
  Pallas kernels  398 us (52%)
  matrix products  193 us (25%)
  other arithmetic  51.1 us (7%)
  local copies, waits for them, and re-layouts  41.9 us (5%)
  waiting for transfers between devices  27.8 us (4%)
  starting transfers between devices  25.5 us (3%)
  between operations  16.5 us (2%)
    dot_general x25, matrix products, dot(): lax.dot_general(left, right, (((left_dim,), (right_dim,)), ((), ())), pre...  193 us
    pallas_call x2, Pallas kernels, line_gather(): pl.pallas_call(functools.partial(line_gather_kernel, count), name='line_g...  114 us
    pallas_call x1, Pallas kernels, attend_back(): pl.pallas_call(functools.partial(attend_back_kernel, group, count), name=...  62.7 us
    pallas_call x1, Pallas kernels, attend(): pl.pallas_call(functools.partial(attend_kernel, group, count), name='atte...  59.2 us
    pallas_call x1, Pallas kernels, line_sum(): pl.pallas_call(functools.partial(line_sum_kernel, count), name='line_sum'...  57.3 us
    pallas_call x1, Pallas kernels, backward_scan(): scan_call(functools.partial(backward_kernel, count), 'backward_scan', til...  51.4 us
    pallas_call x1, Pallas kernels, end_adjoint(): scan_call(functools.partial(end_adjoint_kernel, count), 'end_adjoint', ti...  22.2 us
    reduce_scatter x1, waiting for transfers between devices, per_device(): lax.psum_scatter(ffn_grad_part_t, 'tp', scatter_dimension=1, tiled=True)  21.5 us
  transfers between devices with their start and end apart: 24, of which 3 were waited for; matrix products, arithmetic and copies ran while one was open for 29% of the time, Pallas kernels for 53%

profile of v3, /device:TPU:0, one launch (start us, length us, event | category | flops | bytes accessed | tf_op | source)
XLA Modules:
  0.0 753.7 jit_solution(1014805555747660272)
XLA Ops:
  16.2 59.9 %line_gather.2 = bf16[1600,1024]{1,0:T(8,128)(2,1)} custom-call(bf16[1600,256]{1,0:T(8,128)(2,1)} %bitcast.120), custom_call_target="tpu_custom_call" | custom-call | tf_op jit(solution)/shard_map/line_gather/pallas_call | solution.py:631
  91.8 15.8 %fusion.155.mixed = f32[1024,2528]{1,0:T(8,128)} fusion(bf16[1600,2528]{1,0:T(8,128)(2,1)} %all-gather.7.cloned.1.call-done, bf16[1600,1024]{1,0:T(8,128)(2,1)S(1)} %copy-done.24, f32[1600]{0:T(1024)S(1)} %get-tuple-element.211, f32[1024]{0:T(1024)S(1)} %add_rsqrt_fusion), kind=kOutput, calls=%fused_computation.313 | convolution fusion | flops 8290304000 | bytes 21731584 | tf_op jit(solution)/shard_map/dot_general | solution.py:965
  107.5 11.8 %end_state.1 = f32[16,800]{1,0:T(8,128)S(1)} custom-call(f32[1024,2528]{1,0:T(8,128)} %fusion.155.mixed, f32[1024,8]{1,0:T(8,128)S(1)} %copy.119.aux, f32[8,1024]{1,0:T(8,128)S(1)} %stack.43.aux_t, f32[256,1]{1,0:T(8,128)S(1)} %fusion.126.alive_last, f32[1,800]{1,0:T(1,128)S(1)} %broadcast_in_dim.168.bias, f32[1,800]{1,0:T(1,128)S(1)} %broadcast_in_dim.169.rate, ...), custom_call_target="tpu_custom_call" | custom-call | flops 10000000000 | bytes 16777216 | tf_op jit(solution)/shard_map/end_state/pallas_call | solution.py:441
  123.7 19.2 %forward_scan.1 = (bf16[1024,800]{1,0:T(8,128)(2,1)S(1)}, bf16[4096,800]{1,0:T(8,128)(2,1)}, f32[16,800]{1,0:T(8,128)S(1)}) custom-call(f32[1024,2528]{1,0:T(8,128)} %fusion.155.mixed, f32[1024,8]{1,0:T(8,128)S(1)} %copy.119.aux, f32[8,1024]{1,0:T(8,128)S(1)} %stack.43.aux_t, f32[256,1]{1,0:T(8,128)S(1)} %fusion.126.alive_last, ...), custom_call_target="tpu_custom_call" | custom-call | flops 16000000000 | bytes 16777216 | tf_op jit(solution)/shard_map/forward_scan/pallas_call | solution.py:456
  142.8 7.7 %convolution_convert_fusion.4.source = bf16[1600,1024]{1,0:T(8,128)(2,1)} fusion(bf16[1024,800]{1,0:T(8,128)(2,1)S(1)} %get-tuple-element.109, bf16[1600,3168]{1,0:T(8,128)(2,1)} %all-gather.5.cloned.1.call-done), kind=kOutput, calls=%fused_computation.34 | convolution fusion | flops 2623078400 | bytes 7782400 | tf_op jit(solution)/shard_map/dot_general | solution.py:965
  153.3 4.5 convolution_convert_fusion.8
  169.6 59.2 %attend.1 = (bf16[1600,256]{1,0:T(8,128)(2,1)}, f32[5,8,256]{2,1,0:T(8,128)}, f32[1600,256]{1,0:T(8,128)}) custom-call(bf16[1600,256]{1,0:T(8,128)(2,1)} %fusion.27.query_t, bf16[640,1408]{1,0:T(8,128)(2,1)} %pad_maximum_fusion.5.key_t.value_t, bf16[640,1408]{1,0:T(8,128)(2,1)} %pad_maximum_fusion.5.key_t.value_t, f32[1408,256]{1,0:T(8,128)} %concatenate.65.bias, ...), custom_call_target="tpu_custom_call" | custom-call | tf_op jit(solution)/shard_map/attend/pallas_call | solution.py:883
  230.7 4.6 multiply_reduce_fusion.4
  237.7 54.2 %line_gather.3 = bf16[1600,1024]{1,0:T(8,128)(2,1)} custom-call(bf16[1600,256]{1,0:T(8,128)(2,1)} %multiply_convert_fusion.4.source), custom_call_target="tpu_custom_call" | custom-call | tf_op jit(solution)/shard_map/line_gather/pallas_call | solution.py:631
  292.0 17.3 %fusion.2 = f32[2816,1024]{1,0:T(8,128)} fusion(bf16[1600,1024]{1,0:T(8,128)(2,1)} %line_gather.3, bf16[1600,4224]{1,0:T(8,128)(2,1)} %all-gather.11.cloned.1.call-done), kind=kOutput, calls=%fused_computation.7 | convolution fusion | flops 9227468800 | bytes 23822336 | tf_op jit(solution)/shard_map/dot_general | solution.py:965
  309.3 13.5 %multiply_convert_fusion.2 = (bf16[1408,1024]{1,0:T(8,128)(2,1)S(1)}, bf16[1408,1024]{1,0:T(8,128)(2,1)S(1)}, bf16[1408,1024]{1,0:T(8,128)(2,1)}) fusion(f32[2816,1024]{1,0:T(8,128)} %fusion.2, bf16[1600,256]{1,0:T(8,128)(2,1)S(1)} %copy-done.39, bf16[1600,256]{1,0:T(8,128)(2,1)S(1)} %copy-done.41, bf16[1600,256]{1,0:T(8,128)(2,1)S(1)} %copy-done.43, ...), kind=kOutput, calls=%fused_computation.20 | convolution fusion | flops 4649910272 | bytes 27967488 | tf_op jit(solution)/shard_map/dot_general | solution.py:965
  325.4 13.2 %fusion.16 = bf16[1600,1024]{1,0:T(8,128)(2,1)} fusion(bf16[1600,4224]{1,0:T(8,128)(2,1)} %all-gather.11.cloned.1.call-done, bf16[1408,1024]{1,0:T(8,128)(2,1)S(1)} %get-tuple-element.221, bf16[1408,1024]{1,0:T(8,128)(2,1)S(1)} %get-tuple-element.220), kind=kOutput, calls=%fused_computation.32 | convolution fusion | flops 9240641536 | bytes 18055168 | tf_op jit(solution)/shard_map/dot_general | solution.py:965
  342.7 8.0 %convolution_convert_fusion.3.source = bf16[1200,1024]{1,0:T(8,128)(2,1)} fusion(bf16[1408,1024]{1,0:T(8,128)(2,1)S(1)} %copy-done.57, bf16[1600,4224]{1,0:T(8,128)(2,1)} %all-gather.11.cloned.1.call-done), kind=kOutput, calls=%fused_computation.33 | convolution fusion | flops 3461529600 | bytes 8720384 | tf_op jit(solution)/shard_map/dot_general | solution.py:965
  350.7 6.9 convolution_convert_fusion.1
  357.6 12.9 %convolution_convert_fusion = bf16[1600,2816]{1,0:T(8,128)(2,1)S(1)} fusion(bf16[1600,1024]{1,0:T(8,128)(2,1)} %line_gather.3, bf16[1408,1024]{1,0:T(8,128)(2,1)} %copy-done.59, bf16[1408,1024]{1,0:T(8,128)(2,1)} %copy-done.58), kind=kOutput, calls=%fused_computation.2 | convolution fusion | flops 9243508736 | bytes 18055168 | tf_op jit(solution)/shard_map/dot_general | solution.py:965
  370.6 8.3 %pad_maximum_fusion = bf16[1600,4224]{1,0:T(8,128)(2,1)} fusion(bf16[1600,1408]{1,0:T(8,128)(2,1)} %convolution_convert_fusion.1, bf16[1600,2816]{1,0:T(8,128)(2,1)S(1)} %convolution_convert_fusion), kind=kLoop, calls=%fused_computation.1 | loop fusion | flops 27033600 | bytes 27033600 | tf_op jit(solution)/shard_map/concatenate | solution.py:1190
  378.9 21.5 %reduce-scatter.7.cloned.1.call-done = bf16[1600,256]{1,0:T(8,128)(2,1)} async-done(((bf16[1600,1024]{1,0:T(8,128)(2,1)}), bf16[1600,256]{1,0:T(8,128)(2,1)}) %reduce-scatter.7.cloned.1.call-update) | async-done | bytes 819216 | tf_op jit(solution)/shard_map/reduce_scatter | solution.py:1187
  403.8 4.0 multiply_reduce_fusion
  409.6 5.8 fusion.33.grad_t
  415.5 62.7 %attend_back.1 = (bf16[1600,256]{1,0:T(8,128)(2,1)}, bf16[2,320,1408]{2,1,0:T(8,128)(2,1)}, bf16[1600,1024]{1,0:T(8,128)(2,1)}) custom-call(bf16[1600,256]{1,0:T(8,128)(2,1)} %fusion.27.query_t, bf16[640,1408]{1,0:T(8,128)(2,1)} %pad_maximum_fusion.5.key_t.value_t, bf16[640,1408]{1,0:T(8,128)(2,1)} %pad_maximum_fusion.5.key_t.value_t, ...), custom_call_target="tpu_custom_call" | custom-call | tf_op jit(solution)/shard_map/attend_back/pallas_call | solution.py:922
  490.0 6.1 fusion.30.gated_grad
  496.2 22.2 %end_adjoint.1 = (f32[16,800]{1,0:T(8,128)S(1)}, f32[400,256]{1,0:T(8,128)S(1)}) custom-call(f32[1024,800]{1,0:T(8,128)S(1)} %fusion.30.gated_grad, f32[1024,2528]{1,0:T(8,128)} %fusion.155.mixed, f32[1024,8]{1,0:T(8,128)S(1)} %copy.119.aux, f32[8,1024]{1,0:T(8,128)S(1)} %stack.43.aux_t, f32[256,1]{1,0:T(8,128)S(1)} %fusion.126.alive_last, ...), custom_call_target="tpu_custom_call" | custom-call | flops 10000000000 | bytes 16777216 | tf_op jit(solution)/shard_map/end_adjoint/pallas_call | solution.py:476
  518.5 4.2 fusion.6
  529.1 6.0 fusion.25
  535.1 4.9 fusion.19
  541.4 5.5 fusion.51
  548.2 9.5 %fusion.67 = f32[1600,1024]{1,0:T(8,128)} fusion(bf16[1600,3168]{1,0:T(8,128)(2,1)} %all-gather.5.cloned.1.call-done, bf16[640,1024]{1,0:T(8,128)(2,1)} %collective-permute-done.9, bf16[640,2048]{1,0:T(8,128)(2,1)S(1)} %copy-done.28), kind=kOutput, calls=%fused_computation.112 | convolution fusion | flops 2099773440 | bytes 11223040 | tf_op jit(solution)/shard_map/dot_general | solution.py:965
  559.5 51.4 %backward_scan.1 = (bf16[1024,2528]{1,0:T(8,128)(2,1)}, f32[8,800]{1,0:T(8,128)S(1)}, f32[1200,256]{1,0:T(8,128)S(1)}) custom-call(f32[1024,800]{1,0:T(8,128)} %copy-done.6, f32[1024,2528]{1,0:T(8,128)} %fusion.155.mixed, bf16[4096,800]{1,0:T(8,128)(2,1)} %get-tuple-element.99.states, f32[1024,8]{1,0:T(8,128)S(1)} %copy.119.aux, f32[8,1024]{1,0:T(8,128)S(1)} %stack.43.aux_t, ...), custom_call_target="tpu_custom_call" | custom-call | flops 35999997952 | bytes 16777216 | tf_op jit(solution)/shard_map/backward_scan/pallas_call | solution.py:496
  612.0 15.8 %fusion.159 = (bf16[1600,1024]{1,0:T(8,128)(2,1)S(1)}, f32[1600]{0:T(1024)S(1)}) fusion(f32[1024]{0:T(1024)S(1)} %copy-done.52, bf16[1600,1024]{1,0:T(8,128)(2,1)} %line_gather.2, f32[1600,1024]{1,0:T(8,128)} %fusion.67, bf16[1600,2528]{1,0:T(8,128)(2,1)} %all-gather.7.cloned.1.call-done, bf16[1024,2528]{1,0:T(8,128)(2,1)} %get-tuple-element.116), kind=kOutput, calls=%fused_computation.314 | convolution fusion | flops 8293579264 | bytes 26384640 | tf_op jit(solution)/shard_map/dot_general | solution.py:965
  629.6 14.5 %add_convert_fusion = bf16[1600,2528]{1,0:T(8,128)(2,1)} fusion(f32[1600,16]{1,0:T(8,128)} %copy.129, bf16[1024,2528]{1,0:T(8,128)(2,1)} %get-tuple-element.116, bf16[1600,1024]{1,0:T(8,128)(2,1)} %line_gather.2, f32[1600]{0:T(1024)S(1)} %get-tuple-element.211, f32[1024]{0:T(1024)S(1)} %copy-done.52), kind=kOutput, calls=%fused_computation | convolution fusion | flops 8298393600 | bytes 16656640 | tf_op jit(solution)/shard_map/dot_general | solution.py:965
  644.1 57.3 %line_sum.1 = f32[1600,256]{1,0:T(8,128)S(1)} custom-call(bf16[1600,1024]{1,0:T(8,128)(2,1)S(1)} %get-tuple-element.122.source), custom_call_target="tpu_custom_call" | custom-call | tf_op jit(solution)/shard_map/line_sum/pallas_call | solution.py:761
  731.4 5.6 collective-permute-start.13
  (328 shorter events, 123.1 us)
Async XLA Ops:
  7.2 114.1 %copy-start = (bf16[200,5504]{1,0:T(8,128)(2,1)S(1)}, bf16[200,5504]{1,0:T(8,128)(2,1)}, u32[]{:S(2)}) copy-start(bf16[200,5504]{1,0:T(8,128)(2,1)} %param.37) | copy-start | bytes 6604804
  7.2 81.6 %all-gather.7.cloned.1.call-start = ((), (), s32[]{:S(2)}) async-start(), calls=%async_computation.5 | async-start | bytes 9216000 | tf_op jit(solution)/shard_map/all_gather | solution.py:971
  15.4 127.4 %all-gather.5.cloned.1.call-start = ((), (), s32[]{:S(2)}) async-start(), calls=%async_computation.4 | async-start | bytes 11520000 | tf_op jit(solution)/shard_map/all_gather | solution.py:971
  16.1 64.0 %copy-start.47 = (s32[1,2048]{1,0:T(1,128)S(1)}, s32[1,2048]{1,0:T(1,128)}, u32[]{:S(2)}) copy-start(s32[1,2048]{1,0:T(1,128)} %param.20) | copy-start | bytes 24580
  16.1 214.5 %all-gather.9.cloned.1.call-start = ((), (), s32[]{:S(2)}) async-start(), calls=%async_computation.6 | async-start | bytes 5990400 | tf_op jit(solution)/shard_map/all_gather | solution.py:971
  76.1 74.4 %collective-permute-start.4 = (bf16[1600,256]{1,0:T(8,128)(2,1)}, bf16[1600,256]{1,0:T(8,128)(2,1)}, u32[]{:S(2)}, u32[]{:S(2)}) collective-permute-start(bf16[1600,256]{1,0:T(8,128)(2,1)} %bitcast.6), channel_id=1, source_target_pairs={{0,3},{1,0},{2,1},{3,2},{4,7},{5,4},{6,5},{7,6},{8,11},{9,8},{10,9... | collective-permute-start | bytes 2457608 | tf_op jit(solution)/shard_map/ppermute | solution.py:986
  78.6 72.0 %collective-permute-start.3 = (bf16[1600,256]{1,0:T(8,128)(2,1)}, bf16[1600,256]{1,0:T(8,128)(2,1)}, u32[]{:S(2)}, u32[]{:S(2)}) collective-permute-start(bf16[1600,256]{1,0:T(8,128)(2,1)} %bitcast.6), channel_id=1, source_target_pairs={{0,2},{1,3},{2,0},{3,1},{4,6},{5,7},{6,4},{7,5},{8,10},{9,11},{10,... | collective-permute-start | bytes 2457608 | tf_op jit(solution)/shard_map/ppermute | solution.py:986
  78.6 72.0 %collective-permute-start.2 = (bf16[1600,256]{1,0:T(8,128)(2,1)}, bf16[1600,256]{1,0:T(8,128)(2,1)}, u32[]{:S(2)}, u32[]{:S(2)}) collective-permute-start(bf16[1600,256]{1,0:T(8,128)(2,1)} %bitcast.6), channel_id=1, source_target_pairs={{0,1},{1,2},{2,3},{3,0},{4,5},{5,6},{6,7},{7,4},{8,9},{9,10},{10,1... | collective-permute-start | bytes 2457608 | tf_op jit(solution)/shard_map/ppermute | solution.py:986
  79.3 212.7 %all-gather.11.cloned.1.call-start = ((), (), s32[]{:S(2)}) async-start(), calls=%async_computation.7 | async-start | bytes 15206400 | tf_op jit(solution)/shard_map/all_gather | solution.py:971
  87.4 65.6 %copy-start.51 = (f32[1024]{0:T(1024)}, f32[1024]{0:T(1024)S(1)}, u32[]{:S(2)}) copy-start(f32[1024]{0:T(1024)S(1)} %add_rsqrt_fusion) | copy-start | bytes 12292
  90.1 30.7 %slice-start = ((s8[4403200]{0:T(1024)(128)(4,1)}), s8[4194304]{0:T(1024)(128)(4,1)S(1)}, s32[]{:S(2)}) async-start(s8[4403200]{0:T(1024)(128)(4,1)} %bitcast.127), calls=%async_computation.12 | async-start | bytes 8388608
  91.8 29.1 %slice-start.1 = ((s8[4403200]{0:T(1024)(128)(4,1)}), s8[208896]{0:T(1024)(128)(4,1)S(1)}, s32[]{:S(2)}) async-start(s8[4403200]{0:T(1024)(128)(4,1)} %bitcast.127), calls=%async_computation.13 | async-start | bytes 417792
  119.4 4.3 collective-permute-start.1
  150.6 249.8 %reduce-scatter.7.cloned.1.call-start = ((), (), s32[]{:S(2)}) async-start(), calls=%async_computation.8 | async-start | bytes 4096000 | tf_op jit(solution)/shard_map/reduce_scatter | solution.py:1187
  157.8 9.7 %collective-permute-start = (bf16[640,1024]{1,0:T(8,128)(2,1)S(1)}, bf16[640,1024]{1,0:T(8,128)(2,1)S(1)}, u32[]{:S(2)}, u32[]{:S(2)}) collective-permute-start(bf16[640,1024]{1,0:T(8,128)(2,1)S(1)} %convolution_convert_fusion.8), channel_id=1, source_target_pairs={{0,4},{1,5},{2,6},{3,7},{8,12},{9,13},{10,14},{11,15},{16,20},{17,... | collective-permute-start | bytes 3932168 | tf_op jit(solution)/shard_map/ppermute | solution.py:1126
  236.3 73.0 %copy-start.10 = (f32[1600,256]{1,0:T(8,128)}, f32[1600,256]{1,0:T(8,128)S(1)}, u32[]{:S(2)}) copy-start(f32[1600,256]{1,0:T(8,128)S(1)} %get-tuple-element.217) | copy-start | bytes 4915204
  338.6 219.1 %reduce-scatter.13.cloned.1.call-start = ((), (), s32[]{:S(2)}) async-start(), calls=%async_computation.11 | async-start | bytes 15206400
  400.4 243.7 %reduce-scatter.9.cloned.1.call-start = ((), (), s32[]{:S(2)}) async-start(), calls=%async_computation.9 | async-start | bytes 13824000 | tf_op jit(solution)/shard_map/reduce_scatter | solution.py:980
  480.4 38.0 %collective-permute-start.7 = (bf16[400,256]{1,0:T(8,128)(2,1)}, bf16[400,256]{1,0:T(8,128)(2,1)S(1)}, u32[]{:S(2)}, u32[]{:S(2)}) collective-permute-start(bf16[400,256]{1,0:T(8,128)(2,1)} %get-tuple-element.249), channel_id=1, source_target_pairs={{0,3},{1,0},{2,1},{3,2},{4,7},{5,4},{6,5},{7,6},{8,11},{9,8},{10,9... | collective-permute-start | bytes 614408 | tf_op jit(solution)/shard_map/ppermute | solution.py:986
  482.0 36.5 %collective-permute-start.6 = (bf16[400,256]{1,0:T(8,128)(2,1)}, bf16[400,256]{1,0:T(8,128)(2,1)S(1)}, u32[]{:S(2)}, u32[]{:S(2)}) collective-permute-start(bf16[400,256]{1,0:T(8,128)(2,1)} %get-tuple-element.250), channel_id=1, source_target_pairs={{0,2},{1,3},{2,0},{3,1},{4,6},{5,7},{6,4},{7,5},{8,10},{9,11},{10,... | collective-permute-start | bytes 614408 | tf_op jit(solution)/shard_map/ppermute | solution.py:986
  482.0 36.5 %collective-permute-start.5 = (bf16[400,256]{1,0:T(8,128)(2,1)}, bf16[400,256]{1,0:T(8,128)(2,1)}, u32[]{:S(2)}, u32[]{:S(2)}) collective-permute-start(bf16[400,256]{1,0:T(8,128)(2,1)} %get-tuple-element.251), channel_id=1, source_target_pairs={{0,1},{1,2},{2,3},{3,0},{4,5},{5,6},{6,7},{7,4},{8,9},{9,10},{10,1... | collective-permute-start | bytes 614408 | tf_op jit(solution)/shard_map/ppermute | solution.py:986
  483.1 46.0 %copy-start.27 = (bf16[640,2048]{1,0:T(8,128)(2,1)}, bf16[640,2048]{1,0:T(8,128)(2,1)S(1)}, u32[]{:S(2)}) copy-start(bf16[640,2048]{1,0:T(8,128)(2,1)S(1)} %slice_dynamic-update-slice_fusion) | copy-start | bytes 7864324
  483.2 45.9 %collective-permute-start.9 = (bf16[640,1024]{1,0:T(8,128)(2,1)S(1)}, bf16[640,1024]{1,0:T(8,128)(2,1)}, u32[]{:S(2)}, u32[]{:S(2)}) collective-permute-start(bf16[640,1024]{1,0:T(8,128)(2,1)S(1)} %slice.249), channel_id=1, source_target_pairs={{4,0},{5,1},{6,2},{7,3},{12,8},{13,9},{14,10},{15,11},{20,16},{21,... | collective-permute-start | bytes 3932168 | tf_op jit(solution)/shard_map/ppermute | solution.py:1226
  540.0 189.4 %reduce-scatter.11.cloned.1.call-start = ((), (), s32[]{:S(2)}) async-start(), calls=%async_computation.10 | async-start | bytes 9216000 | tf_op jit(solution)/shard_map/reduce_scatter | solution.py:980
  546.9 10.8 %collective-permute-start.8 = (f32[16,800]{1,0:T(8,128)S(1)}, f32[16,800]{1,0:T(8,128)S(1)}, u32[]{:S(2)}, u32[]{:S(2)}) collective-permute-start(f32[16,800]{1,0:T(8,128)S(1)} %get-tuple-element.102), channel_id=1, source_target_pairs={{4,0},{5,1},{6,2},{7,3},{12,8},{13,9},{14,10},{15,11},{20,16},{21,... | collective-permute-start | bytes 153608 | tf_op jit(solution)/shard_map/ppermute | solution.py:1235
  644.1 57.3 %copy-start.33 = (f32[1600,256]{1,0:T(8,128)S(1)}, f32[1600,256]{1,0:T(8,128)}, u32[]{:S(2)}) copy-start(f32[1600,256]{1,0:T(8,128)} %get-tuple-element.270) | copy-start | bytes 4915204
  707.9 16.1 %collective-permute-start.10 = (bf16[1,200,592]{2,1,0:T(8,128)(2,1)S(1)}, bf16[1,200,592]{2,1,0:T(8,128)(2,1)S(1)}, u32[]{:S(2)}, u32[]{:S(2)}) collective-permute-start(bf16[1,200,592]{2,1,0:T(8,128)(2,1)S(1)} %get-tuple-element.242), channel_id=1, source_target_pairs={{0,2},{1,3},{2,0},{3,1},{4,6},{5,7},{6,4},{7,5},{8,10},{9,11},{10,... | collective-permute-start | bytes 710408 | tf_op jit(solution)/shard_map/ppermute | solution.py:986
  709.5 14.6 %collective-permute-start.12 = (bf16[1,200,592]{2,1,0:T(8,128)(2,1)S(1)}, bf16[1,200,592]{2,1,0:T(8,128)(2,1)S(1)}, u32[]{:S(2)}, u32[]{:S(2)}) collective-permute-start(bf16[1,200,592]{2,1,0:T(8,128)(2,1)S(1)} %get-tuple-element.243), channel_id=1, source_target_pairs={{0,3},{1,0},{2,1},{3,2},{4,7},{5,4},{6,5},{7,6},{8,11},{9,8},{10,9... | collective-permute-start | bytes 710408 | tf_op jit(solution)/shard_map/ppermute | solution.py:986
  712.2 14.7 %collective-permute-start.11 = (bf16[1,200,592]{2,1,0:T(8,128)(2,1)S(1)}, bf16[1,200,592]{2,1,0:T(8,128)(2,1)S(1)}, u32[]{:S(2)}, u32[]{:S(2)}) collective-permute-start(bf16[1,200,592]{2,1,0:T(8,128)(2,1)S(1)} %get-tuple-element.244), channel_id=1, source_target_pairs={{0,1},{1,2},{2,3},{3,0},{4,5},{5,6},{6,7},{7,4},{8,9},{9,10},{10,1... | collective-permute-start | bytes 710408 | tf_op jit(solution)/shard_map/ppermute | solution.py:986
  731.4 14.1 %collective-permute-start.13 = (bf16[1,200,12]{1,2,0:T(8,128)(2,1)S(1)}, bf16[1,200,12]{1,2,0:T(8,128)(2,1)S(1)}, u32[]{:S(2)}, u32[]{:S(2)}) collective-permute-start(bf16[1,200,12]{1,2,0:T(8,128)(2,1)S(1)} %get-tuple-element.255), channel_id=1, source_target_pairs={{0,2},{1,3},{2,0},{3,1},{4,6},{5,7},{6,4},{7,5},{8,10},{9,11},{10,... | collective-permute-start | bytes 14408 | tf_op jit(solution)/shard_map/ppermute | solution.py:986
  736.9 8.5 %collective-permute-start.14 = (bf16[1,200,12]{1,2,0:T(8,128)(2,1)S(1)}, bf16[1,200,12]{1,2,0:T(8,128)(2,1)S(1)}, u32[]{:S(2)}, u32[]{:S(2)}) collective-permute-start(bf16[1,200,12]{1,2,0:T(8,128)(2,1)S(1)} %get-tuple-element.256), channel_id=1, source_target_pairs={{0,1},{1,2},{2,3},{3,0},{4,5},{5,6},{6,7},{7,4},{8,9},{9,10},{10,1... | collective-permute-start | bytes 14408 | tf_op jit(solution)/shard_map/ppermute | solution.py:986
  736.9 8.5 %collective-permute-start.15 = (bf16[1,200,12]{1,2,0:T(8,128)(2,1)S(1)}, bf16[1,200,12]{1,2,0:T(8,128)(2,1)S(1)}, u32[]{:S(2)}, u32[]{:S(2)}) collective-permute-start(bf16[1,200,12]{1,2,0:T(8,128)(2,1)S(1)} %get-tuple-element.257), channel_id=1, source_target_pairs={{0,3},{1,0},{2,1},{3,2},{4,7},{5,4},{6,5},{7,6},{8,11},{9,8},{10,9... | collective-permute-start | bytes 14408 | tf_op jit(solution)/shard_map/ppermute | solution.py:986
  (57 other events, 333.8 us)
Sparse Core Ops, SparseCore 0:
  15.5 56.2 all-gather.6
  74.2 62.2 all-gather.4
  138.4 41.4 all-gather.8
  181.7 76.0 all-gather.10
  338.7 61.6 reduce-scatter.6
  403.8 98.3 reduce-scatter.12
  540.1 91.2 reduce-scatter.8
  644.3 69.4 reduce-scatter.10

commit v4 on v3

--- a/solution.py
+++ b/solution.py
@@ -112,7 +112,7 @@
             keep[pl.ds(pl.multiple_of(k * STATE, STATE), STATE), :] = state.astype(bf16)
         return block_ref[pl.ds(k, 1), :] * state + local_ref[pl.ds(pl.multiple_of(k * STATE, STATE), STATE), :]
 
-    return lax.fori_loop(0, TILE // SUB, one, state, unroll=8)
+    return lax.fori_loop(0, TILE // SUB, one, state, unroll=True)
 
 
 def end_state_kernel(
@@ -193,7 +193,7 @@
             return (new, carry[1])
         return (new, jnp.sum(new * states[rows, :].astype(f32), axis=0, keepdims=True))
 
-    return lax.fori_loop(0, count, one, carry, unroll=8)
+    return lax.fori_loop(0, count, one, carry, unroll=True)
 
 
 def end_adjoint_kernel(
@@ -403,7 +403,7 @@
     ]
 
 
-def scan_call(kernel, name, tiles, in_specs, out_specs, out_shape, scratch, flops, collective=None):
+def scan_call(kernel, name, tiles, in_specs, out_specs, out_shape, scratch, flops, collective=None, room=16):
     return pl.pallas_call(
         kernel,
         name=name,
@@ -413,12 +413,12 @@
         scratch_shapes=scratch,
         out_shape=out_shape,
         compiler_params=pltpu.CompilerParams(
-            vmem_limit_bytes=48 << 20,
+            vmem_limit_bytes=room << 20,
             dimension_semantics=("arbitrary",),
             collective_id=collective,
             has_side_effects=collective is not None,
         ),
-        cost_estimate=pl.CostEstimate(flops=flops, bytes_accessed=1 << 24, transcendentals=0),
+        cost_estimate=pl.CostEstimate(flops=flops, bytes_accessed=flops // 100, transcendentals=0),
     )
 
 
@@ -446,7 +446,7 @@
         state,
         jax.ShapeDtypeStruct((STATE, channels), f32),
         scan_scratch(channels),
-        10**10,
+        10**7,
     )(mixed, *side)
 
 
@@ -465,7 +465,7 @@
             jax.ShapeDtypeStruct((STATE, channels), f32),
         ],
         scan_scratch(channels),
-        16 * 10**9,
+        10**7,
     )(mixed, *side, skip, start)
 
 
@@ -486,6 +486,7 @@
         scan_scratch(channels) + line_sum_scratch(count, height, each),
         10**10,
         collective,
+        24,
     )(gated_grad, mixed, *side, source)
 
 
@@ -526,6 +527,7 @@
         + line_sum_scratch(count, height, each),
         36 * 10**9,
         collective,
+        48,
     )(gated_grad, mixed, states, *side, skip, start, final, source)
 
 
@@ -574,29 +576,30 @@
     def neighbour(side):
         return place < count - 1 if side == 0 else place > 0
 
-    def send(step):
-        for side in (0, 1):
-
-            @pl.when(neighbour(side) & has(side, step))
-            def _():
-                remote(side, step).start()
-
-    def receive(step):
-        for side in (0, 1):
-
-            @pl.when(has(side, step + 1))
-            def _():
-                remote(side, step).wait_recv()
+    def send(side, step):
+        @pl.when(neighbour(side) & has(side, step))
+        def _():
+            remote(side, step).start()
+
+    def receive(side, step):
+        @pl.when(has(side, step + 1))
+        def _():
+            remote(side, step).wait_recv()
 
     def start():
         neighbour_barrier(count)
         local().start()
-        send(0)
+        for side in (0, 1):
+            send(side, 0)
 
     def step(k):
-        receive(k - 1)
-        if k < count - 1:
-            send(k)
+        for side in (0, 1):
+            receive(side, k - 1)
+        for side in (0, 1):
+            if k < count - 1:
+                send(side, k)
+
+    step.send, step.receive = send, receive
 
     def finish():
         for k in range(count - 1):
@@ -768,7 +771,156 @@
         compiler_params=pltpu.CompilerParams(
             vmem_limit_bytes=24 << 20, collective_id=collective, has_side_effects=True
         ),
+        cost_estimate=pl.CostEstimate(flops=5 * 10**10, bytes_accessed=1 << 24, transcendentals=0),
     )(source)
+
+
+def feed_kernel(
+    count,
+    blocks,
+    source,
+    other,
+    weights,
+    group,
+    gate_up_grad,
+    hidden,
+    part_sum,
+    maps,
+    tokens,
+    grads,
+    grad_rows,
+    hidden_rows,
+    partial,
+    copies,
+    loads,
+    stores,
+    send_sems,
+    recv_sems,
+):
+    place = lax.axis_index("tp")
+    start, step, finish = line_steps(count, source, group, copies, send_sems, recv_sems)
+    receive, send = step.receive, step.send
+    ff = hidden.shape[1]
+    width = source.shape[1]
+    near = jnp.minimum(place, count - 1 - place)
+
+    def owner_of(q):
+        spread_out = jnp.where(q % 2 == 1, place - (q + 1) // 2, place + q // 2)
+        rest = jnp.where(place < count - 1 - place, q, count - 1 - q)
+        return jnp.where(q <= 2 * near, spread_out, rest)
+
+    def load(what, where, k):
+        return pltpu.make_async_copy(what, where, loads.at[k])
+
+    def columns(array, owner):
+        return array.at[:, pl.ds(pl.multiple_of(owner * width, width), width)]
+
+    def store(q):
+        owner, slot = owner_of(q), q % 2
+        at = pl.ds(pl.multiple_of(owner * width, width), width)
+        return [
+            pltpu.make_async_copy(grad_rows.at[slot], gate_up_grad.at[at, :], stores.at[slot, 0]),
+            pltpu.make_async_copy(hidden_rows.at[slot], hidden.at[at, :], stores.at[slot, 1]),
+            pltpu.make_async_copy(partial.at[slot], columns(part_sum, owner), stores.at[slot, 2]),
+        ]
+
+    start()
+    load(other, grads, 2).start()
+    load(weights.at[:, : 3 * ff], maps, 0).start()
+
+    def one(q, carry):
+        owner, slot = owner_of(q), q % 2
+        for far in range(1, count):
+            for side in (0, 1):
+                here = place - far if side == 0 else place + far
+
+                @pl.when((q > 0) & (owner == here))
+                def _():
+                    receive(side, far - 1)
+                    if far < count - 1:
+                        send(side, far)
+
+        @pl.when(q == 0)
+        def _():
+            load(source, tokens, 1).start()
+            load(source, tokens, 1).wait()
+
+        @pl.when(q > 0)
+        def _():
+            load(columns(group, owner), tokens, 1).start()
+            load(columns(group, owner), tokens, 1).wait()
+
+        @pl.when(q == 0)
+        def _():
+            load(other, grads, 2).wait()
+            load(weights.at[:, : 3 * ff], maps, 0).wait()
+
+        @pl.when(q > 1)
+        def _():
+            for copy in store(q - 2):
+                copy.wait()
+
+        rows = tokens[...].T
+        outs = columns(grads, owner)[...].T
+        for begin, wide in blocks:
+            gate = mm(rows, maps[:, begin : begin + wide])
+            up = mm(rows, maps[:, ff + begin : ff + begin + wide])
+            grad = mm(outs, maps[:, 2 * ff + begin : 2 * ff + begin + wide])
+            sigma = lax.logistic(gate)
+            active = gate * sigma
+            hidden_rows[slot, :, begin : begin + wide] = (active * up).astype(bf16)
+            grad_rows[slot, :, begin : begin + wide] = (
+                grad * up * (sigma * (1.0 + gate * (1.0 - sigma)))
+            ).astype(bf16)
+            grad_rows[slot, :, ff + begin : ff + begin + wide] = (grad * active).astype(bf16)
+        partial[slot] = mm_nt(maps[:, : 2 * ff], grad_rows[slot]).astype(bf16)
+        for copy in store(q):
+            copy.start()
+        return carry
+
+    lax.fori_loop(0, count, one, 0)
+    for q in (count - 2, count - 1):
+        for copy in store(q):
+            copy.wait()
+    finish()
+
+
+def feed_forward(source, other, weights, ff, count, collective):
+    depth, width = source.shape
+    blocks = []
+    begin = 0
+    while begin < ff:
+        blocks.append((begin, min(256, ff - begin)))
+        begin = begin + 256
+    anywhere = pl.BlockSpec(memory_space=pl.ANY)
+    return pl.pallas_call(
+        functools.partial(feed_kernel, count, tuple(blocks)),
+        name="feed_forward",
+        in_specs=[anywhere] * 3,
+        out_specs=[anywhere] * 4,
+        out_shape=[
+            jax.ShapeDtypeStruct((depth, width * count), bf16),
+            jax.ShapeDtypeStruct((width * count, 2 * ff), bf16),
+            jax.ShapeDtypeStruct((width * count, ff), bf16),
+            jax.ShapeDtypeStruct((depth, width * count), bf16),
+        ],
+        scratch_shapes=[
+            pltpu.VMEM((depth, 3 * ff), bf16),
+            pltpu.VMEM((depth, width), bf16),
+            pltpu.VMEM((depth, width * count), bf16),
+            pltpu.VMEM((2, width, 2 * ff), bf16),
+            pltpu.VMEM((2, width, ff), bf16),
+            pltpu.VMEM((2, depth, width), bf16),
+            pltpu.SemaphoreType.DMA,
+            pltpu.SemaphoreType.DMA((3,)),
+            pltpu.SemaphoreType.DMA((2, 3)),
+            pltpu.SemaphoreType.DMA((2, count - 1)),
+            pltpu.SemaphoreType.DMA((2, count - 1)),
+        ],
+        compiler_params=pltpu.CompilerParams(
+            vmem_limit_bytes=56 << 20, collective_id=collective, has_side_effects=True
+        ),
+    )(source, other, weights)
 
 
 def attend_kernel(
@@ -1126,15 +1278,14 @@
     earlier_t = lax.ppermute(keyval_group_t, "ctx", [(0, 1)])
 
     gated, states, state_final = forward_scan(mixed, side, skip_row, state_start)
+    third = jnp.concatenate(
+        [jnp.pad(piece, ((0, 0), (0, ff_wide - ff))) for piece in ffn_shards] + [attn_output],
+        axis=1,
+    )
+    third, gated, *cotangent_pieces = lax.optimization_barrier((third, gated, *cotangent_pieces))
+    third = gather_rows(third)
     mamba_part_t = dot(state_out_map, gated, 1, 1).astype(bf16)
-    third = jnp.concatenate(
-        [jnp.pad(piece, ((0, 0), (0, ff_wide - ff))) for piece in ffn_shards], axis=1
-    )
-    mamba_part_t, third, *cotangent_pieces = lax.optimization_barrier(
-        (mamba_part_t, third, *cotangent_pieces)
-    )
-    third = gather_rows(third)
-    up_map, down_map = cut(third, [2 * ff_wide, ff_wide])
+    up_map, down_map, attn_map = cut(third, [2 * ff_wide, ff_wide, query_width])
 
     key_start = span + tp_index * rows - WIN
     keyval_t = jnp.concatenate(
@@ -1169,29 +1320,17 @@
 
     mid = residual + 0.5 * (rms_norm(attn_out, attn_gain) + rms_norm(mamba_out, mamba_gain))
     ffn_normed_t = rms_norm(mid, ffn_gain).astype(bf16)
-    ffn_normed_group_t = line_gather(ffn_normed_t, tp, 1)
-
-    gate_up = dot(up_map, ffn_normed_group_t, 0, 0)
-    gate, up = gate_up[:ff_wide], gate_up[ff_wide:]
-    sigma = jax.nn.sigmoid(gate)
-    hidden_t = (gate * sigma * up).astype(bf16)
-    hidden_grad = dot(down_map, cotangent_group_t, 0, 0)
-    gate_up_grad_t = jnp.concatenate(
-        [
-            (hidden_grad * up * (sigma * (1.0 + gate * (1.0 - sigma)))).astype(bf16),
-            (hidden_grad * gate * sigma).astype(bf16),
-        ],
-        axis=0,
-    )
-    ffn_grad_part_t = dot(up_map, gate_up_grad_t, 1, 0).astype(bf16)
+    ffn_normed_group_t, gate_up_grad, hidden, ffn_grad_part_t = feed_forward(
+        ffn_normed_t, cotangent_group_t, third, ff_wide, tp, 1
+    )
     ffn_normed_grad_t = lax.psum_scatter(ffn_grad_part_t, "tp", scatter_dimension=1, tiled=True)
-    up_wide = dot(ffn_normed_group_t, gate_up_grad_t, 1, 1).astype(bf16)
-    down_wide = dot(cotangent_group_t, hidden_t, 1, 1).astype(bf16)
+    up_wide = dot(ffn_normed_group_t, gate_up_grad, 1, 0).astype(bf16)
+    down_wide = dot(cotangent_group_t, hidden, 1, 0).astype(bf16)
     ffn_wide = jnp.concatenate([up_wide, down_wide], axis=1)
     fourth = width // 4 // 16 * 16
     out_parts = [
-        dot(down_map[:fourth], hidden_t, 1, 0).astype(bf16),
-        dot(down_map[fourth:], hidden_t, 1, 0).astype(bf16),
+        dot(down_map[:fourth], hidden, 1, 1).astype(bf16),
+        dot(down_map[fourth:], hidden, 1, 1).astype(bf16),
     ]
     ffn_normed_grad_t, ffn_wide, out_parts = lax.optimization_barrier(
         (ffn_normed_grad_t, ffn_wide, out_parts)
@@ -1293,17 +1432,6 @@
     last_wide = by_rows((dot(normed_group_t, mix_grad, 1, 0) + tail).astype(bf16))
     last_wide, early_columns = lax.optimization_barrier((last_wide, early_columns))
     last_columns = scatter_rows(last_wide)
-    normed_grad_low, last_wide = lax.optimization_barrier((normed_grad_low, last_wide))
-    normed_grad = line_sum(normed_grad_low, tp, 4) + query_term
-    early_columns, ffn_columns, normed_grad = lax.optimization_barrier(
-        (early_columns, ffn_columns, normed_grad)
-    )
-    residual_extra, _ = rms_back(residual, mix_gain, normed_grad)
-    grad_tokens_t = (mid_grad + residual_extra).astype(bf16)
-    grad_gate, grad_up, grad_ffn_output = [
-        piece[:, :ff].astype(f32) for piece in cut(ffn_columns, [ff_wide] * 3)
-    ]
-    grad_ffn_input = jnp.stack([grad_gate, grad_up], axis=1)
     attn_shares, _, grad_query, _, meta_shares, keyval_shares, grad_mamba_output = cut(
         early_columns,
         [
@@ -1323,9 +1451,20 @@
     shares = jnp.concatenate(
         [to_device(attn_shares), to_device(keyval_shares), to_device(meta_shares)], axis=2
     )
+    normed_grad_low, last_wide, shares = lax.optimization_barrier(
+        (normed_grad_low, last_wide, shares)
+    )
     grad_attn_output, grad_keyval, grad_meta = cut(
         permute_sums(shares, 0)[0], [each, keyval_width // tp, meta_count // tp]
     )
+    normed_grad = line_sum(normed_grad_low, tp, 4) + query_term
+    ffn_columns, normed_grad = lax.optimization_barrier((ffn_columns, normed_grad))
+    residual_extra, _ = rms_back(residual, mix_gain, normed_grad)
+    grad_tokens_t = (mid_grad + residual_extra).astype(bf16)
+    grad_gate, grad_up, grad_ffn_output = [
+        piece[:, :ff].astype(f32) for piece in cut(ffn_columns, [ff_wide] * 3)
+    ]
+    grad_ffn_input = jnp.stack([grad_gate, grad_up], axis=1)
     select_shares, gain_shares, grad_vectors = cut(last_columns, [2 * STATE, 4, vector_columns])
     shares = jnp.concatenate(
         [to_device(select_shares), jnp.broadcast_to(gain_shares[None], (tp, shard, 4))], axis=2

time: 763 us -> 748 us (0.980)
  matrix products: 193 us -> 138 us
  Pallas kernels: 398 us -> 419 us
  waiting for transfers between devices: 27.8 us -> 45.7 us
    pallas_call x0 -> x1, Pallas kernels: none -> 77.1 us  [feed_forward(): pl.pallas_call(functools.partial(feed_kernel, count, tuple(blocks)), name...]
    dot_general x25 -> x22, matrix products: 193 us -> 138 us  [dot(): lax.dot_general(left, right, (((left_dim,), (right_dim,)), ((), ())), pre...]
    pallas_call x2 -> x1, Pallas kernels: 114 us -> 59.9 us  [line_gather(): pl.pallas_call(functools.partial(line_gather_kernel, count), name='line_g...]
    all_gather x4 -> x3, waiting for transfers between devices: 0.06 us -> 8.2 us  [gather_rows(): return lax.all_gather(whole, ('fsdp', 'ctx'), axis=0, tiled=True)]
    pallas_call x1, Pallas kernels: 59.2 us -> 66.9 us  [attend(): pl.pallas_call(functools.partial(attend_kernel, group, count), name='atte...]
    unnamed x127 -> x129, local copies, waits for them, and re-layouts: 13.1 us -> 18.5 us
  transfers between devices with their start and end apart: 24 -> 23, of which waited for: 3 -> 5; matrix products, arithmetic and copies ran while one was open for 29% -> 27% of each run, Pallas kernels for 53% -> 46%
where the time goes in v4:
time: 748 us; the launch traced here: 736 us
  Pallas kernels  419 us (56%)
  matrix products  138 us (18%)
  other arithmetic  49.9 us (7%)
  local copies, waits for them, and re-layouts  46.9 us (6%)
  waiting for transfers between devices  45.7 us (6%)
  starting transfers between devices  19.8 us (3%)
  between operations  16.9 us (2%)
    dot_general x22, matrix products, dot(): lax.dot_general(left, right, (((left_dim,), (right_dim,)), ((), ())), pre...  138 us
    pallas_call x1, Pallas kernels, feed_forward(): pl.pallas_call(functools.partial(feed_kernel, count, tuple(blocks)), name...  77.1 us
    pallas_call x1, Pallas kernels, attend(): pl.pallas_call(functools.partial(attend_kernel, group, count), name='atte...  66.9 us
    pallas_call x1, Pallas kernels, attend_back(): pl.pallas_call(functools.partial(attend_back_kernel, group, count), name=...  62.4 us
    pallas_call x1, Pallas kernels, line_gather(): pl.pallas_call(functools.partial(line_gather_kernel, count), name='line_g...  59.9 us
    pallas_call x1, Pallas kernels, line_sum(): pl.pallas_call(functools.partial(line_sum_kernel, count), name='line_sum'...  56.7 us
    pallas_call x1, Pallas kernels, backward_scan(): scan_call(functools.partial(backward_kernel, count), 'backward_scan', til...  51.5 us
    reduce_scatter x1, waiting for transfers between devices, per_device(): lax.psum_scatter(ffn_grad_part_t, 'tp', scatter_dimension=1, tiled=True)  25.9 us
  transfers between devices with their start and end apart: 23, of which 5 were waited for; matrix products, arithmetic and copies ran while one was open for 27% of the time, Pallas kernels for 46%

profile of v4, /device:TPU:0, one launch (start us, length us, event | category | flops | bytes accessed | tf_op | source)
XLA Modules:
  0.0 736.0 jit_solution(5749014358602148789)
XLA Ops:
  16.2 59.9 %line_gather.1 = bf16[1600,1024]{1,0:T(8,128)(2,1)} custom-call(bf16[1600,256]{1,0:T(8,128)(2,1)} %bitcast.96), custom_call_target="tpu_custom_call" | custom-call | tf_op jit(solution)/shard_map/line_gather/pallas_call | solution.py:634
  91.6 12.8 %fusion.144.mixed = f32[1024,2528]{1,0:T(8,128)S(1)} fusion(bf16[1600,2528]{1,0:T(8,128)(2,1)} %all-gather.4.cloned.1.call-done, bf16[1600,1024]{1,0:T(8,128)(2,1)S(1)} %copy-done.24, f32[1600]{0:T(1024)S(1)} %get-tuple-element.219, f32[1024]{0:T(1024)S(1)} %add_rsqrt_fusion), kind=kOutput, calls=%fused_computation.295 | convolution fusion | flops 8290304000 | bytes 21731584 | tf_op jit(solution)/shard_map/dot_general | solution.py:1117
  104.4 9.2 %end_state.1 = f32[16,800]{1,0:T(8,128)S(1)} custom-call(f32[1024,2528]{1,0:T(8,128)S(1)} %fusion.144.mixed, f32[1024,8]{1,0:T(8,128)S(1)} %copy.116.aux, f32[8,1024]{1,0:T(8,128)S(1)} %stack.43.aux_t, f32[256,1]{1,0:T(8,128)S(1)} %fusion.118.alive_last, f32[1,800]{1,0:T(1,128)S(1)} %broadcast_in_dim.166.bias, f32[1,800]{1,0:T(1,128)S(1)} %broadcast_in_dim.167.rate, ...), custom_call_target="tpu_custom_call" | custom-call | flops 10000000 | bytes 100000 | tf_op jit(solution)/shard_map/end_state/pallas_call | solution.py:441
  116.7 4.0 fusion.37
  120.7 4.1 copy-done.3
  124.8 13.3 %forward_scan.1 = (bf16[1024,800]{1,0:T(8,128)(2,1)S(1)}, bf16[4096,800]{1,0:T(8,128)(2,1)S(1)}, f32[16,800]{1,0:T(8,128)S(1)}) custom-call(f32[1024,2528]{1,0:T(8,128)S(1)} %copy-done.3, f32[1024,8]{1,0:T(8,128)S(1)} %copy.116.aux, f32[8,1024]{1,0:T(8,128)S(1)} %stack.43.aux_t, f32[256,1]{1,0:T(8,128)S(1)} %fusion.118.alive_last, ...), custom_call_target="tpu_custom_call" | custom-call | flops 10000000 | bytes 100000 | tf_op jit(solution)/shard_map/forward_scan/pallas_call | solution.py:456
  149.4 5.5 convolution_convert_fusion.7
  160.8 5.5 convolution_convert_fusion.4.source
  168.4 66.9 %attend.1 = (bf16[1600,256]{1,0:T(8,128)(2,1)}, f32[5,8,256]{2,1,0:T(8,128)}, f32[1600,256]{1,0:T(8,128)}) custom-call(bf16[1600,256]{1,0:T(8,128)(2,1)} %fusion.26.query_t, bf16[640,1408]{1,0:T(8,128)(2,1)} %pad_maximum_fusion.2.key_t.value_t, bf16[640,1408]{1,0:T(8,128)(2,1)} %pad_maximum_fusion.2.key_t.value_t, f32[1408,256]{1,0:T(8,128)} %concatenate.67.bias, ...), custom_call_target="tpu_custom_call" | custom-call | tf_op jit(solution)/shard_map/attend/pallas_call | solution.py:1035
  236.9 8.2 %all-gather.6.cloned.1.call-done.weights = bf16[1600,5824]{1,0:T(8,128)(2,1)} async-done(((bf16[200,5824]{1,0:T(8,128)(2,1)}), bf16[1600,5824]{1,0:T(8,128)(2,1)}) %all-gather.6.cloned.1.call-update) | async-done | bytes 18636816 | tf_op jit(solution)/shard_map/all_gather | solution.py:1123
  245.1 4.6 multiply_reduce_fusion.6
  252.3 77.1 %feed_forward.1 = (bf16[1600,1024]{1,0:T(8,128)(2,1)}, bf16[1024,2816]{1,0:T(8,128)(2,1)}, bf16[1024,1408]{1,0:T(8,128)(2,1)}, bf16[1600,1024]{1,0:T(8,128)(2,1)}) custom-call(bf16[1600,256]{1,0:T(8,128)(2,1)} %multiply_convert_fusion.2.source, bf16[1600,1024]{1,0:T(8,128)(2,1)} %pad_maximum_fusion.1.other, ...), custom_call_target="tpu_custom_call" | custom-call | tf_op jit(solution)/shard_map/feed_forward/pallas_call | solution.py:896
  333.3 7.7 %convolution_convert_fusion.3.source = bf16[1200,1024]{1,0:T(8,128)(2,1)} fusion(bf16[1024,1408]{1,0:T(8,128)(2,1)S(1)} %copy-done.53, bf16[1600,5824]{1,0:T(8,128)(2,1)} %all-gather.6.cloned.1.call-done.weights), kind=kOutput, calls=%fused_computation.33 | convolution fusion | flops 3461529600 | bytes 8720384 | tf_op jit(solution)/shard_map/dot_general | solution.py:1117
  341.0 5.5 convolution_convert_fusion.1
  346.5 10.1 %convolution_convert_fusion = bf16[1600,2816]{1,0:T(8,128)(2,1)S(1)} fusion(bf16[1600,1024]{1,0:T(8,128)(2,1)S(1)} %copy-done.52, bf16[1024,2816]{1,0:T(8,128)(2,1)S(1)} %bitcast.122), kind=kOutput, calls=%fused_computation.2 | convolution fusion | flops 9231974400 | bytes 18055168 | tf_op jit(solution)/shard_map/dot_general | solution.py:1117
  356.6 6.6 pad_maximum_fusion
  363.2 25.9 %reduce-scatter.7.cloned.1.call-done = bf16[1600,256]{1,0:T(8,128)(2,1)} async-done(((bf16[1600,1024]{1,0:T(8,128)(2,1)}), bf16[1600,256]{1,0:T(8,128)(2,1)}) %reduce-scatter.7.cloned.1.call-update) | async-done | bytes 819216 | tf_op jit(solution)/shard_map/reduce_scatter | solution.py:1326
  392.5 4.0 multiply_reduce_fusion
  398.6 5.3 fusion.23.grad_t
  403.8 62.4 %attend_back.1 = (bf16[1600,256]{1,0:T(8,128)(2,1)}, bf16[2,320,1408]{2,1,0:T(8,128)(2,1)}, bf16[1600,1024]{1,0:T(8,128)(2,1)}) custom-call(bf16[1600,256]{1,0:T(8,128)(2,1)} %fusion.26.query_t, bf16[640,1408]{1,0:T(8,128)(2,1)} %pad_maximum_fusion.2.key_t.value_t, bf16[640,1408]{1,0:T(8,128)(2,1)} %pad_maximum_fusion.2.key_t.value_t, ...), custom_call_target="tpu_custom_call" | custom-call | tf_op jit(solution)/shard_map/attend_back/pallas_call | solution.py:1074
  478.7 6.3 fusion.29.gated_grad
  485.0 22.4 %end_adjoint.1 = (f32[16,800]{1,0:T(8,128)S(1)}, f32[400,256]{1,0:T(8,128)S(1)}) custom-call(f32[1024,800]{1,0:T(8,128)S(1)} %fusion.29.gated_grad, f32[1024,2528]{1,0:T(8,128)S(1)} %bitcast.94, f32[1024,8]{1,0:T(8,128)S(1)} %copy.116.aux, f32[8,1024]{1,0:T(8,128)S(1)} %stack.43.aux_t, f32[256,1]{1,0:T(8,128)S(1)} %fusion.118.alive_last, ...), custom_call_target="tpu_custom_call" | custom-call | flops 10000000000 | bytes 100000000 | tf_op jit(solution)/shard_map/end_adjoint/pallas_call | solution.py:476
  507.5 4.1 fusion.2
  517.2 4.4 fusion.21
  521.6 4.9 fusion.19
  527.9 5.5 fusion.50
  534.7 7.7 %fusion.59 = f32[1600,1024]{1,0:T(8,128)} fusion(bf16[1600,3168]{1,0:T(8,128)(2,1)} %all-gather.8.cloned.1.call-done, bf16[640,1024]{1,0:T(8,128)(2,1)S(1)} %copy-done.55, bf16[640,2048]{1,0:T(8,128)(2,1)S(1)} %copy-done.27), kind=kOutput, calls=%fused_computation.98 | convolution fusion | flops 2099773440 | bytes 11223040 | tf_op jit(solution)/shard_map/dot_general | solution.py:1117
  544.6 51.5 %backward_scan.1 = (bf16[1024,2528]{1,0:T(8,128)(2,1)}, f32[8,800]{1,0:T(8,128)S(1)}, f32[1200,256]{1,0:T(8,128)S(1)}) custom-call(f32[1024,800]{1,0:T(8,128)} %copy-done.7, f32[1024,2528]{1,0:T(8,128)} %copy-done.2, bf16[4096,800]{1,0:T(8,128)(2,1)} %copy-done.4, f32[1024,8]{1,0:T(8,128)S(1)} %copy.116.aux, f32[8,1024]{1,0:T(8,128)S(1)} %stack.43.aux_t, ...), custom_call_target="tpu_custom_call" | custom-call | flops 35999997952 | bytes 360000000 | tf_op jit(solution)/shard_map/backward_scan/pallas_call | solution.py:497
  596.1 17.6 %fusion.4 = (f32[1600]{0:T(1024)S(1)}, bf16[1600,1024]{1,0:T(8,128)(2,1)}) fusion(bf16[1600,1024]{1,0:T(8,128)(2,1)} %line_gather.1, f32[1024]{0:T(1024)S(1)} %add_rsqrt_fusion, f32[1600,1024]{1,0:T(8,128)} %fusion.59, bf16[1600,2528]{1,0:T(8,128)(2,1)} %all-gather.4.cloned.1.call-done, bf16[1024,2528]{1,0:T(8,128)(2,1)} %get-tuple-element.126), kind=kOutput, calls=%fused_computation.15 | convolution fusion | flops 8293579264 | bytes 26384640 | tf_op jit(solution)/shard_map/dot_general | solution.py:1117
  614.6 14.5 %add_convert_fusion = bf16[1600,2528]{1,0:T(8,128)(2,1)} fusion(f32[1600,16]{1,0:T(8,128)S(1)} %copy.129, bf16[1024,2528]{1,0:T(8,128)(2,1)} %get-tuple-element.126, bf16[1600,1024]{1,0:T(8,128)(2,1)} %line_gather.1, f32[1600]{0:T(1024)S(1)} %get-tuple-element.219, f32[1024]{0:T(1024)S(1)} %add_rsqrt_fusion), kind=kOutput, calls=%fused_computation | convolution fusion | flops 8298393600 | bytes 16656640 | tf_op jit(solution)/shard_map/dot_general | solution.py:1117
  635.9 56.7 %line_sum.1 = f32[1600,256]{1,0:T(8,128)S(1)} custom-call(bf16[1600,1024]{1,0:T(8,128)(2,1)S(1)} %copy-done.9), custom_call_target="tpu_custom_call" | custom-call | flops 49999998976 | bytes 16777216 | tf_op jit(solution)/shard_map/line_sum/pallas_call | solution.py:764
  708.4 7.6 %collective-permute-done.10 = bf16[1,200,592]{2,1,0:T(8,128)(2,1)S(1)} collective-permute-done((bf16[1,200,592]{2,1,0:T(8,128)(2,1)S(1)}, bf16[1,200,592]{2,1,0:T(8,128)(2,1)S(1)}, u32[]{:S(2)}, u32[]{:S(2)}) %collective-permute-start.10) | collective-permute-done | bytes 236832 | tf_op jit(solution)/shard_map/ppermute | solution.py:1138
  (326 shorter events, 117.8 us)
Async XLA Ops:
  7.2 107.0 %copy-start = (bf16[200,5504]{1,0:T(8,128)(2,1)S(1)}, bf16[200,5504]{1,0:T(8,128)(2,1)}, u32[]{:S(2)}) copy-start(bf16[200,5504]{1,0:T(8,128)(2,1)} %param.37) | copy-start | bytes 6604804
  7.2 81.4 %all-gather.4.cloned.1.call-start = ((), (), s32[]{:S(2)}) async-start(), calls=%async_computation.4 | async-start | bytes 9216000 | tf_op jit(solution)/shard_map/all_gather | solution.py:1123
  15.4 64.6 %copy-start.47 = (s32[1,2048]{1,0:T(1,128)S(1)}, s32[1,2048]{1,0:T(1,128)}, u32[]{:S(2)}) copy-start(s32[1,2048]{1,0:T(1,128)} %param.20) | copy-start | bytes 24580
  15.4 134.0 %all-gather.8.cloned.1.call-start = ((), (), s32[]{:S(2)}) async-start(), calls=%async_computation.6 | async-start | bytes 11520000 | tf_op jit(solution)/shard_map/all_gather | solution.py:1123
  16.1 68.4 %copy-start.49 = (f32[800]{0:T(1024)S(1)}, f32[800]{0:T(1024)}, u32[]{:S(2)}) copy-start(f32[800]{0:T(1024)} %param.30) | copy-start | bytes 9604
  16.2 68.4 %copy-start.48 = (f32[800]{0:T(1024)S(1)}, f32[800]{0:T(1024)}, u32[]{:S(2)}) copy-start(f32[800]{0:T(1024)} %param.31) | copy-start | bytes 9604
  16.2 68.4 %copy-start.50 = (f32[800]{0:T(1024)S(1)}, f32[800]{0:T(1024)}, u32[]{:S(2)}) copy-start(f32[800]{0:T(1024)} %param.32) | copy-start | bytes 9604
  16.2 228.9 %all-gather.6.cloned.1.call-start = ((), (), s32[]{:S(2)}) async-start(), calls=%async_computation.5 | async-start | bytes 21196800 | tf_op jit(solution)/shard_map/all_gather | solution.py:1123
  76.1 64.9 %collective-permute-start.1 = (bf16[1600,256]{1,0:T(8,128)(2,1)}, bf16[1600,256]{1,0:T(8,128)(2,1)}, u32[]{:S(2)}, u32[]{:S(2)}) collective-permute-start(bf16[1600,256]{1,0:T(8,128)(2,1)} %bitcast.6), channel_id=1, source_target_pairs={{0,1},{1,2},{2,3},{3,0},{4,5},{5,6},{6,7},{7,4},{8,9},{9,10},{10,1... | collective-permute-start | bytes 2457608 | tf_op jit(solution)/shard_map/ppermute | solution.py:1138
  76.2 64.8 %collective-permute-start.2 = (bf16[1600,256]{1,0:T(8,128)(2,1)}, bf16[1600,256]{1,0:T(8,128)(2,1)}, u32[]{:S(2)}, u32[]{:S(2)}) collective-permute-start(bf16[1600,256]{1,0:T(8,128)(2,1)} %bitcast.6), channel_id=1, source_target_pairs={{0,2},{1,3},{2,0},{3,1},{4,6},{5,7},{6,4},{7,5},{8,10},{9,11},{10,... | collective-permute-start | bytes 2457608 | tf_op jit(solution)/shard_map/ppermute | solution.py:1138
  79.1 61.9 %collective-permute-start.3 = (bf16[1600,256]{1,0:T(8,128)(2,1)}, bf16[1600,256]{1,0:T(8,128)(2,1)}, u32[]{:S(2)}, u32[]{:S(2)}) collective-permute-start(bf16[1600,256]{1,0:T(8,128)(2,1)} %bitcast.6), channel_id=1, source_target_pairs={{0,3},{1,0},{2,1},{3,2},{4,7},{5,4},{6,5},{7,6},{8,11},{9,8},{10,9... | collective-permute-start | bytes 2457608 | tf_op jit(solution)/shard_map/ppermute | solution.py:1138
  89.9 23.8 %slice-start.3 = ((s8[4403200]{0:T(1024)(128)(4,1)}), s8[4194304]{0:T(1024)(128)(4,1)S(1)}, s32[]{:S(2)}) async-start(s8[4403200]{0:T(1024)(128)(4,1)} %bitcast.103), calls=%async_computation.14 | async-start | bytes 8388608
  115.2 5.5 collective-permute-start
  141.0 248.0 %reduce-scatter.7.cloned.1.call-start = ((), (), s32[]{:S(2)}) async-start(), calls=%async_computation.7 | async-start | bytes 4096000 | tf_op jit(solution)/shard_map/reduce_scatter | solution.py:1326
  154.8 11.4 %collective-permute-start.4 = (bf16[640,1024]{1,0:T(8,128)(2,1)S(1)}, bf16[640,1024]{1,0:T(8,128)(2,1)S(1)}, u32[]{:S(2)}, u32[]{:S(2)}) collective-permute-start(bf16[640,1024]{1,0:T(8,128)(2,1)S(1)} %convolution_convert_fusion.7), channel_id=1, source_target_pairs={{0,4},{1,5},{2,6},{3,7},{8,12},{9,13},{10,14},{11,15},{16,20},{17,... | collective-permute-start | bytes 3932168 | tf_op jit(solution)/shard_map/ppermute | solution.py:1278
  250.8 78.5 %copy-start.10 = (f32[1600,256]{1,0:T(8,128)}, f32[1600,256]{1,0:T(8,128)S(1)}, u32[]{:S(2)}) copy-start(f32[1600,256]{1,0:T(8,128)S(1)} %get-tuple-element.225) | copy-start | bytes 4915204
  329.4 213.0 %reduce-scatter.13.cloned.1.call-start = ((), (), s32[]{:S(2)}) async-start(), calls=%async_computation.10 | async-start | bytes 15206400
  389.1 240.0 %reduce-scatter.9.cloned.1.call-start = ((), (), s32[]{:S(2)}) async-start(), calls=%async_computation.8 | async-start | bytes 13824000 | tf_op jit(solution)/shard_map/reduce_scatter | solution.py:1132
  467.6 39.8 %collective-permute-start.5 = (bf16[400,256]{1,0:T(8,128)(2,1)S(1)}, bf16[400,256]{1,0:T(8,128)(2,1)S(1)}, u32[]{:S(2)}, u32[]{:S(2)}) collective-permute-start(bf16[400,256]{1,0:T(8,128)(2,1)S(1)} %get-tuple-element.256), channel_id=1, source_target_pairs={{0,1},{1,2},{2,3},{3,0},{4,5},{5,6},{6,7},{7,4},{8,9},{9,10},{10,1... | collective-permute-start | bytes 614408 | tf_op jit(solution)/shard_map/ppermute | solution.py:1138
  467.7 39.8 %collective-permute-start.6 = (bf16[400,256]{1,0:T(8,128)(2,1)S(1)}, bf16[400,256]{1,0:T(8,128)(2,1)S(1)}, u32[]{:S(2)}, u32[]{:S(2)}) collective-permute-start(bf16[400,256]{1,0:T(8,128)(2,1)S(1)} %get-tuple-element.255), channel_id=1, source_target_pairs={{0,2},{1,3},{2,0},{3,1},{4,6},{5,7},{6,4},{7,5},{8,10},{9,11},{10,... | collective-permute-start | bytes 614408 | tf_op jit(solution)/shard_map/ppermute | solution.py:1138
  470.4 37.1 %collective-permute-start.7 = (bf16[400,256]{1,0:T(8,128)(2,1)S(1)}, bf16[400,256]{1,0:T(8,128)(2,1)S(1)}, u32[]{:S(2)}, u32[]{:S(2)}) collective-permute-start(bf16[400,256]{1,0:T(8,128)(2,1)S(1)} %get-tuple-element.254), channel_id=1, source_target_pairs={{0,3},{1,0},{2,1},{3,2},{4,7},{5,4},{6,5},{7,6},{8,11},{9,8},{10,9... | collective-permute-start | bytes 614408 | tf_op jit(solution)/shard_map/ppermute | solution.py:1138
  472.0 45.2 %copy-start.26 = (bf16[640,2048]{1,0:T(8,128)(2,1)}, bf16[640,2048]{1,0:T(8,128)(2,1)S(1)}, u32[]{:S(2)}) copy-start(bf16[640,2048]{1,0:T(8,128)(2,1)S(1)} %slice_dynamic-update-slice_fusion) | copy-start | bytes 7864324
  472.2 45.0 %collective-permute-start.9 = (bf16[640,1024]{1,0:T(8,128)(2,1)S(1)}, bf16[640,1024]{1,0:T(8,128)(2,1)S(1)}, u32[]{:S(2)}, u32[]{:S(2)}) collective-permute-start(bf16[640,1024]{1,0:T(8,128)(2,1)S(1)} %slice.235), channel_id=1, source_target_pairs={{4,0},{5,1},{6,2},{7,3},{12,8},{13,9},{14,10},{15,11},{20,16},{21,... | collective-permute-start | bytes 3932168 | tf_op jit(solution)/shard_map/ppermute | solution.py:1365
  526.5 192.0 %reduce-scatter.11.cloned.1.call-start = ((), (), s32[]{:S(2)}) async-start(), calls=%async_computation.9 | async-start | bytes 9216000 | tf_op jit(solution)/shard_map/reduce_scatter | solution.py:1132
  533.4 9.0 %collective-permute-start.8 = (f32[16,800]{1,0:T(8,128)S(1)}, f32[16,800]{1,0:T(8,128)S(1)}, u32[]{:S(2)}, u32[]{:S(2)}) collective-permute-start(f32[16,800]{1,0:T(8,128)S(1)} %get-tuple-element.110), channel_id=1, source_target_pairs={{4,0},{5,1},{6,2},{7,3},{12,8},{13,9},{14,10},{15,11},{20,16},{21,... | collective-permute-start | bytes 153608 | tf_op jit(solution)/shard_map/ppermute | solution.py:1374
  635.9 56.7 %copy-start.39 = (f32[1600,256]{1,0:T(8,128)S(1)}, f32[1600,256]{1,0:T(8,128)}, u32[]{:S(2)}) copy-start(f32[1600,256]{1,0:T(8,128)} %get-tuple-element.276) | copy-start | bytes 4915204
  692.9 12.3 %collective-permute-start.12 = (bf16[1,200,592]{2,1,0:T(8,128)(2,1)S(1)}, bf16[1,200,592]{2,1,0:T(8,128)(2,1)S(1)}, u32[]{:S(2)}, u32[]{:S(2)}) collective-permute-start(bf16[1,200,592]{2,1,0:T(8,128)(2,1)S(1)} %get-tuple-element.248), channel_id=1, source_target_pairs={{0,3},{1,0},{2,1},{3,2},{4,7},{5,4},{6,5},{7,6},{8,11},{9,8},{10,9... | collective-permute-start | bytes 710408 | tf_op jit(solution)/shard_map/ppermute | solution.py:1138
  694.9 13.4 %collective-permute-start.11 = (bf16[1,200,592]{2,1,0:T(8,128)(2,1)S(1)}, bf16[1,200,592]{2,1,0:T(8,128)(2,1)S(1)}, u32[]{:S(2)}, u32[]{:S(2)}) collective-permute-start(bf16[1,200,592]{2,1,0:T(8,128)(2,1)S(1)} %get-tuple-element.249), channel_id=1, source_target_pairs={{0,1},{1,2},{2,3},{3,0},{4,5},{5,6},{6,7},{7,4},{8,9},{9,10},{10,1... | collective-permute-start | bytes 710408 | tf_op jit(solution)/shard_map/ppermute | solution.py:1138
  695.0 20.9 %collective-permute-start.10 = (bf16[1,200,592]{2,1,0:T(8,128)(2,1)S(1)}, bf16[1,200,592]{2,1,0:T(8,128)(2,1)S(1)}, u32[]{:S(2)}, u32[]{:S(2)}) collective-permute-start(bf16[1,200,592]{2,1,0:T(8,128)(2,1)S(1)} %get-tuple-element.247), channel_id=1, source_target_pairs={{0,2},{1,3},{2,0},{3,1},{4,6},{5,7},{6,4},{7,5},{8,10},{9,11},{10,... | collective-permute-start | bytes 710408 | tf_op jit(solution)/shard_map/ppermute | solution.py:1138
  720.5 7.0 collective-permute-start.15
  722.0 5.5 collective-permute-start.14
  722.5 5.0 collective-permute-start.13
  (56 other events, 307.3 us)
Sparse Core Ops, SparseCore 0:
  15.5 56.2 all-gather.3
  74.2 62.2 all-gather.7
  141.2 103.8 all-gather.5
  329.5 59.5 reduce-scatter.6
  392.5 98.3 reduce-scatter.12
  526.7 90.6 reduce-scatter.8
  629.2 69.6 reduce-scatter.10

commit v5 on v4

--- a/solution.py
+++ b/solution.py
@@ -225,7 +225,7 @@
 ):
     tile, tiles = pl.program_id(0), pl.num_programs(0)
     begin, step_line, finish = line_sum_steps(
-        count, source, own, sent, got, total_out, loads, send_sems, recv_sems
+        count, source.at[: total_out.shape[0]], own, sent, got, total_out, loads, send_sems, recv_sems
     )
 
     @pl.when(tile == 0)
@@ -293,7 +293,7 @@
 ):
     tile, tiles = pl.program_id(0), pl.num_programs(0)
     begin, step_line, finish = line_sum_steps(
-        count, source, own, sent, got, total_out, loads, send_sems, recv_sems
+        count, source.at[source.shape[0] - total_out.shape[0] :], own, sent, got, total_out, loads, send_sems, recv_sems
     )
 
     @pl.when(tile == 0)
@@ -469,8 +469,8 @@
     )(mixed, *side, skip, start)
 
 
-def end_adjoint(gated_grad, mixed, side, source, count, collective):
-    height, each = source.shape[0], source.shape[1] // count
+def end_adjoint(gated_grad, mixed, side, source, height, count, collective):
+    each = source.shape[1] // count
     tokens, channels = mixed.shape[0], (mixed.shape[1] - HEAD) // 3
     tiles, mixed_s, rows, states, side_s, row, state = scan_specs(tokens, channels, True)
     return scan_call(
@@ -490,8 +490,8 @@
     )(gated_grad, mixed, *side, source)
 
 
-def backward_scan(gated_grad, mixed, states, side, skip, start, final, source, count, collective):
-    height, each = source.shape[0], source.shape[1] // count
+def backward_scan(gated_grad, mixed, states, side, skip, start, final, source, height, count, collective):
+    each = source.shape[1] // count
     tokens, channels = mixed.shape[0], (mixed.shape[1] - HEAD) // 3
     tiles, mixed_s, rows, states_s, side_s, row, state = scan_specs(tokens, channels, True)
     return scan_call(
@@ -809,6 +809,9 @@
         rest = jnp.where(place < count - 1 - place, q, count - 1 - q)
         return jnp.where(q <= 2 * near, spread_out, rest)
 
+    def reach(q):
+        return jnp.where(q <= 2 * near, (q + 1) // 2, q - near)
+
     def load(what, where, k):
         return pltpu.make_async_copy(what, where, loads.at[k])
 
@@ -831,12 +834,12 @@
     def one(q, carry):
         owner, slot = owner_of(q), q % 2
         for far in range(1, count):
-            for side in (0, 1):
-                here = place - far if side == 0 else place + far
-
-                @pl.when((q > 0) & (owner == here))
-                def _():
+
+            @pl.when((reach(q) == far) & (reach(q - 1) < far))
+            def _():
+                for side in (0, 1):
                     receive(side, far - 1)
+                for side in (0, 1):
                     if far < count - 1:
                         send(side, far)
 
@@ -921,6 +924,106 @@
             vmem_limit_bytes=56 << 20, collective_id=collective, has_side_effects=True
         ),
     )(source, other, weights)
+
+
+def wide_sum_kernel(
+    count,
+    ups,
+    downs,
+    tokens,
+    others,
+    gate_up_grad,
+    hidden,
+    hidden_rows,
+    maps,
+    source,
+    wide,
+    out_part,
+    total,
+    own,
+    sent,
+    got,
+    loads,
+    send_sems,
+    recv_sems,
+):
+    step, steps = pl.program_id(0), pl.num_programs(0)
+    start, advance, finish = line_sum_steps(
+        count, source, own, sent, got, total, loads, send_sems, recv_sems
+    )
+
+    @pl.when(step == 0)
+    def _():
+        start()
+
+    for k in range(1, count - 1):
+
+        @pl.when(step == steps * k // (count - 1))
+        def _():
+            advance(k)
+
+    @pl.when(step < ups)
+    def _():
+        wide[...] = mm(tokens[...], gate_up_grad[...]).astype(bf16)
+
+    @pl.when((step >= ups) & (step < ups + downs))
+    def _():
+        wide[...] = mm(others[...], hidden[...]).astype(bf16)
+
+    @pl.when(step >= ups + downs)
+    def _():
+        out_part[...] = mm_nt(maps[...], hidden_rows[...]).astype(bf16)
+
+    @pl.when(step == steps - 1)
+    def _():
+        advance(count - 1)
+        finish()
+
+
+def wide_sum(tokens, others, gate_up_grad, hidden, maps, source, count, collective):
+    depth, span = tokens.shape
+    ff = hidden.shape[1]
+    ups, downs, strip = 2 * ff // 128, ff // 128, 320
+    strips = depth // strip
+    each = source.shape[1] // count
+
+    def strip_of(j):
+        return jnp.clip(j - ups - downs, 0, strips - 1)
+
+    def whole(*shape):
+        return pl.BlockSpec(shape, lambda j: (0, 0), pipeline_mode=pl.Buffered(1))
+
+    return pl.pallas_call(
+        functools.partial(wide_sum_kernel, count, ups, downs),
+        name="wide_sum",
+        grid=(ups + downs + strips,),
+        in_specs=[
+            whole(depth, span),
+            whole(depth, span),
+            pl.BlockSpec((span, 128), lambda j: (0, jnp.minimum(j, ups - 1))),
+            pl.BlockSpec((span, 128), lambda j: (0, jnp.clip(j - ups, 0, downs - 1))),
+            whole(span, ff),
+            pl.BlockSpec((strip, ff), lambda j: (strip_of(j), 2)),
+            pl.BlockSpec(memory_space=pl.ANY),
+        ],
+        out_specs=[
+            pl.BlockSpec((depth, 128), lambda j: (0, jnp.minimum(j, ups + downs - 1))),
+            pl.BlockSpec((strip, span), lambda j: (strip_of(j), 0)),
+            pl.BlockSpec((depth, each), lambda j: (0, 0)),
+        ],
+        out_shape=[
+            jax.ShapeDtypeStruct((depth, 3 * ff), bf16),
+            jax.ShapeDtypeStruct((depth, span), bf16),
+            jax.ShapeDtypeStruct((depth, each), f32),
+        ],
+        scratch_shapes=line_sum_scratch(count, depth, each),
+        compiler_params=pltpu.CompilerParams(
+            vmem_limit_bytes=48 << 20,
+            dimension_semantics=("arbitrary",),
+            collective_id=collective,
+            has_side_effects=True,
+        ),
+    )(tokens, others, gate_up_grad, hidden, hidden, maps, source)
 
 
 def attend_kernel(
@@ -1323,17 +1426,9 @@
     ffn_normed_group_t, gate_up_grad, hidden, ffn_grad_part_t = feed_forward(
         ffn_normed_t, cotangent_group_t, third, ff_wide, tp, 1
     )
-    ffn_normed_grad_t = lax.psum_scatter(ffn_grad_part_t, "tp", scatter_dimension=1, tiled=True)
-    up_wide = dot(ffn_normed_group_t, gate_up_grad, 1, 0).astype(bf16)
-    down_wide = dot(cotangent_group_t, hidden, 1, 0).astype(bf16)
-    ffn_wide = jnp.concatenate([up_wide, down_wide], axis=1)
-    fourth = width // 4 // 16 * 16
-    out_parts = [
-        dot(down_map[:fourth], hidden, 1, 1).astype(bf16),
-        dot(down_map[fourth:], hidden, 1, 1).astype(bf16),
-    ]
-    ffn_normed_grad_t, ffn_wide, out_parts = lax.optimization_barrier(
-        (ffn_normed_grad_t, ffn_wide, out_parts)
+    fourth = width // 6 // 16 * 16
+    ffn_wide, out_part_t, ffn_normed_grad_t = wide_sum(
+        ffn_normed_group_t, cotangent_group_t, gate_up_grad, hidden, third, ffn_grad_part_t, tp, 7
     )
     ffn_columns = scatter_rows(ffn_wide)
 
@@ -1367,7 +1462,9 @@
     keyval_part_t = current.astype(bf16)
     keyval_meta_t = keyval_grad_t[:, :meta_count]
     gated_grad = dot(mamba_grad_group_t, state_out_map, 0, 0)
-    adjoint_end, out_head = end_adjoint(gated_grad, mixed, side, out_parts[0], tp, 6)
+    adjoint_end, out_head = end_adjoint(
+        gated_grad, mixed, side, out_part_t, fourth, tp, 6
+    )
     adjoint_end, late_attended_t, late_gated, query_pieces = lax.optimization_barrier(
         (adjoint_end, attended_t, gated, query_pieces)
     )
@@ -1405,7 +1502,8 @@
         skip_row,
         adjoint_start,
         state_final,
-        out_parts[1],
+        out_part_t,
+        width - fourth,
         tp,
         5,
     )

time: 748 us -> 737 us (0.985)
  the two profiles are of different devices: /device:TPU:0 before, /device:TPU:14 now
where the time goes in v5:
time: 737 us; the launch traced here: 726 us
  Pallas kernels  453 us (61%)
  matrix products  112 us (15%)
  local copies, waits for them, and re-layouts  50.3 us (7%)
  other arithmetic  42.3 us (6%)
  starting transfers between devices  29.2 us (4%)
  waiting for transfers between devices  23 us (3%)
  between operations  16.7 us (2%)
    dot_general x18, matrix products, dot(): lax.dot_general(left, right, (((left_dim,), (right_dim,)), ((), ())), pre...  112 us
    pallas_call x1, Pallas kernels, wide_sum(): pl.pallas_call(functools.partial(wide_sum_kernel, count, ups, downs), nam...  71.5 us
    pallas_call x1, Pallas kernels, attend(): pl.pallas_call(functools.partial(attend_kernel, group, count), name='atte...  59.4 us
    pallas_call x1, Pallas kernels, line_sum(): pl.pallas_call(functools.partial(line_sum_kernel, count), name='line_sum'...  58.4 us
    pallas_call x1, Pallas kernels, feed_forward(): pl.pallas_call(functools.partial(feed_kernel, count, tuple(blocks)), name...  57.7 us
    pallas_call x1, Pallas kernels, backward_scan(): scan_call(functools.partial(backward_kernel, count), 'backward_scan', til...  57 us
    pallas_call x1, Pallas kernels, line_gather(): pl.pallas_call(functools.partial(line_gather_kernel, count), name='line_g...  56.4 us
    pallas_call x1, Pallas kernels, attend_back(): pl.pallas_call(functools.partial(attend_back_kernel, group, count), name=...  53.6 us
  transfers between devices with their start and end apart: 22, of which 5 were waited for; matrix products, arithmetic and copies ran while one was open for 23% of the time, Pallas kernels for 45%

profile of v5, /device:TPU:14, one launch (start us, length us, event | category | flops | bytes accessed | tf_op | source)
XLA Modules:
  0.0 726.3 jit_solution(9962314343884351461)
XLA Ops:
  12.9 3.4 concatenate.55
  17.2 56.4 %line_gather.1 = bf16[1600,1024]{1,0:T(8,128)(2,1)} custom-call(bf16[1600,256]{1,0:T(8,128)(2,1)} %bitcast.91), custom_call_target="tpu_custom_call" | custom-call | tf_op jit(solution)/shard_map/line_gather/pallas_call | solution.py:634
  75.2 3.3 collective-permute-start.2
  91.6 13.1 %fusion.136.mixed = f32[1024,2528]{1,0:T(8,128)S(1)} fusion(bf16[1600,2528]{1,0:T(8,128)(2,1)} %all-gather.4.cloned.1.call-done, bf16[1600,1024]{1,0:T(8,128)(2,1)S(1)} %copy-done.26, f32[1600]{0:T(1024)S(1)} %get-tuple-element.217, f32[1024]{0:T(1024)S(1)} %add_rsqrt_fusion), kind=kOutput, calls=%fused_computation.283 | convolution fusion | flops 8290304000 | bytes 21731584 | tf_op jit(solution)/shard_map/dot_general | solution.py:1220
  104.7 9.3 %end_state.1 = f32[16,800]{1,0:T(8,128)S(1)} custom-call(f32[1024,2528]{1,0:T(8,128)S(1)} %fusion.136.mixed, f32[1024,8]{1,0:T(8,128)S(1)} %copy.116.aux, f32[8,1024]{1,0:T(8,128)S(1)} %stack.43.aux_t, f32[256,1]{1,0:T(8,128)S(1)} %fusion.110.alive_last, f32[1,800]{1,0:T(1,128)S(1)} %broadcast_in_dim.166.bias, f32[1,800]{1,0:T(1,128)S(1)} %broadcast_in_dim.167.rate, ...), custom_call_target="tpu_custom_call" | custom-call | flops 10000000 | bytes 100000 | tf_op jit(solution)/shard_map/end_state/pallas_call | solution.py:441
  117.1 4.0 fusion.36
  121.1 4.0 copy-done.3
  125.1 13.4 %forward_scan.1 = (bf16[1024,800]{1,0:T(8,128)(2,1)S(1)}, bf16[4096,800]{1,0:T(8,128)(2,1)S(1)}, f32[16,800]{1,0:T(8,128)S(1)}) custom-call(f32[1024,2528]{1,0:T(8,128)S(1)} %copy-done.3, f32[1024,8]{1,0:T(8,128)S(1)} %copy.116.aux, f32[8,1024]{1,0:T(8,128)S(1)} %stack.43.aux_t, f32[256,1]{1,0:T(8,128)S(1)} %fusion.110.alive_last, ...), custom_call_target="tpu_custom_call" | custom-call | flops 10000000 | bytes 100000 | tf_op jit(solution)/shard_map/forward_scan/pallas_call | solution.py:456
  153.3 6.4 convolution_convert_fusion.4
  165.5 5.5 convolution_convert_fusion.1.source
  173.1 59.4 %attend.1 = (bf16[1600,256]{1,0:T(8,128)(2,1)}, f32[5,8,256]{2,1,0:T(8,128)}, f32[1600,256]{1,0:T(8,128)}) custom-call(bf16[1600,256]{1,0:T(8,128)(2,1)} %fusion.25.query_t, bf16[640,1408]{1,0:T(8,128)(2,1)} %pad_maximum_fusion.1.key_t.value_t, bf16[640,1408]{1,0:T(8,128)(2,1)} %pad_maximum_fusion.1.key_t.value_t, f32[1408,256]{1,0:T(8,128)} %concatenate.64.bias, ...), custom_call_target="tpu_custom_call" | custom-call | tf_op jit(solution)/shard_map/attend/pallas_call | solution.py:1138
  234.2 9.4 %all-gather.6.cloned.1.call-done.weights.maps = bf16[1600,5824]{1,0:T(8,128)(2,1)} async-done(((bf16[200,5824]{1,0:T(8,128)(2,1)}), bf16[1600,5824]{1,0:T(8,128)(2,1)}) %all-gather.6.cloned.1.call-update) | async-done | bytes 18636816 | tf_op jit(solution)/shard_map/all_gather | solution.py:1226
  243.6 4.6 multiply_reduce_fusion.8
  250.8 57.7 %feed_forward.1 = (bf16[1600,1024]{1,0:T(8,128)(2,1)}, bf16[1024,2816]{1,0:T(8,128)(2,1)}, bf16[1024,1408]{1,0:T(8,128)(2,1)}, bf16[1600,1024]{1,0:T(8,128)(2,1)}) custom-call(bf16[1600,256]{1,0:T(8,128)(2,1)} %multiply_convert_fusion.2.source, bf16[1600,1024]{1,0:T(8,128)(2,1)} %pad_maximum_fusion.other.others, ...), custom_call_target="tpu_custom_call" | custom-call | tf_op jit(solution)/shard_map/feed_forward/pallas_call | solution.py:899
  310.4 71.5 %wide_sum.1 = (bf16[1600,4224]{1,0:T(8,128)(2,1)}, bf16[1600,1024]{1,0:T(8,128)(2,1)}, f32[1600,256]{1,0:T(8,128)S(1)}) custom-call(bf16[1600,1024]{1,0:T(8,128)(2,1)} %get-tuple-element.98.tokens, bf16[1600,1024]{1,0:T(8,128)(2,1)} %pad_maximum_fusion.other.others, bf16[1024,2816]{1,0:T(8,128)(2,1)} %get-tuple-element.99.gate_up_grad, ...), custom_call_target="tpu_custom_call" | custom-call | tf_op jit(solution)/shard_map/wide_sum/pallas_call | solution.py:996
  384.6 3.4 multiply_reduce_fusion.1
  389.8 6.5 fusion.22.grad_t
  396.2 53.6 %attend_back.1 = (bf16[1600,256]{1,0:T(8,128)(2,1)}, bf16[2,320,1408]{2,1,0:T(8,128)(2,1)}, bf16[1600,1024]{1,0:T(8,128)(2,1)}) custom-call(bf16[1600,256]{1,0:T(8,128)(2,1)} %fusion.25.query_t, bf16[640,1408]{1,0:T(8,128)(2,1)} %pad_maximum_fusion.1.key_t.value_t, bf16[640,1408]{1,0:T(8,128)(2,1)} %pad_maximum_fusion.1.key_t.value_t, ...), custom_call_target="tpu_custom_call" | custom-call | tf_op jit(solution)/shard_map/attend_back/pallas_call | solution.py:1177
  451.9 4.4 collective-permute-start.6
  463.6 6.3 fusion.28.gated_grad
  469.9 16.7 %end_adjoint.1 = (f32[16,800]{1,0:T(8,128)S(1)}, f32[256,256]{1,0:T(8,128)S(1)}) custom-call(f32[1024,800]{1,0:T(8,128)S(1)} %fusion.28.gated_grad, f32[1024,2528]{1,0:T(8,128)S(1)} %bitcast.89, f32[1024,8]{1,0:T(8,128)S(1)} %copy.116.aux, f32[8,1024]{1,0:T(8,128)S(1)} %stack.43.aux_t, f32[256,1]{1,0:T(8,128)S(1)} %fusion.110.alive_last, ...), custom_call_target="tpu_custom_call" | custom-call | flops 10000000000 | bytes 100000000 | tf_op jit(solution)/shard_map/end_adjoint/pallas_call | solution.py:476
  486.7 4.1 fusion.2
  496.3 4.3 fusion.20
  500.7 4.9 fusion.19
  507.0 5.5 fusion.43
  513.8 7.2 fusion.52
  523.6 57.0 %backward_scan.1 = (bf16[1024,2528]{1,0:T(8,128)(2,1)}, f32[8,800]{1,0:T(8,128)S(1)}, f32[1344,256]{1,0:T(8,128)S(1)}) custom-call(f32[1024,800]{1,0:T(8,128)} %copy-done.10, f32[1024,2528]{1,0:T(8,128)} %copy-done.2, bf16[4096,800]{1,0:T(8,128)(2,1)} %copy-done.5, f32[1024,8]{1,0:T(8,128)S(1)} %copy.116.aux, f32[8,1024]{1,0:T(8,128)S(1)} %stack.43.aux_t, ...), custom_call_target="tpu_custom_call" | custom-call | flops 35999997952 | bytes 360000000 | tf_op jit(solution)/shard_map/backward_scan/pallas_call | solution.py:497
  580.7 17.0 %fusion.4 = (f32[1600]{0:T(1024)S(1)}, bf16[1600,1024]{1,0:T(8,128)(2,1)}) fusion(bf16[1600,1024]{1,0:T(8,128)(2,1)} %line_gather.1, f32[1024]{0:T(1024)S(1)} %add_rsqrt_fusion, f32[1600,1024]{1,0:T(8,128)} %fusion.52, bf16[1600,2528]{1,0:T(8,128)(2,1)} %all-gather.4.cloned.1.call-done, bf16[1024,2528]{1,0:T(8,128)(2,1)} %get-tuple-element.124), kind=kOutput, calls=%fused_computation.12 | convolution fusion | flops 8293579264 | bytes 26384640 | tf_op jit(solution)/shard_map/dot_general | solution.py:1220
  598.7 14.1 %add_convert_fusion = bf16[1600,2528]{1,0:T(8,128)(2,1)} fusion(f32[1600,16]{1,0:T(8,128)S(1)} %copy.129, bf16[1024,2528]{1,0:T(8,128)(2,1)} %get-tuple-element.124, bf16[1600,1024]{1,0:T(8,128)(2,1)} %line_gather.1, f32[1600]{0:T(1024)S(1)} %get-tuple-element.217, f32[1024]{0:T(1024)S(1)} %add_rsqrt_fusion), kind=kOutput, calls=%fused_computation | convolution fusion | flops 8298393600 | bytes 16656640 | tf_op jit(solution)/shard_map/dot_general | solution.py:1220
  620.8 58.4 %line_sum.1 = f32[1600,256]{1,0:T(8,128)S(1)} custom-call(bf16[1600,1024]{1,0:T(8,128)(2,1)S(1)} %copy-done.11), custom_call_target="tpu_custom_call" | custom-call | flops 49999998976 | bytes 16777216 | tf_op jit(solution)/shard_map/line_sum/pallas_call | solution.py:764
  693.6 5.4 collective-permute-done.12
  707.8 5.2 collective-permute-start.13
  (294 shorter events, 114.3 us)
Async XLA Ops:
  7.2 107.3 %copy-start = (bf16[200,5504]{1,0:T(8,128)(2,1)S(1)}, bf16[200,5504]{1,0:T(8,128)(2,1)}, u32[]{:S(2)}) copy-start(bf16[200,5504]{1,0:T(8,128)(2,1)} %param.37) | copy-start | bytes 6604804
  7.2 81.4 %all-gather.4.cloned.1.call-start = ((), (), s32[]{:S(2)}) async-start(), calls=%async_computation.3 | async-start | bytes 9216000 | tf_op jit(solution)/shard_map/all_gather | solution.py:1226
  16.4 137.0 %all-gather.8.cloned.1.call-start = ((), (), s32[]{:S(2)}) async-start(), calls=%async_computation.5 | async-start | bytes 11520000 | tf_op jit(solution)/shard_map/all_gather | solution.py:1226
  17.1 62.0 %copy-start.39 = (s32[1,2048]{1,0:T(1,128)S(1)}, s32[1,2048]{1,0:T(1,128)}, u32[]{:S(2)}) copy-start(s32[1,2048]{1,0:T(1,128)} %param.20) | copy-start | bytes 24580
  17.1 66.5 %copy-start.41 = (f32[800]{0:T(1024)S(1)}, f32[800]{0:T(1024)}, u32[]{:S(2)}) copy-start(f32[800]{0:T(1024)} %param.30) | copy-start | bytes 9604
  17.2 66.5 %copy-start.40 = (f32[800]{0:T(1024)S(1)}, f32[800]{0:T(1024)}, u32[]{:S(2)}) copy-start(f32[800]{0:T(1024)} %param.31) | copy-start | bytes 9604
  17.2 66.5 %copy-start.42 = (f32[800]{0:T(1024)S(1)}, f32[800]{0:T(1024)}, u32[]{:S(2)}) copy-start(f32[800]{0:T(1024)} %param.32) | copy-start | bytes 9604
  17.2 226.4 %all-gather.6.cloned.1.call-start = ((), (), s32[]{:S(2)}) async-start(), calls=%async_computation.4 | async-start | bytes 21196800 | tf_op jit(solution)/shard_map/all_gather | solution.py:1226
  73.6 67.8 %collective-permute-start.1 = (bf16[1600,256]{1,0:T(8,128)(2,1)}, bf16[1600,256]{1,0:T(8,128)(2,1)}, u32[]{:S(2)}, u32[]{:S(2)}) collective-permute-start(bf16[1600,256]{1,0:T(8,128)(2,1)} %bitcast.6), channel_id=1, source_target_pairs={{0,1},{1,2},{2,3},{3,0},{4,5},{5,6},{6,7},{7,4},{8,9},{9,10},{10,1... | collective-permute-start | bytes 2457608 | tf_op jit(solution)/shard_map/ppermute | solution.py:1241
  75.2 68.3 %collective-permute-start.2 = (bf16[1600,256]{1,0:T(8,128)(2,1)}, bf16[1600,256]{1,0:T(8,128)(2,1)}, u32[]{:S(2)}, u32[]{:S(2)}) collective-permute-start(bf16[1600,256]{1,0:T(8,128)(2,1)} %bitcast.6), channel_id=1, source_target_pairs={{0,2},{1,3},{2,0},{3,1},{4,6},{5,7},{6,4},{7,5},{8,10},{9,11},{10,... | collective-permute-start | bytes 2457608 | tf_op jit(solution)/shard_map/ppermute | solution.py:1241
  78.5 68.1 %collective-permute-start.3 = (bf16[1600,256]{1,0:T(8,128)(2,1)}, bf16[1600,256]{1,0:T(8,128)(2,1)}, u32[]{:S(2)}, u32[]{:S(2)}) collective-permute-start(bf16[1600,256]{1,0:T(8,128)(2,1)} %bitcast.6), channel_id=1, source_target_pairs={{0,3},{1,0},{2,1},{3,2},{4,7},{5,4},{6,5},{7,6},{8,11},{9,8},{10,9... | collective-permute-start | bytes 2457608 | tf_op jit(solution)/shard_map/ppermute | solution.py:1241
  89.9 24.1 %slice-start.3 = ((s8[4403200]{0:T(1024)(128)(4,1)}), s8[4194304]{0:T(1024)(128)(4,1)S(1)}, s32[]{:S(2)}) async-start(s8[4403200]{0:T(1024)(128)(4,1)} %bitcast.98), calls=%async_computation.12 | async-start | bytes 8388608
  115.5 5.6 collective-permute-start
  141.5 24.0 %copy-start.8 = (bf16[1024,800]{1,0:T(8,128)(2,1)}, bf16[1024,800]{1,0:T(8,128)(2,1)S(1)}, u32[]{:S(2)}) copy-start(bf16[1024,800]{1,0:T(8,128)(2,1)S(1)} %get-tuple-element.116) | copy-start | bytes 4915204
  146.7 374.3 %reduce-scatter.10.cloned.1.call-start = ((), (), s32[]{:S(2)}) async-start(), calls=%async_computation.8 | async-start | bytes 15206400
  159.7 11.2 %collective-permute-start.4 = (bf16[640,1024]{1,0:T(8,128)(2,1)S(1)}, bf16[640,1024]{1,0:T(8,128)(2,1)S(1)}, u32[]{:S(2)}, u32[]{:S(2)}) collective-permute-start(bf16[640,1024]{1,0:T(8,128)(2,1)S(1)} %convolution_convert_fusion.4), channel_id=1, source_target_pairs={{0,4},{1,5},{2,6},{3,7},{8,12},{9,13},{10,14},{11,15},{16,20},{17,... | collective-permute-start | bytes 3932168 | tf_op jit(solution)/shard_map/ppermute | solution.py:1381
  249.4 59.1 %copy-start.12 = (f32[1600,256]{1,0:T(8,128)}, f32[1600,256]{1,0:T(8,128)S(1)}, u32[]{:S(2)}) copy-start(f32[1600,256]{1,0:T(8,128)S(1)} %get-tuple-element.223) | copy-start | bytes 4915204
  381.8 231.0 %reduce-scatter.6.cloned.1.call-start = ((), (), s32[]{:S(2)}) async-start(), calls=%async_computation.6 | async-start | bytes 13824000 | tf_op jit(solution)/shard_map/reduce_scatter | solution.py:1235
  451.4 35.2 %collective-permute-start.5 = (bf16[400,256]{1,0:T(8,128)(2,1)S(1)}, bf16[400,256]{1,0:T(8,128)(2,1)S(1)}, u32[]{:S(2)}, u32[]{:S(2)}) collective-permute-start(bf16[400,256]{1,0:T(8,128)(2,1)S(1)} %get-tuple-element.254), channel_id=1, source_target_pairs={{0,1},{1,2},{2,3},{3,0},{4,5},{5,6},{6,7},{7,4},{8,9},{9,10},{10,1... | collective-permute-start | bytes 614408 | tf_op jit(solution)/shard_map/ppermute | solution.py:1241
  451.9 34.8 %collective-permute-start.6 = (bf16[400,256]{1,0:T(8,128)(2,1)S(1)}, bf16[400,256]{1,0:T(8,128)(2,1)S(1)}, u32[]{:S(2)}, u32[]{:S(2)}) collective-permute-start(bf16[400,256]{1,0:T(8,128)(2,1)S(1)} %get-tuple-element.253), channel_id=1, source_target_pairs={{0,2},{1,3},{2,0},{3,1},{4,6},{5,7},{6,4},{7,5},{8,10},{9,11},{10,... | collective-permute-start | bytes 614408 | tf_op jit(solution)/shard_map/ppermute | solution.py:1241
  456.2 30.4 %collective-permute-start.7 = (bf16[400,256]{1,0:T(8,128)(2,1)S(1)}, bf16[400,256]{1,0:T(8,128)(2,1)S(1)}, u32[]{:S(2)}, u32[]{:S(2)}) collective-permute-start(bf16[400,256]{1,0:T(8,128)(2,1)S(1)} %get-tuple-element.252), channel_id=1, source_target_pairs={{0,3},{1,0},{2,1},{3,2},{4,7},{5,4},{6,5},{7,6},{8,11},{9,8},{10,9... | collective-permute-start | bytes 614408 | tf_op jit(solution)/shard_map/ppermute | solution.py:1241
  456.8 39.6 %copy-start.28 = (bf16[640,2048]{1,0:T(8,128)(2,1)}, bf16[640,2048]{1,0:T(8,128)(2,1)S(1)}, u32[]{:S(2)}) copy-start(bf16[640,2048]{1,0:T(8,128)(2,1)S(1)} %slice_dynamic-update-slice_fusion) | copy-start | bytes 7864324
  456.9 39.4 %collective-permute-start.9 = (bf16[640,1024]{1,0:T(8,128)(2,1)S(1)}, bf16[640,1024]{1,0:T(8,128)(2,1)S(1)}, u32[]{:S(2)}, u32[]{:S(2)}) collective-permute-start(bf16[640,1024]{1,0:T(8,128)(2,1)S(1)} %slice.222), channel_id=1, source_target_pairs={{4,0},{5,1},{6,2},{7,3},{12,8},{13,9},{14,10},{15,11},{20,16},{21,... | collective-permute-start | bytes 3932168 | tf_op jit(solution)/shard_map/ppermute | solution.py:1460
  505.6 198.2 %reduce-scatter.8.cloned.1.call-start = ((), (), s32[]{:S(2)}) async-start(), calls=%async_computation.7 | async-start | bytes 9216000 | tf_op jit(solution)/shard_map/reduce_scatter | solution.py:1235
  512.5 8.5 %collective-permute-start.8 = (f32[16,800]{1,0:T(8,128)S(1)}, f32[16,800]{1,0:T(8,128)S(1)}, u32[]{:S(2)}, u32[]{:S(2)}) collective-permute-start(f32[16,800]{1,0:T(8,128)S(1)} %get-tuple-element.109), channel_id=1, source_target_pairs={{4,0},{5,1},{6,2},{7,3},{12,8},{13,9},{14,10},{15,11},{20,16},{21,... | collective-permute-start | bytes 153608 | tf_op jit(solution)/shard_map/ppermute | solution.py:1471
  620.8 58.4 %copy-start.32 = (f32[1600,256]{1,0:T(8,128)S(1)}, f32[1600,256]{1,0:T(8,128)}, u32[]{:S(2)}) copy-start(f32[1600,256]{1,0:T(8,128)} %get-tuple-element.274) | copy-start | bytes 4915204
  679.6 19.4 %collective-permute-start.12 = (bf16[1,200,592]{2,1,0:T(8,128)(2,1)S(1)}, bf16[1,200,592]{2,1,0:T(8,128)(2,1)S(1)}, u32[]{:S(2)}, u32[]{:S(2)}) collective-permute-start(bf16[1,200,592]{2,1,0:T(8,128)(2,1)S(1)} %get-tuple-element.246), channel_id=1, source_target_pairs={{0,3},{1,0},{2,1},{3,2},{4,7},{5,4},{6,5},{7,6},{8,11},{9,8},{10,9... | collective-permute-start | bytes 710408 | tf_op jit(solution)/shard_map/ppermute | solution.py:1241
  680.0 18.9 %collective-permute-start.11 = (bf16[1,200,592]{2,1,0:T(8,128)(2,1)S(1)}, bf16[1,200,592]{2,1,0:T(8,128)(2,1)S(1)}, u32[]{:S(2)}, u32[]{:S(2)}) collective-permute-start(bf16[1,200,592]{2,1,0:T(8,128)(2,1)S(1)} %get-tuple-element.247), channel_id=1, source_target_pairs={{0,1},{1,2},{2,3},{3,0},{4,5},{5,6},{6,7},{7,4},{8,9},{9,10},{10,1... | collective-permute-start | bytes 710408 | tf_op jit(solution)/shard_map/ppermute | solution.py:1241
  681.9 19.3 %collective-permute-start.10 = (bf16[1,200,592]{2,1,0:T(8,128)(2,1)S(1)}, bf16[1,200,592]{2,1,0:T(8,128)(2,1)S(1)}, u32[]{:S(2)}, u32[]{:S(2)}) collective-permute-start(bf16[1,200,592]{2,1,0:T(8,128)(2,1)S(1)} %get-tuple-element.245), channel_id=1, source_target_pairs={{0,2},{1,3},{2,0},{3,1},{4,6},{5,7},{6,4},{7,5},{8,10},{9,11},{10,... | collective-permute-start | bytes 710408 | tf_op jit(solution)/shard_map/ppermute | solution.py:1241
  705.7 12.1 %collective-permute-start.15 = (bf16[1,200,12]{1,2,0:T(8,128)(2,1)S(1)}, bf16[1,200,12]{1,2,0:T(8,128)(2,1)S(1)}, u32[]{:S(2)}, u32[]{:S(2)}) collective-permute-start(bf16[1,200,12]{1,2,0:T(8,128)(2,1)S(1)} %get-tuple-element.260), channel_id=1, source_target_pairs={{0,3},{1,0},{2,1},{3,2},{4,7},{5,4},{6,5},{7,6},{8,11},{9,8},{10,9... | collective-permute-start | bytes 14408 | tf_op jit(solution)/shard_map/ppermute | solution.py:1241
  707.7 10.1 %collective-permute-start.14 = (bf16[1,200,12]{1,2,0:T(8,128)(2,1)S(1)}, bf16[1,200,12]{1,2,0:T(8,128)(2,1)S(1)}, u32[]{:S(2)}, u32[]{:S(2)}) collective-permute-start(bf16[1,200,12]{1,2,0:T(8,128)(2,1)S(1)} %get-tuple-element.259), channel_id=1, source_target_pairs={{0,1},{1,2},{2,3},{3,0},{4,5},{5,6},{6,7},{7,4},{8,9},{9,10},{10,1... | collective-permute-start | bytes 14408 | tf_op jit(solution)/shard_map/ppermute | solution.py:1241
  707.8 10.1 %collective-permute-start.13 = (bf16[1,200,12]{1,2,0:T(8,128)(2,1)S(1)}, bf16[1,200,12]{1,2,0:T(8,128)(2,1)S(1)}, u32[]{:S(2)}, u32[]{:S(2)}) collective-permute-start(bf16[1,200,12]{1,2,0:T(8,128)(2,1)S(1)} %get-tuple-element.258), channel_id=1, source_target_pairs={{0,2},{1,3},{2,0},{3,1},{4,6},{5,7},{6,4},{7,5},{8,10},{9,11},{10,... | collective-permute-start | bytes 14408 | tf_op jit(solution)/shard_map/ppermute | solution.py:1241
  (43 other events, 216.3 us)
Sparse Core Ops, SparseCore 0:
  16.5 53.7 all-gather.3
  72.7 62.2 all-gather.7
  146.8 96.7 all-gather.5
  382.0 97.2 reduce-scatter.9
  505.7 91.5 reduce-scatter.5
  613.0 69.7 reduce-scatter.7

commit v6 on v5

--- a/solution.py
+++ b/solution.py
@@ -68,12 +68,12 @@
 
 def part(mixed, k):
     channels = (mixed.shape[1] - HEAD) // 3
-    return mixed[:, HEAD + k * channels : HEAD + (k + 1) * channels]
+    return mixed[:, HEAD + k * channels : HEAD + (k + 1) * channels].astype(f32)
 
 
 def both_ways(mixed):
     head = mixed[:, :HEAD]
-    return head.astype(bf16), head.T.astype(bf16)
+    return head, head.astype(f32).T.astype(bf16)
 
 
 def decays(step_raw, bias_ref, rate_ref, alive_last_ref, sums_ref):
@@ -1352,7 +1352,7 @@
     meta_rows = meta_full.astype(f32)
     meta_normed_t = rms_norm(meta_rows, mix_gain).astype(bf16)
 
-    mixed = dot(normed_group_t, first, 0, 0)
+    mixed = dot(normed_group_t, first, 0, 0).astype(bf16)
     seg_current = lax.dynamic_slice_in_dim(segments, ctx_index * span, span, 0)
     seg_earlier = lax.dynamic_slice_in_dim(segments, jnp.maximum(ctx_index - 1, 0) * span, span, 0)
     seg_before = jnp.where(
@@ -1509,7 +1509,8 @@
     )
     layer_out_t = (mid + jnp.concatenate([out_head, out_rest], axis=0)).astype(bf16)
     query_term = dot(query_map, query_grad_t, 1, 0)
-    normed_grad_part = dot(first, mix_grad, 1, 1) + dot(keyval_map, keyval_part_t, 1, 0)
+    keyval_term = dot(keyval_map, keyval_part_t, 1, 0).astype(bf16)
+    normed_grad_part = dot(first, mix_grad, 1, 1) + keyval_term.astype(f32)
     _, group_terms = rms_back(residual_group, mix_gain, normed_grad_part)
     _, query_terms = rms_back(residual, mix_gain, query_term)
     normed_grad_low, mix_grad = lax.optimization_barrier(

time: 737 us -> 729 us (0.989)
  the two profiles are of different devices: /device:TPU:14 before, /device:TPU:0 now
where the time goes in v6:
time: 729 us; the launch traced here: 722 us
  Pallas kernels  465 us (64%)
  matrix products  109 us (15%)
  local copies, waits for them, and re-layouts  48.9 us (7%)
  other arithmetic  42 us (6%)
  starting transfers between devices  22.7 us (3%)
  waiting for transfers between devices  17.6 us (2%)
  between operations  16.5 us (2%)
    dot_general x18, matrix products, dot(): lax.dot_general(left, right, (((left_dim,), (right_dim,)), ((), ())), pre...  109 us
    pallas_call x1, Pallas kernels, feed_forward(): pl.pallas_call(functools.partial(feed_kernel, count, tuple(blocks)), name...  68.9 us
    pallas_call x1, Pallas kernels, attend(): pl.pallas_call(functools.partial(attend_kernel, group, count), name='atte...  67.8 us
    pallas_call x1, Pallas kernels, line_gather(): pl.pallas_call(functools.partial(line_gather_kernel, count), name='line_g...  59.9 us
    pallas_call x1, Pallas kernels, wide_sum(): pl.pallas_call(functools.partial(wide_sum_kernel, count, ups, downs), nam...  58.8 us
    pallas_call x1, Pallas kernels, attend_back(): pl.pallas_call(functools.partial(attend_back_kernel, group, count), name=...  57.7 us
    pallas_call x1, Pallas kernels, line_sum(): pl.pallas_call(functools.partial(line_sum_kernel, count), name='line_sum'...  56.6 us
    pallas_call x1, Pallas kernels, backward_scan(): scan_call(functools.partial(backward_kernel, count), 'backward_scan', til...  55.3 us
  transfers between devices with their start and end apart: 22, of which 2 were waited for; matrix products, arithmetic and copies ran while one was open for 23% of the time, Pallas kernels for 47%

profile of v6, /device:TPU:0, one launch (start us, length us, event | category | flops | bytes accessed | tf_op | source)
XLA Modules:
  0.0 721.6 jit_solution(9653729812119560733)
XLA Ops:
  12.9 3.4 concatenate.55
  17.2 59.9 %line_gather.1 = bf16[1600,1024]{1,0:T(8,128)(2,1)} custom-call(bf16[1600,256]{1,0:T(8,128)(2,1)} %bitcast.91), custom_call_target="tpu_custom_call" | custom-call | tf_op jit(solution)/shard_map/line_gather/pallas_call | solution.py:634
  93.4 13.0 %convolution_convert_fusion.1.mixed = bf16[1024,2528]{1,0:T(8,128)(2,1)S(1)} fusion(bf16[1600,2528]{1,0:T(8,128)(2,1)} %all-gather.4.cloned.1.call-done, bf16[1600,1024]{1,0:T(8,128)(2,1)S(1)} %copy-done.26, f32[1600]{0:T(1024)S(1)} %get-tuple-element.217, f32[1024]{0:T(1024)S(1)} %add_rsqrt_fusion), kind=kOutput, calls=%fused_computation.15 | convolution fusion | flops 8292892672 | bytes 16554240 | tf_op jit(solution)/shard_map/dot_general | solution.py:1220
  106.5 9.5 %end_state.1 = f32[16,800]{1,0:T(8,128)S(1)} custom-call(bf16[1024,2528]{1,0:T(8,128)(2,1)S(1)} %convolution_convert_fusion.1.mixed, f32[1024,8]{1,0:T(8,128)S(1)} %copy.107.aux, f32[8,1024]{1,0:T(8,128)S(1)} %stack.43.aux_t, f32[256,1]{1,0:T(8,128)S(1)} %fusion.110.alive_last, f32[1,800]{1,0:T(1,128)S(1)} %broadcast_in_dim.166.bias, ...), custom_call_target="tpu_custom_call" | custom-call | flops 10000000 | bytes 100000 | tf_op jit(solution)/shard_map/end_state/pallas_call | solution.py:441
  118.8 4.0 fusion.37
  125.3 13.5 %forward_scan.1 = (bf16[1024,800]{1,0:T(8,128)(2,1)S(1)}, bf16[4096,800]{1,0:T(8,128)(2,1)S(1)}, f32[16,800]{1,0:T(8,128)S(1)}) custom-call(bf16[1024,2528]{1,0:T(8,128)(2,1)S(1)} %copy-done.3, f32[1024,8]{1,0:T(8,128)S(1)} %copy.107.aux, f32[8,1024]{1,0:T(8,128)S(1)} %stack.43.aux_t, f32[256,1]{1,0:T(8,128)S(1)} %fusion.110.alive_last, ...), custom_call_target="tpu_custom_call" | custom-call | flops 10000000 | bytes 100000 | tf_op jit(solution)/shard_map/forward_scan/pallas_call | solution.py:456
  148.5 5.5 convolution_convert_fusion.6
  156.9 3.0 fusion.26.query_t
  159.9 5.5 convolution_convert_fusion.3.source
  167.5 67.8 %attend.1 = (bf16[1600,256]{1,0:T(8,128)(2,1)}, f32[5,8,256]{2,1,0:T(8,128)}, f32[1600,256]{1,0:T(8,128)}) custom-call(bf16[1600,256]{1,0:T(8,128)(2,1)} %fusion.26.query_t, bf16[640,1408]{1,0:T(8,128)(2,1)} %pad_maximum_fusion.1.key_t.value_t, bf16[640,1408]{1,0:T(8,128)(2,1)} %pad_maximum_fusion.1.key_t.value_t, f32[1408,256]{1,0:T(8,128)} %concatenate.64.bias, ...), custom_call_target="tpu_custom_call" | custom-call | tf_op jit(solution)/shard_map/attend/pallas_call | solution.py:1138
  237.0 9.1 %all-gather.6.cloned.1.call-done.weights.maps = bf16[1600,5824]{1,0:T(8,128)(2,1)} async-done(((bf16[200,5824]{1,0:T(8,128)(2,1)}), bf16[1600,5824]{1,0:T(8,128)(2,1)}) %all-gather.6.cloned.1.call-update) | async-done | bytes 18636816 | tf_op jit(solution)/shard_map/all_gather | solution.py:1226
  246.1 4.6 multiply_reduce_fusion.8
  253.2 68.9 %feed_forward.1 = (bf16[1600,1024]{1,0:T(8,128)(2,1)}, bf16[1024,2816]{1,0:T(8,128)(2,1)}, bf16[1024,1408]{1,0:T(8,128)(2,1)}, bf16[1600,1024]{1,0:T(8,128)(2,1)}) custom-call(bf16[1600,256]{1,0:T(8,128)(2,1)} %multiply_convert_fusion.2.source, bf16[1600,1024]{1,0:T(8,128)(2,1)} %pad_maximum_fusion.other.others, ...), custom_call_target="tpu_custom_call" | custom-call | tf_op jit(solution)/shard_map/feed_forward/pallas_call | solution.py:899
  323.9 58.8 %wide_sum.1 = (bf16[1600,4224]{1,0:T(8,128)(2,1)}, bf16[1600,1024]{1,0:T(8,128)(2,1)}, f32[1600,256]{1,0:T(8,128)S(1)}) custom-call(bf16[1600,1024]{1,0:T(8,128)(2,1)} %get-tuple-element.98.tokens, bf16[1600,1024]{1,0:T(8,128)(2,1)} %pad_maximum_fusion.other.others, bf16[1024,2816]{1,0:T(8,128)(2,1)} %get-tuple-element.99.gate_up_grad, ...), custom_call_target="tpu_custom_call" | custom-call | tf_op jit(solution)/shard_map/wide_sum/pallas_call | solution.py:996
  385.5 3.4 multiply_reduce_fusion.1
  390.7 6.3 fusion.23.grad_t
  397.0 57.7 %attend_back.1 = (bf16[1600,256]{1,0:T(8,128)(2,1)}, bf16[2,320,1408]{2,1,0:T(8,128)(2,1)}, bf16[1600,1024]{1,0:T(8,128)(2,1)}) custom-call(bf16[1600,256]{1,0:T(8,128)(2,1)} %fusion.26.query_t, bf16[640,1408]{1,0:T(8,128)(2,1)} %pad_maximum_fusion.1.key_t.value_t, bf16[640,1408]{1,0:T(8,128)(2,1)} %pad_maximum_fusion.1.key_t.value_t, ...), custom_call_target="tpu_custom_call" | custom-call | tf_op jit(solution)/shard_map/attend_back/pallas_call | solution.py:1177
  467.1 6.3 fusion.29.gated_grad
  473.4 17.1 %end_adjoint.1 = (f32[16,800]{1,0:T(8,128)S(1)}, f32[256,256]{1,0:T(8,128)S(1)}) custom-call(f32[1024,800]{1,0:T(8,128)S(1)} %fusion.29.gated_grad, bf16[1024,2528]{1,0:T(8,128)(2,1)S(1)} %bitcast.89, f32[1024,8]{1,0:T(8,128)S(1)} %copy.107.aux, f32[8,1024]{1,0:T(8,128)S(1)} %stack.43.aux_t, f32[256,1]{1,0:T(8,128)S(1)} %fusion.110.alive_last, ...), custom_call_target="tpu_custom_call" | custom-call | flops 10000000000 | bytes 100000000 | tf_op jit(solution)/shard_map/end_adjoint/pallas_call | solution.py:476
  490.6 4.2 fusion.2
  494.9 3.2 fusion.22
  500.3 4.3 fusion.21
  504.6 4.9 fusion.20
  510.9 6.0 fusion.44
  518.2 6.3 convolution_convert_fusion.2
  527.0 55.3 %backward_scan.1 = (bf16[1024,2528]{1,0:T(8,128)(2,1)}, f32[8,800]{1,0:T(8,128)S(1)}, f32[1344,256]{1,0:T(8,128)S(1)}) custom-call(f32[1024,800]{1,0:T(8,128)} %copy-done.10, bf16[1024,2528]{1,0:T(8,128)(2,1)} %copy-done.2, bf16[4096,800]{1,0:T(8,128)(2,1)} %copy-done.5, f32[1024,8]{1,0:T(8,128)S(1)} %copy.107.aux, f32[8,1024]{1,0:T(8,128)S(1)} %stack.43.aux_t, ...), custom_call_target="tpu_custom_call" | custom-call | flops 35999997952 | bytes 360000000 | tf_op jit(solution)/shard_map/backward_scan/pallas_call | solution.py:497
  582.4 15.9 %fusion.4 = (f32[1600]{0:T(1024)S(1)}, bf16[1600,1024]{1,0:T(8,128)(2,1)}) fusion(bf16[1600,1024]{1,0:T(8,128)(2,1)S(1)} %copy-done.28, bf16[1600,1024]{1,0:T(8,128)(2,1)} %convolution_convert_fusion.2, f32[1024]{0:T(1024)S(1)} %add_rsqrt_fusion, bf16[1600,2528]{1,0:T(8,128)(2,1)} %all-gather.4.cloned.1.call-done, bf16[1024,2528]{1,0:T(8,128)(2,1)} %get-tuple-element.124), kind=kOutput, calls=%fused_computation.12 | convolution fusion | flops 8295217664 | bytes 23107840 | tf_op jit(solution)/shard_map/dot_general | solution.py:1220
  599.2 14.0 %add_convert_fusion = bf16[1600,2528]{1,0:T(8,128)(2,1)} fusion(f32[1600,16]{1,0:T(8,128)S(1)} %copy.117, bf16[1024,2528]{1,0:T(8,128)(2,1)} %get-tuple-element.124, bf16[1600,1024]{1,0:T(8,128)(2,1)} %line_gather.1, f32[1600]{0:T(1024)S(1)} %get-tuple-element.217, f32[1024]{0:T(1024)S(1)} %add_rsqrt_fusion), kind=kOutput, calls=%fused_computation | convolution fusion | flops 8298393600 | bytes 16656640 | tf_op jit(solution)/shard_map/dot_general | solution.py:1220
  616.0 3.2 reshape.219
  621.8 56.6 %line_sum.1 = f32[1600,256]{1,0:T(8,128)S(1)} custom-call(bf16[1600,1024]{1,0:T(8,128)(2,1)S(1)} %copy-done.11), custom_call_target="tpu_custom_call" | custom-call | flops 49999998976 | bytes 16777216 | tf_op jit(solution)/shard_map/line_sum/pallas_call | solution.py:764
  681.1 4.2 collective-permute-start.10
  694.1 7.7 %collective-permute-done.10 = bf16[1,200,592]{2,1,0:T(8,128)(2,1)S(1)} collective-permute-done((bf16[1,200,592]{2,1,0:T(8,128)(2,1)S(1)}, bf16[1,200,592]{2,1,0:T(8,128)(2,1)S(1)}, u32[]{:S(2)}, u32[]{:S(2)}) %collective-permute-start.10) | collective-permute-done | bytes 236832 | tf_op jit(solution)/shard_map/ppermute | solution.py:1241
  (294 shorter events, 101.9 us)
Async XLA Ops:
  7.2 109.2 %copy-start = (bf16[200,5504]{1,0:T(8,128)(2,1)S(1)}, bf16[200,5504]{1,0:T(8,128)(2,1)}, u32[]{:S(2)}) copy-start(bf16[200,5504]{1,0:T(8,128)(2,1)} %param.37) | copy-start | bytes 6604804
  7.2 83.2 %all-gather.4.cloned.1.call-start = ((), (), s32[]{:S(2)}) async-start(), calls=%async_computation.3 | async-start | bytes 9216000 | tf_op jit(solution)/shard_map/all_gather | solution.py:1226
  16.4 132.1 %all-gather.8.cloned.1.call-start = ((), (), s32[]{:S(2)}) async-start(), calls=%async_computation.5 | async-start | bytes 11520000 | tf_op jit(solution)/shard_map/all_gather | solution.py:1226
  17.1 63.9 %copy-start.40 = (s32[1,2048]{1,0:T(1,128)S(1)}, s32[1,2048]{1,0:T(1,128)}, u32[]{:S(2)}) copy-start(s32[1,2048]{1,0:T(1,128)} %param.20) | copy-start | bytes 24580
  17.1 68.4 %copy-start.42 = (f32[800]{0:T(1024)S(1)}, f32[800]{0:T(1024)}, u32[]{:S(2)}) copy-start(f32[800]{0:T(1024)} %param.30) | copy-start | bytes 9604
  17.2 68.4 %copy-start.41 = (f32[800]{0:T(1024)S(1)}, f32[800]{0:T(1024)}, u32[]{:S(2)}) copy-start(f32[800]{0:T(1024)} %param.31) | copy-start | bytes 9604
  17.2 68.4 %copy-start.43 = (f32[800]{0:T(1024)S(1)}, f32[800]{0:T(1024)}, u32[]{:S(2)}) copy-start(f32[800]{0:T(1024)} %param.32) | copy-start | bytes 9604
  17.2 228.9 %all-gather.6.cloned.1.call-start = ((), (), s32[]{:S(2)}) async-start(), calls=%async_computation.4 | async-start | bytes 21196800 | tf_op jit(solution)/shard_map/all_gather | solution.py:1226
  77.1 64.6 %collective-permute-start.1 = (bf16[1600,256]{1,0:T(8,128)(2,1)}, bf16[1600,256]{1,0:T(8,128)(2,1)}, u32[]{:S(2)}, u32[]{:S(2)}) collective-permute-start(bf16[1600,256]{1,0:T(8,128)(2,1)} %bitcast.6), channel_id=1, source_target_pairs={{0,1},{1,2},{2,3},{3,0},{4,5},{5,6},{6,7},{7,4},{8,9},{9,10},{10,1... | collective-permute-start | bytes 2457608 | tf_op jit(solution)/shard_map/ppermute | solution.py:1241
  77.2 64.5 %collective-permute-start.2 = (bf16[1600,256]{1,0:T(8,128)(2,1)}, bf16[1600,256]{1,0:T(8,128)(2,1)}, u32[]{:S(2)}, u32[]{:S(2)}) collective-permute-start(bf16[1600,256]{1,0:T(8,128)(2,1)} %bitcast.6), channel_id=1, source_target_pairs={{0,2},{1,3},{2,0},{3,1},{4,6},{5,7},{6,4},{7,5},{8,10},{9,11},{10,... | collective-permute-start | bytes 2457608 | tf_op jit(solution)/shard_map/ppermute | solution.py:1241
  80.1 61.5 %collective-permute-start.3 = (bf16[1600,256]{1,0:T(8,128)(2,1)}, bf16[1600,256]{1,0:T(8,128)(2,1)}, u32[]{:S(2)}, u32[]{:S(2)}) collective-permute-start(bf16[1600,256]{1,0:T(8,128)(2,1)} %bitcast.6), channel_id=1, source_target_pairs={{0,3},{1,0},{2,1},{3,2},{4,7},{5,4},{6,5},{7,6},{8,11},{9,8},{10,9... | collective-permute-start | bytes 2457608 | tf_op jit(solution)/shard_map/ppermute | solution.py:1241
  91.8 24.2 %slice-start.2 = ((s8[4403200]{0:T(1024)(128)(4,1)}), s8[4194304]{0:T(1024)(128)(4,1)S(1)}, s32[]{:S(2)}) async-start(s8[4403200]{0:T(1024)(128)(4,1)} %bitcast.98), calls=%async_computation.11 | async-start | bytes 8388608
  117.5 5.3 collective-permute-start
  141.7 382.8 %reduce-scatter.10.cloned.1.call-start = ((), (), s32[]{:S(2)}) async-start(), calls=%async_computation.8 | async-start | bytes 15206400
  154.0 11.4 %collective-permute-start.4 = (bf16[640,1024]{1,0:T(8,128)(2,1)S(1)}, bf16[640,1024]{1,0:T(8,128)(2,1)S(1)}, u32[]{:S(2)}, u32[]{:S(2)}) collective-permute-start(bf16[640,1024]{1,0:T(8,128)(2,1)S(1)} %convolution_convert_fusion.6), channel_id=1, source_target_pairs={{0,4},{1,5},{2,6},{3,7},{8,12},{9,13},{10,14},{11,15},{16,20},{17,... | collective-permute-start | bytes 3932168 | tf_op jit(solution)/shard_map/ppermute | solution.py:1381
  251.9 70.2 %copy-start.12 = (f32[1600,256]{1,0:T(8,128)}, f32[1600,256]{1,0:T(8,128)S(1)}, u32[]{:S(2)}) copy-start(f32[1600,256]{1,0:T(8,128)S(1)} %get-tuple-element.223) | copy-start | bytes 4915204
  382.7 230.5 %reduce-scatter.6.cloned.1.call-start = ((), (), s32[]{:S(2)}) async-start(), calls=%async_computation.6 | async-start | bytes 13824000 | tf_op jit(solution)/shard_map/reduce_scatter | solution.py:1235
  456.2 34.4 %collective-permute-start.5 = (bf16[400,256]{1,0:T(8,128)(2,1)S(1)}, bf16[400,256]{1,0:T(8,128)(2,1)S(1)}, u32[]{:S(2)}, u32[]{:S(2)}) collective-permute-start(bf16[400,256]{1,0:T(8,128)(2,1)S(1)} %get-tuple-element.254), channel_id=1, source_target_pairs={{0,1},{1,2},{2,3},{3,0},{4,5},{5,6},{6,7},{7,4},{8,9},{9,10},{10,1... | collective-permute-start | bytes 614408 | tf_op jit(solution)/shard_map/ppermute | solution.py:1241
  456.2 34.3 %collective-permute-start.6 = (bf16[400,256]{1,0:T(8,128)(2,1)S(1)}, bf16[400,256]{1,0:T(8,128)(2,1)S(1)}, u32[]{:S(2)}, u32[]{:S(2)}) collective-permute-start(bf16[400,256]{1,0:T(8,128)(2,1)S(1)} %get-tuple-element.253), channel_id=1, source_target_pairs={{0,2},{1,3},{2,0},{3,1},{4,6},{5,7},{6,4},{7,5},{8,10},{9,11},{10,... | collective-permute-start | bytes 614408 | tf_op jit(solution)/shard_map/ppermute | solution.py:1241
  458.1 32.5 %collective-permute-start.7 = (bf16[400,256]{1,0:T(8,128)(2,1)S(1)}, bf16[400,256]{1,0:T(8,128)(2,1)S(1)}, u32[]{:S(2)}, u32[]{:S(2)}) collective-permute-start(bf16[400,256]{1,0:T(8,128)(2,1)S(1)} %get-tuple-element.252), channel_id=1, source_target_pairs={{0,3},{1,0},{2,1},{3,2},{4,7},{5,4},{6,5},{7,6},{8,11},{9,8},{10,9... | collective-permute-start | bytes 614408 | tf_op jit(solution)/shard_map/ppermute | solution.py:1241
  460.6 39.7 %copy-start.29 = (bf16[640,2048]{1,0:T(8,128)(2,1)}, bf16[640,2048]{1,0:T(8,128)(2,1)S(1)}, u32[]{:S(2)}) copy-start(bf16[640,2048]{1,0:T(8,128)(2,1)S(1)} %slice_dynamic-update-slice_fusion) | copy-start | bytes 7864324
  460.7 39.6 %collective-permute-start.9 = (bf16[640,1024]{1,0:T(8,128)(2,1)S(1)}, bf16[640,1024]{1,0:T(8,128)(2,1)S(1)}, u32[]{:S(2)}, u32[]{:S(2)}) collective-permute-start(bf16[640,1024]{1,0:T(8,128)(2,1)S(1)} %slice.222), channel_id=1, source_target_pairs={{4,0},{5,1},{6,2},{7,3},{12,8},{13,9},{14,10},{15,11},{20,16},{21,... | collective-permute-start | bytes 3932168 | tf_op jit(solution)/shard_map/ppermute | solution.py:1460
  509.6 194.8 %reduce-scatter.8.cloned.1.call-start = ((), (), s32[]{:S(2)}) async-start(), calls=%async_computation.7 | async-start | bytes 9216000 | tf_op jit(solution)/shard_map/reduce_scatter | solution.py:1235
  516.9 7.6 %collective-permute-start.8 = (f32[16,800]{1,0:T(8,128)S(1)}, f32[16,800]{1,0:T(8,128)S(1)}, u32[]{:S(2)}, u32[]{:S(2)}) collective-permute-start(f32[16,800]{1,0:T(8,128)S(1)} %get-tuple-element.109), channel_id=1, source_target_pairs={{4,0},{5,1},{6,2},{7,3},{12,8},{13,9},{14,10},{15,11},{20,16},{21,... | collective-permute-start | bytes 153608 | tf_op jit(solution)/shard_map/ppermute | solution.py:1471
  527.0 55.4 %copy-start.28 = (bf16[1600,1024]{1,0:T(8,128)(2,1)S(1)}, bf16[1600,1024]{1,0:T(8,128)(2,1)}, u32[]{:S(2)}) copy-start(bf16[1600,1024]{1,0:T(8,128)(2,1)} %line_gather.1) | copy-start | bytes 9830404
  621.8 56.6 %copy-start.33 = (f32[1600,256]{1,0:T(8,128)S(1)}, f32[1600,256]{1,0:T(8,128)}, u32[]{:S(2)}) copy-start(f32[1600,256]{1,0:T(8,128)} %get-tuple-element.273) | copy-start | bytes 4915204
  678.8 15.3 %collective-permute-start.12 = (bf16[1,200,592]{2,1,0:T(8,128)(2,1)S(1)}, bf16[1,200,592]{2,1,0:T(8,128)(2,1)S(1)}, u32[]{:S(2)}, u32[]{:S(2)}) collective-permute-start(bf16[1,200,592]{2,1,0:T(8,128)(2,1)S(1)} %get-tuple-element.246), channel_id=1, source_target_pairs={{0,3},{1,0},{2,1},{3,2},{4,7},{5,4},{6,5},{7,6},{8,11},{9,8},{10,9... | collective-permute-start | bytes 710408 | tf_op jit(solution)/shard_map/ppermute | solution.py:1241
  679.4 14.7 %collective-permute-start.11 = (bf16[1,200,592]{2,1,0:T(8,128)(2,1)S(1)}, bf16[1,200,592]{2,1,0:T(8,128)(2,1)S(1)}, u32[]{:S(2)}, u32[]{:S(2)}) collective-permute-start(bf16[1,200,592]{2,1,0:T(8,128)(2,1)S(1)} %get-tuple-element.247), channel_id=1, source_target_pairs={{0,1},{1,2},{2,3},{3,0},{4,5},{5,6},{6,7},{7,4},{8,9},{9,10},{10,1... | collective-permute-start | bytes 710408 | tf_op jit(solution)/shard_map/ppermute | solution.py:1241
  681.1 20.6 %collective-permute-start.10 = (bf16[1,200,592]{2,1,0:T(8,128)(2,1)S(1)}, bf16[1,200,592]{2,1,0:T(8,128)(2,1)S(1)}, u32[]{:S(2)}, u32[]{:S(2)}) collective-permute-start(bf16[1,200,592]{2,1,0:T(8,128)(2,1)S(1)} %get-tuple-element.245), channel_id=1, source_target_pairs={{0,2},{1,3},{2,0},{3,1},{4,6},{5,7},{6,4},{7,5},{8,10},{9,11},{10,... | collective-permute-start | bytes 710408 | tf_op jit(solution)/shard_map/ppermute | solution.py:1241
  706.3 6.9 collective-permute-start.15
  706.7 6.6 collective-permute-start.14
  708.4 4.9 collective-permute-start.13
  (43 other events, 223.0 us)
Sparse Core Ops, SparseCore 0:
  16.5 56.2 all-gather.3
  75.2 62.2 all-gather.7
  141.8 104.1 all-gather.5
  382.9 98.7 reduce-scatter.9
  509.7 89.8 reduce-scatter.5
  613.4 68.9 reduce-scatter.7

commit v7 on v6

--- a/solution.py
+++ b/solution.py
@@ -1385,9 +1385,14 @@
         [jnp.pad(piece, ((0, 0), (0, ff_wide - ff))) for piece in ffn_shards] + [attn_output],
         axis=1,
     )
-    third, gated, *cotangent_pieces = lax.optimization_barrier((third, gated, *cotangent_pieces))
+    third, gated, cotangent_pieces[2] = lax.optimization_barrier(
+        (third, gated, cotangent_pieces[2])
+    )
     third = gather_rows(third)
     mamba_part_t = dot(state_out_map, gated, 1, 1).astype(bf16)
+    mamba_part_t, cotangent_pieces[1], cotangent_pieces[3] = lax.optimization_barrier(
+        (mamba_part_t, cotangent_pieces[1], cotangent_pieces[3])
+    )
     up_map, down_map, attn_map = cut(third, [2 * ff_wide, ff_wide, query_width])
 
     key_start = span + tp_index * rows - WIN

time: 729 us -> 720 us (0.988)
  Pallas kernels: 465 us -> 447 us
  waiting for transfers between devices: 17.6 us -> 28.9 us
    ppermute x12, waiting for transfers between devices: 7.7 us -> 28 us  [send(): lax.ppermute(values, 'tp', [(i, (i + by) % count) for i in range(count)])]
    all_gather x3, waiting for transfers between devices: 9.13 us -> 0.05 us  [gather_rows(): return lax.all_gather(whole, ('fsdp', 'ctx'), axis=0, tiled=True)]
  transfers between devices with their start and end apart: 22 -> 22, of which waited for: 2 -> 4; matrix products, arithmetic and copies ran while one was open for 23% -> 24% of each run, Pallas kernels for 47% -> 46%
where the time goes in v7:
time: 720 us; the launch traced here: 713 us
  Pallas kernels  447 us (62%)
  matrix products  110 us (15%)
  local copies, waits for them, and re-layouts  45.3 us (6%)
  other arithmetic  44.1 us (6%)
  waiting for transfers between devices  28.9 us (4%)
  starting transfers between devices  20.4 us (3%)
  between operations  16.6 us (2%)
    dot_general x18, matrix products, dot(): lax.dot_general(left, right, (((left_dim,), (right_dim,)), ((), ())), pre...  110 us
    pallas_call x1, Pallas kernels, feed_forward(): pl.pallas_call(functools.partial(feed_kernel, count, tuple(blocks)), name...  62.7 us
    pallas_call x1, Pallas kernels, attend(): pl.pallas_call(functools.partial(attend_kernel, group, count), name='atte...  62.1 us
    pallas_call x1, Pallas kernels, line_gather(): pl.pallas_call(functools.partial(line_gather_kernel, count), name='line_g...  59.9 us
    pallas_call x1, Pallas kernels, attend_back(): pl.pallas_call(functools.partial(attend_back_kernel, group, count), name=...  56.5 us
    pallas_call x1, Pallas kernels, wide_sum(): pl.pallas_call(functools.partial(wide_sum_kernel, count, ups, downs), nam...  56.1 us
    pallas_call x1, Pallas kernels, line_sum(): pl.pallas_call(functools.partial(line_sum_kernel, count), name='line_sum'...  55.6 us
    pallas_call x1, Pallas kernels, backward_scan(): scan_call(functools.partial(backward_kernel, count), 'backward_scan', til...  55.1 us
  transfers between devices with their start and end apart: 22, of which 4 were waited for; matrix products, arithmetic and copies ran while one was open for 24% of the time, Pallas kernels for 46%

profile of v7, /device:TPU:0, one launch (start us, length us, event | category | flops | bytes accessed | tf_op | source)
XLA Modules:
  0.0 712.6 jit_solution(5050600304233440714)
XLA Ops:
  11.9 3.5 concatenate.55
  16.2 59.9 %line_gather.1 = bf16[1600,1024]{1,0:T(8,128)(2,1)} custom-call(bf16[1600,256]{1,0:T(8,128)(2,1)} %bitcast.91), custom_call_target="tpu_custom_call" | custom-call | tf_op jit(solution)/shard_map/line_gather/pallas_call | solution.py:634
  81.4 3.1 fusion.5
  89.5 12.9 %convolution_convert_fusion.1.mixed = bf16[1024,2528]{1,0:T(8,128)(2,1)S(1)} fusion(bf16[1600,2528]{1,0:T(8,128)(2,1)} %all-gather.4.cloned.1.call-done, bf16[1600,1024]{1,0:T(8,128)(2,1)S(1)} %copy-done.26, f32[1600]{0:T(1024)S(1)} %get-tuple-element.217, f32[1024]{0:T(1024)S(1)} %add_rsqrt_fusion), kind=kOutput, calls=%fused_computation.15 | convolution fusion | flops 8292892672 | bytes 16554240 | tf_op jit(solution)/shard_map/dot_general | solution.py:1220
  102.4 9.5 %end_state.1 = f32[16,800]{1,0:T(8,128)S(1)} custom-call(bf16[1024,2528]{1,0:T(8,128)(2,1)S(1)} %convolution_convert_fusion.1.mixed, f32[1024,8]{1,0:T(8,128)S(1)} %copy.107.aux, f32[8,1024]{1,0:T(8,128)S(1)} %stack.43.aux_t, f32[256,1]{1,0:T(8,128)S(1)} %fusion.110.alive_last, f32[1,800]{1,0:T(1,128)S(1)} %broadcast_in_dim.166.bias, ...), custom_call_target="tpu_custom_call" | custom-call | flops 10000000 | bytes 100000 | tf_op jit(solution)/shard_map/end_state/pallas_call | solution.py:441
  114.7 4.0 fusion.37
  121.2 13.4 %forward_scan.1 = (bf16[1024,800]{1,0:T(8,128)(2,1)S(1)}, bf16[4096,800]{1,0:T(8,128)(2,1)S(1)}, f32[16,800]{1,0:T(8,128)S(1)}) custom-call(bf16[1024,2528]{1,0:T(8,128)(2,1)S(1)} %copy-done.3, f32[1024,8]{1,0:T(8,128)S(1)} %copy.107.aux, f32[8,1024]{1,0:T(8,128)S(1)} %stack.43.aux_t, f32[256,1]{1,0:T(8,128)S(1)} %fusion.110.alive_last, ...), custom_call_target="tpu_custom_call" | custom-call | flops 10000000 | bytes 100000 | tf_op jit(solution)/shard_map/forward_scan/pallas_call | solution.py:456
  143.7 6.5 convolution_convert_fusion.6
  152.2 5.1 convolution_convert_fusion.3.source
  157.3 3.6 collective-permute-done.3
  160.9 13.8 %collective-permute-done.4 = bf16[1600,256]{1,0:T(8,128)(2,1)} collective-permute-done((bf16[1600,256]{1,0:T(8,128)(2,1)}, bf16[1600,256]{1,0:T(8,128)(2,1)}, u32[]{:S(2)}, u32[]{:S(2)}) %collective-permute-start.4) | collective-permute-done | bytes 819232 | tf_op jit(solution)/shard_map/ppermute | solution.py:1241
  185.3 62.1 %attend.1 = (bf16[1600,256]{1,0:T(8,128)(2,1)}, f32[5,8,256]{2,1,0:T(8,128)}, f32[1600,256]{1,0:T(8,128)}) custom-call(bf16[1600,256]{1,0:T(8,128)(2,1)} %fusion.26.query_t, bf16[640,1408]{1,0:T(8,128)(2,1)} %pad_maximum_fusion.1.key_t.value_t, bf16[640,1408]{1,0:T(8,128)(2,1)} %pad_maximum_fusion.1.key_t.value_t, f32[1408,256]{1,0:T(8,128)} %concatenate.64.bias, ...), custom_call_target="tpu_custom_call" | custom-call | tf_op jit(solution)/shard_map/attend/pallas_call | solution.py:1138
  249.1 4.6 multiply_reduce_fusion.8
  256.2 62.7 %feed_forward.1 = (bf16[1600,1024]{1,0:T(8,128)(2,1)}, bf16[1024,2816]{1,0:T(8,128)(2,1)}, bf16[1024,1408]{1,0:T(8,128)(2,1)}, bf16[1600,1024]{1,0:T(8,128)(2,1)}) custom-call(bf16[1600,256]{1,0:T(8,128)(2,1)} %multiply_convert_fusion.2.source, bf16[1600,1024]{1,0:T(8,128)(2,1)} %pad_maximum_fusion.other.others, ...), custom_call_target="tpu_custom_call" | custom-call | tf_op jit(solution)/shard_map/feed_forward/pallas_call | solution.py:899
  320.8 56.1 %wide_sum.1 = (bf16[1600,4224]{1,0:T(8,128)(2,1)}, bf16[1600,1024]{1,0:T(8,128)(2,1)}, f32[1600,256]{1,0:T(8,128)S(1)}) custom-call(bf16[1600,1024]{1,0:T(8,128)(2,1)} %get-tuple-element.98.tokens, bf16[1600,1024]{1,0:T(8,128)(2,1)} %pad_maximum_fusion.other.others, bf16[1024,2816]{1,0:T(8,128)(2,1)} %get-tuple-element.99.gate_up_grad, ...), custom_call_target="tpu_custom_call" | custom-call | tf_op jit(solution)/shard_map/wide_sum/pallas_call | solution.py:996
  379.8 3.4 multiply_reduce_fusion.1
  385.1 6.3 fusion.23.grad_t
  391.4 56.5 %attend_back.1 = (bf16[1600,256]{1,0:T(8,128)(2,1)}, bf16[2,320,1408]{2,1,0:T(8,128)(2,1)}, bf16[1600,1024]{1,0:T(8,128)(2,1)}) custom-call(bf16[1600,256]{1,0:T(8,128)(2,1)} %fusion.26.query_t, bf16[640,1408]{1,0:T(8,128)(2,1)} %pad_maximum_fusion.1.key_t.value_t, bf16[640,1408]{1,0:T(8,128)(2,1)} %pad_maximum_fusion.1.key_t.value_t, ...), custom_call_target="tpu_custom_call" | custom-call | tf_op jit(solution)/shard_map/attend_back/pallas_call | solution.py:1177
  455.2 3.2 fusion.88
  460.4 6.3 fusion.29.gated_grad
  466.7 16.5 %end_adjoint.1 = (f32[16,800]{1,0:T(8,128)S(1)}, f32[256,256]{1,0:T(8,128)S(1)}) custom-call(f32[1024,800]{1,0:T(8,128)S(1)} %fusion.29.gated_grad, bf16[1024,2528]{1,0:T(8,128)(2,1)S(1)} %bitcast.89, f32[1024,8]{1,0:T(8,128)S(1)} %copy.107.aux, f32[8,1024]{1,0:T(8,128)S(1)} %stack.43.aux_t, f32[256,1]{1,0:T(8,128)S(1)} %fusion.110.alive_last, ...), custom_call_target="tpu_custom_call" | custom-call | flops 10000000000 | bytes 100000000 | tf_op jit(solution)/shard_map/end_adjoint/pallas_call | solution.py:476
  483.3 4.3 fusion.2
  487.7 3.3 fusion.22
  493.1 4.4 fusion.21
  497.5 4.9 fusion.20
  503.8 5.5 fusion.44
  510.6 6.6 convolution_convert_fusion.2
  520.0 55.1 %backward_scan.1 = (bf16[1024,2528]{1,0:T(8,128)(2,1)}, f32[8,800]{1,0:T(8,128)S(1)}, f32[1344,256]{1,0:T(8,128)S(1)}) custom-call(f32[1024,800]{1,0:T(8,128)} %copy-done.10, bf16[1024,2528]{1,0:T(8,128)(2,1)} %copy-done.2, bf16[4096,800]{1,0:T(8,128)(2,1)} %copy-done.5, f32[1024,8]{1,0:T(8,128)S(1)} %copy.107.aux, f32[8,1024]{1,0:T(8,128)S(1)} %stack.43.aux_t, ...), custom_call_target="tpu_custom_call" | custom-call | flops 35999997952 | bytes 360000000 | tf_op jit(solution)/shard_map/backward_scan/pallas_call | solution.py:497
  575.1 16.1 %fusion.4 = (f32[1600]{0:T(1024)S(1)}, bf16[1600,1024]{1,0:T(8,128)(2,1)}) fusion(bf16[1600,1024]{1,0:T(8,128)(2,1)S(1)} %copy-done.28, bf16[1600,1024]{1,0:T(8,128)(2,1)} %convolution_convert_fusion.2, f32[1024]{0:T(1024)S(1)} %add_rsqrt_fusion, bf16[1600,2528]{1,0:T(8,128)(2,1)} %all-gather.4.cloned.1.call-done, bf16[1024,2528]{1,0:T(8,128)(2,1)} %get-tuple-element.124), kind=kOutput, calls=%fused_computation.12 | convolution fusion | flops 8295217664 | bytes 23107840 | tf_op jit(solution)/shard_map/dot_general | solution.py:1220
  592.1 14.2 %add_convert_fusion = bf16[1600,2528]{1,0:T(8,128)(2,1)} fusion(f32[1600,16]{1,0:T(8,128)S(1)} %copy.117, bf16[1024,2528]{1,0:T(8,128)(2,1)} %get-tuple-element.124, bf16[1600,1024]{1,0:T(8,128)(2,1)} %line_gather.1, f32[1600]{0:T(1024)S(1)} %get-tuple-element.217, f32[1024]{0:T(1024)S(1)} %add_rsqrt_fusion), kind=kOutput, calls=%fused_computation | convolution fusion | flops 8298393600 | bytes 16656640 | tf_op jit(solution)/shard_map/dot_general | solution.py:1220
  613.7 55.6 %line_sum.1 = f32[1600,256]{1,0:T(8,128)S(1)} custom-call(bf16[1600,1024]{1,0:T(8,128)(2,1)S(1)} %copy-done.11), custom_call_target="tpu_custom_call" | custom-call | flops 49999998976 | bytes 16777216 | tf_op jit(solution)/shard_map/line_sum/pallas_call | solution.py:764
  684.8 7.8 %collective-permute-done.10 = bf16[1,200,592]{2,1,0:T(8,128)(2,1)S(1)} collective-permute-done((bf16[1,200,592]{2,1,0:T(8,128)(2,1)S(1)}, bf16[1,200,592]{2,1,0:T(8,128)(2,1)S(1)}, u32[]{:S(2)}, u32[]{:S(2)}) %collective-permute-start.10) | collective-permute-done | bytes 236832 | tf_op jit(solution)/shard_map/ppermute | solution.py:1241
  (294 shorter events, 105.3 us)
Async XLA Ops:
  7.2 105.2 %copy-start = (bf16[200,5504]{1,0:T(8,128)(2,1)S(1)}, bf16[200,5504]{1,0:T(8,128)(2,1)}, u32[]{:S(2)}) copy-start(bf16[200,5504]{1,0:T(8,128)(2,1)} %param.37) | copy-start | bytes 6604804
  7.2 79.3 %all-gather.4.cloned.1.call-start = ((), (), s32[]{:S(2)}) async-start(), calls=%async_computation.3 | async-start | bytes 9216000 | tf_op jit(solution)/shard_map/all_gather | solution.py:1226
  15.4 128.3 %all-gather.8.cloned.1.call-start = ((), (), s32[]{:S(2)}) async-start(), calls=%async_computation.5 | async-start | bytes 11520000 | tf_op jit(solution)/shard_map/all_gather | solution.py:1226
  16.1 60.5 %copy-start.40 = (s32[1,2048]{1,0:T(1,128)S(1)}, s32[1,2048]{1,0:T(1,128)}, u32[]{:S(2)}) copy-start(s32[1,2048]{1,0:T(1,128)} %param.20) | copy-start | bytes 24580
  16.1 65.0 %copy-start.42 = (f32[800]{0:T(1024)S(1)}, f32[800]{0:T(1024)}, u32[]{:S(2)}) copy-start(f32[800]{0:T(1024)} %param.30) | copy-start | bytes 9604
  16.2 65.0 %copy-start.41 = (f32[800]{0:T(1024)S(1)}, f32[800]{0:T(1024)}, u32[]{:S(2)}) copy-start(f32[800]{0:T(1024)} %param.31) | copy-start | bytes 9604
  16.2 65.1 %copy-start.43 = (f32[800]{0:T(1024)S(1)}, f32[800]{0:T(1024)}, u32[]{:S(2)}) copy-start(f32[800]{0:T(1024)} %param.32) | copy-start | bytes 9604
  16.2 232.9 %all-gather.6.cloned.1.call-start = ((), (), s32[]{:S(2)}) async-start(), calls=%async_computation.4 | async-start | bytes 21196800 | tf_op jit(solution)/shard_map/all_gather | solution.py:1226
  76.1 61.3 %collective-permute-start.1 = (bf16[1600,256]{1,0:T(8,128)(2,1)}, bf16[1600,256]{1,0:T(8,128)(2,1)}, u32[]{:S(2)}, u32[]{:S(2)}) collective-permute-start(bf16[1600,256]{1,0:T(8,128)(2,1)} %bitcast.6), channel_id=1, source_target_pairs={{0,2},{1,3},{2,0},{3,1},{4,6},{5,7},{6,4},{7,5},{8,10},{9,11},{10,... | collective-permute-start | bytes 2457608 | tf_op jit(solution)/shard_map/ppermute | solution.py:1241
  87.9 24.0 %slice-start.2 = ((s8[4403200]{0:T(1024)(128)(4,1)}), s8[4194304]{0:T(1024)(128)(4,1)S(1)}, s32[]{:S(2)}) async-start(s8[4403200]{0:T(1024)(128)(4,1)} %bitcast.98), calls=%async_computation.11 | async-start | bytes 8388608
  113.4 5.3 collective-permute-start
  137.5 379.7 %reduce-scatter.10.cloned.1.call-start = ((), (), s32[]{:S(2)}) async-start(), calls=%async_computation.8 | async-start | bytes 15206400
  137.5 23.4 %collective-permute-start.3 = (bf16[1600,256]{1,0:T(8,128)(2,1)}, bf16[1600,256]{1,0:T(8,128)(2,1)}, u32[]{:S(2)}, u32[]{:S(2)}) collective-permute-start(bf16[1600,256]{1,0:T(8,128)(2,1)} %bitcast.6), channel_id=1, source_target_pairs={{0,1},{1,2},{2,3},{3,0},{4,5},{5,6},{6,7},{7,4},{8,9},{9,10},{10,1... | collective-permute-start | bytes 2457608 | tf_op jit(solution)/shard_map/ppermute | solution.py:1241
  139.9 34.8 %collective-permute-start.4 = (bf16[1600,256]{1,0:T(8,128)(2,1)}, bf16[1600,256]{1,0:T(8,128)(2,1)}, u32[]{:S(2)}, u32[]{:S(2)}) collective-permute-start(bf16[1600,256]{1,0:T(8,128)(2,1)} %bitcast.6), channel_id=1, source_target_pairs={{0,3},{1,0},{2,1},{3,2},{4,7},{5,4},{6,5},{7,6},{8,11},{9,8},{10,9... | collective-permute-start | bytes 2457608 | tf_op jit(solution)/shard_map/ppermute | solution.py:1241
  150.2 33.0 %collective-permute-start.2 = (bf16[640,1024]{1,0:T(8,128)(2,1)S(1)}, bf16[640,1024]{1,0:T(8,128)(2,1)S(1)}, u32[]{:S(2)}, u32[]{:S(2)}) collective-permute-start(bf16[640,1024]{1,0:T(8,128)(2,1)S(1)} %convolution_convert_fusion.6), channel_id=1, source_target_pairs={{0,4},{1,5},{2,6},{3,7},{8,12},{9,13},{10,14},{11,15},{16,20},{17,... | collective-permute-start | bytes 3932168 | tf_op jit(solution)/shard_map/ppermute | solution.py:1381
  254.8 64.1 %copy-start.12 = (f32[1600,256]{1,0:T(8,128)}, f32[1600,256]{1,0:T(8,128)S(1)}, u32[]{:S(2)}) copy-start(f32[1600,256]{1,0:T(8,128)S(1)} %get-tuple-element.223) | copy-start | bytes 4915204
  376.9 229.4 %reduce-scatter.6.cloned.1.call-start = ((), (), s32[]{:S(2)}) async-start(), calls=%async_computation.6 | async-start | bytes 13824000 | tf_op jit(solution)/shard_map/reduce_scatter | solution.py:1235
  449.3 34.0 %collective-permute-start.5 = (bf16[400,256]{1,0:T(8,128)(2,1)S(1)}, bf16[400,256]{1,0:T(8,128)(2,1)S(1)}, u32[]{:S(2)}, u32[]{:S(2)}) collective-permute-start(bf16[400,256]{1,0:T(8,128)(2,1)S(1)} %get-tuple-element.254), channel_id=1, source_target_pairs={{0,1},{1,2},{2,3},{3,0},{4,5},{5,6},{6,7},{7,4},{8,9},{9,10},{10,1... | collective-permute-start | bytes 614408 | tf_op jit(solution)/shard_map/ppermute | solution.py:1241
  449.4 33.9 %collective-permute-start.6 = (bf16[400,256]{1,0:T(8,128)(2,1)S(1)}, bf16[400,256]{1,0:T(8,128)(2,1)S(1)}, u32[]{:S(2)}, u32[]{:S(2)}) collective-permute-start(bf16[400,256]{1,0:T(8,128)(2,1)S(1)} %get-tuple-element.253), channel_id=1, source_target_pairs={{0,2},{1,3},{2,0},{3,1},{4,6},{5,7},{6,4},{7,5},{8,10},{9,11},{10,... | collective-permute-start | bytes 614408 | tf_op jit(solution)/shard_map/ppermute | solution.py:1241
  451.3 32.0 %collective-permute-start.7 = (bf16[400,256]{1,0:T(8,128)(2,1)S(1)}, bf16[400,256]{1,0:T(8,128)(2,1)S(1)}, u32[]{:S(2)}, u32[]{:S(2)}) collective-permute-start(bf16[400,256]{1,0:T(8,128)(2,1)S(1)} %get-tuple-element.252), channel_id=1, source_target_pairs={{0,3},{1,0},{2,1},{3,2},{4,7},{5,4},{6,5},{7,6},{8,11},{9,8},{10,9... | collective-permute-start | bytes 614408 | tf_op jit(solution)/shard_map/ppermute | solution.py:1241
  453.7 39.4 %copy-start.29 = (bf16[640,2048]{1,0:T(8,128)(2,1)}, bf16[640,2048]{1,0:T(8,128)(2,1)S(1)}, u32[]{:S(2)}) copy-start(bf16[640,2048]{1,0:T(8,128)(2,1)S(1)} %slice_dynamic-update-slice_fusion) | copy-start | bytes 7864324
  453.9 39.2 %collective-permute-start.9 = (bf16[640,1024]{1,0:T(8,128)(2,1)S(1)}, bf16[640,1024]{1,0:T(8,128)(2,1)S(1)}, u32[]{:S(2)}, u32[]{:S(2)}) collective-permute-start(bf16[640,1024]{1,0:T(8,128)(2,1)S(1)} %slice.222), channel_id=1, source_target_pairs={{4,0},{5,1},{6,2},{7,3},{12,8},{13,9},{14,10},{15,11},{20,16},{21,... | collective-permute-start | bytes 3932168 | tf_op jit(solution)/shard_map/ppermute | solution.py:1465
  502.4 192.8 %reduce-scatter.8.cloned.1.call-start = ((), (), s32[]{:S(2)}) async-start(), calls=%async_computation.7 | async-start | bytes 9216000 | tf_op jit(solution)/shard_map/reduce_scatter | solution.py:1235
  509.3 7.9 %collective-permute-start.8 = (f32[16,800]{1,0:T(8,128)S(1)}, f32[16,800]{1,0:T(8,128)S(1)}, u32[]{:S(2)}, u32[]{:S(2)}) collective-permute-start(f32[16,800]{1,0:T(8,128)S(1)} %get-tuple-element.109), channel_id=1, source_target_pairs={{4,0},{5,1},{6,2},{7,3},{12,8},{13,9},{14,10},{15,11},{20,16},{21,... | collective-permute-start | bytes 153608 | tf_op jit(solution)/shard_map/ppermute | solution.py:1476
  520.0 55.1 %copy-start.28 = (bf16[1600,1024]{1,0:T(8,128)(2,1)S(1)}, bf16[1600,1024]{1,0:T(8,128)(2,1)}, u32[]{:S(2)}) copy-start(bf16[1600,1024]{1,0:T(8,128)(2,1)} %line_gather.1) | copy-start | bytes 9830404
  613.7 55.6 %copy-start.33 = (f32[1600,256]{1,0:T(8,128)S(1)}, f32[1600,256]{1,0:T(8,128)}, u32[]{:S(2)}) copy-start(f32[1600,256]{1,0:T(8,128)} %get-tuple-element.273) | copy-start | bytes 4915204
  669.6 12.3 %collective-permute-start.12 = (bf16[1,200,592]{2,1,0:T(8,128)(2,1)S(1)}, bf16[1,200,592]{2,1,0:T(8,128)(2,1)S(1)}, u32[]{:S(2)}, u32[]{:S(2)}) collective-permute-start(bf16[1,200,592]{2,1,0:T(8,128)(2,1)S(1)} %get-tuple-element.246), channel_id=1, source_target_pairs={{0,3},{1,0},{2,1},{3,2},{4,7},{5,4},{6,5},{7,6},{8,11},{9,8},{10,9... | collective-permute-start | bytes 710408 | tf_op jit(solution)/shard_map/ppermute | solution.py:1241
  671.3 13.4 %collective-permute-start.11 = (bf16[1,200,592]{2,1,0:T(8,128)(2,1)S(1)}, bf16[1,200,592]{2,1,0:T(8,128)(2,1)S(1)}, u32[]{:S(2)}, u32[]{:S(2)}) collective-permute-start(bf16[1,200,592]{2,1,0:T(8,128)(2,1)S(1)} %get-tuple-element.247), channel_id=1, source_target_pairs={{0,1},{1,2},{2,3},{3,0},{4,5},{5,6},{6,7},{7,4},{8,9},{9,10},{10,1... | collective-permute-start | bytes 710408 | tf_op jit(solution)/shard_map/ppermute | solution.py:1241
  671.7 20.9 %collective-permute-start.10 = (bf16[1,200,592]{2,1,0:T(8,128)(2,1)S(1)}, bf16[1,200,592]{2,1,0:T(8,128)(2,1)S(1)}, u32[]{:S(2)}, u32[]{:S(2)}) collective-permute-start(bf16[1,200,592]{2,1,0:T(8,128)(2,1)S(1)} %get-tuple-element.245), channel_id=1, source_target_pairs={{0,2},{1,3},{2,0},{3,1},{4,6},{5,7},{6,4},{7,5},{8,10},{9,11},{10,... | collective-permute-start | bytes 710408 | tf_op jit(solution)/shard_map/ppermute | solution.py:1241
  697.1 6.9 collective-permute-start.15
  698.3 5.8 collective-permute-start.14
  699.2 4.9 collective-permute-start.13
  (43 other events, 215.7 us)
Sparse Core Ops, SparseCore 0:
  15.5 56.2 all-gather.3
  74.3 62.2 all-gather.7
  138.4 98.5 all-gather.5
  377.0 101.9 reduce-scatter.9
  502.5 90.7 reduce-scatter.5
  606.5 70.3 reduce-scatter.7
